TPU v7x, 768 devices: a whole 4x8x12 slice. The times are simulated.
768 devices in a mesh: ctx: 192 (over z_lo, y, x, core), tp: 4 (over z_hi).
Axes of the slice: x: 4, y: 8, z: 12 (z_hi: 4, z_lo: 3; z = z_hi * 3 + z_lo), core: 2. Of those that a mesh axis runs over, the one named last changes fastest.
Arguments:
- queries: bfloat16 [6144, 2560], P(('ctx', 'tp')), may hold values from -128 to 128
- keys: bfloat16 [6144, 2560], P(('ctx', 'tp')), may hold values from -5 to 5
- vals: bfloat16 [6144, 2560], P(('ctx', 'tp')), may hold values from -24 to 24
- out_weight: bfloat16 [2560, 5120], P(None, 'tp'), may hold values from -0.25 to 0.25
- gate: float32 [5120], P('tp'), may hold values from 0.5 to 4
Outputs:
- mixed: bfloat16 [6144, 5120], P('ctx', 'tp')
All inputs are finite; a program needn't handle non-finite values.
Results may differ from a plain program's by a relative error of at most 0.0057.
Values may be sent and summed in bfloat16 or wider, within the bound.
No kernel may reach another device: no remote copies, remote signals or barrier semaphores. Data moves between devices by JAX's collectives and lax.ppermute only.
A program may use at most 64 MiB of HBM per device.

v0:
```python
import jax
import jax.numpy as jnp
from jax import lax
from jax.sharding import PartitionSpec as P

HEAD_DIM = 128


def attend_block(state_now, query_heads, key_rows, value_rows, heads_local):
    running_max, totals, accumulated = state_now
    key_count = key_rows.shape[0]
    key_heads = key_rows.reshape(key_count, heads_local, HEAD_DIM)
    value_heads = value_rows.reshape(key_count, heads_local, HEAD_DIM)
    scores = jnp.einsum(
        "qhd,khd->qhk", query_heads, key_heads, preferred_element_type=jnp.float32
    ) * HEAD_DIM ** (-0.5)
    highest = jnp.maximum(running_max, jnp.max(scores, axis=-1))
    expd = jnp.exp(scores - highest[..., None])
    totals = jnp.sum(expd, axis=-1)
    accumulated = jnp.einsum(
        "qhk,khd->qhd", expd.astype(jnp.bfloat16), value_heads, preferred_element_type=jnp.float32
    )
    return (highest, totals, accumulated)


def on_device(queries, keys, vals, out_weight, gate):
    local_queries, local_keys, local_vals = (
        lax.all_to_all(queries, "tp", split_axis=1, concat_axis=0, tiled=True),
        lax.all_to_all(keys, "tp", split_axis=1, concat_axis=0, tiled=True),
        lax.all_to_all(vals, "tp", split_axis=1, concat_axis=0, tiled=True),
    )
    token_local = local_queries.shape[0]
    head_width = local_queries.shape[1]
    heads_local = head_width // HEAD_DIM
    query_heads = local_queries.reshape(token_local, heads_local, HEAD_DIM)
    start_state = (
        jnp.full((token_local, heads_local), -1e30, jnp.float32),
        jnp.zeros((token_local, heads_local), jnp.float32),
        jnp.zeros((token_local, heads_local, HEAD_DIM), jnp.float32),
    )
    every_key, every_value = (
        lax.all_gather(local_keys, "ctx", axis=0, tiled=True),
        lax.all_gather(local_vals, "ctx", axis=0, tiled=True),
    )
    final_state = attend_block(start_state, query_heads, every_key, every_value, heads_local)
    totals = final_state[1]
    accumulated = final_state[2]
    attended = (
        (accumulated / totals[..., None]).astype(jnp.bfloat16).reshape(token_local, head_width)
    )
    product = jnp.dot(
        lax.all_gather(attended, "tp", axis=1, tiled=True),
        out_weight,
        preferred_element_type=jnp.float32,
    )
    return (product * gate[None, :]).astype(jnp.bfloat16)


def solution(mesh):
    return jax.shard_map(
        on_device,
        mesh=mesh,
        in_specs=(
            P(("ctx", "tp"), None),
            P(("ctx", "tp"), None),
            P(("ctx", "tp"), None),
            P(None, "tp"),
            P("tp"),
        ),
        out_specs=P("ctx", "tp"),
        check_vma=False,
    )
```

profile of v0, /device:TPU:1, one launch (start us, length us, event | category | flops | bytes accessed | tf_op | source)
XLA Modules:
  0.0 2051.4 jit_solution(8343478045733496193)
XLA Ops:
  6.5 0.0 all-gather.3.cloned.1.call-start
  6.5 24.5 %all_to_all.54 = bf16[8,4,640]{2,0,1:T(8,128)(2,1)} all-to-all(bf16[8,4,640]{2,0,1:T(8,128)(2,1)} %bitcast.37), channel_id=1, replica_groups=mesh['ctx'=192,'tp'=4] {'tp'}, dimensions={1} | all-to-all | bytes 81920 | tf_op jit(solution)/shard_map/all_to_all | solution.py:29
  31.0 0.0 all-gather.3.cloned.1.call-update
  31.1 0.0 all-gather.5.cloned.1.call-start
  31.1 13.1 all_to_all.55
  44.2 0.0 all-gather.5.cloned.1.call-update
  44.2 12.4 all_to_all.56
  56.6 0.1 reshape.28
  56.7 858.3 %all-gather.3.cloned.1.call-done = bf16[6144,640]{1,0:T(8,128)(2,1)} async-done(((bf16[32,640]{1,0:T(8,128)(2,1)}), bf16[6144,640]{1,0:T(8,128)(2,1)}) %all-gather.3.cloned.1.call-update) | async-done | bytes 7864336 | tf_op jit(solution)/shard_map/all_gather | solution.py:42
  915.0 10.7 copy.12
  925.7 4.5 fusion.20
  930.1 0.0 copy-start
  930.1 1.9 copy-done
  932.0 0.7 fusion.1
  932.7 971.4 %all-gather.5.cloned.1.call-done = bf16[6144,640]{1,0:T(8,128)(2,1)} async-done(((bf16[32,640]{1,0:T(8,128)(2,1)}), bf16[6144,640]{1,0:T(8,128)(2,1)}) %all-gather.5.cloned.1.call-update) | async-done | bytes 7864336 | tf_op jit(solution)/shard_map/all_gather | solution.py:43
  1904.1 10.7 copy.15
  1914.7 0.0 copy-start.1
  1914.7 7.3 fusion.16
  1922.0 117.8 %all_gather.11 = bf16[32,2560]{1,0:T(8,128)(2,1)S(1)} all-gather(bf16[32,640]{1,0:T(8,128)(2,1)S(1)} %bitcast.36), channel_id=1, replica_groups=mesh['ctx'=192,'tp'=4] {'tp'}, dimensions={1}, use_global_device_ids=true | all-gather | bytes 204800 | tf_op jit(solution)/shard_map/all_gather | solution.py:52
  2039.9 0.0 copy-done.1
  2039.9 4.7 fusion.3
  (2 shorter events, 0.0 us)
Async XLA Ops:
  6.5 908.4 %all-gather.3.cloned.1.call-start = ((), (), s32[]{:S(2)}) async-start(), calls=%async_computation.3 | async-start | bytes 7905280 | tf_op jit(solution)/shard_map/all_gather | solution.py:42
  31.1 1873.0 %all-gather.5.cloned.1.call-start = ((), (), s32[]{:S(2)}) async-start(), calls=%async_computation.4 | async-start | bytes 7905280 | tf_op jit(solution)/shard_map/all_gather | solution.py:43
  930.1 1.9 copy-start
  1914.7 125.1 %copy-start.1 = (f32[1280]{0:T(1024)S(1)}, f32[1280]{0:T(1024)}, u32[]{:S(2)}) copy-start(f32[1280]{0:T(1024)} %param.9) | copy-start | bytes 15364
Sparse Core Ops, SparseCore 0:
  31.2 883.7 all-gather.2
  917.4 986.6 all-gather.4
where the time goes:
time: 2050 us
  waiting for transfers between devices  1830 us (89%)
  blocking collectives  168 us (8%)
  local copies, waits for them, and re-layouts  23.3 us (1%)
    all_gather x1, waiting for transfers between devices, on_device(): lax.all_gather(local_vals, 'ctx', axis=0, tiled=True)  971 us
    all_gather x1, waiting for transfers between devices, on_device(): lax.all_gather(local_keys, 'ctx', axis=0, tiled=True)  858 us
    all_gather x1, blocking collectives, on_device(): lax.all_gather(attended, 'tp', axis=1, tiled=True)  118 us
  transfers between devices with their start and end apart: 2, of which 2 were waited for; matrix products, arithmetic and copies ran while one was open for 1% of the time, Pallas kernels for 0%

commit v1 on v0

v1 whole, which is shorter than its diff:
```python
import jax
import jax.numpy as jnp
from jax import lax
from jax.experimental import pallas as pl
from jax.experimental.pallas import tpu as pltpu
from jax.sharding import Mesh, PartitionSpec as P

HEAD_DIM = 128
LOG2E = 1.4426950408889634
SCALE = HEAD_DIM ** -0.5
QUERY_AXES = ("y",)
KEY_AXES = ("zl", "x")
SUM_LANE = 8
PIECE_LANES = 16


def split_pieces(stats):
    high = stats.astype(jnp.bfloat16).astype(jnp.float32)
    rest = stats - high
    middle = rest.astype(jnp.bfloat16).astype(jnp.float32)
    low = rest - middle
    lane = lax.broadcasted_iota(jnp.int32, stats.shape, 1)
    spread = jnp.where(
        lane < PIECE_LANES,
        high,
        jnp.where(
            lane < 2 * PIECE_LANES,
            pltpu.roll(middle, PIECE_LANES, 1),
            pltpu.roll(low, 2 * PIECE_LANES, 1),
        ),
    )
    return spread.astype(jnp.bfloat16)


def attend_kernel(q_ref, own_ref, other_ref, out_ref):
    groups, tokens, width = q_ref.shape
    heads = width // HEAD_DIM
    rows = groups * tokens
    lane = lax.broadcasted_iota(jnp.int32, (rows, HEAD_DIM), 1)
    stats = jnp.zeros((rows, HEAD_DIM), jnp.float32)
    for head in range(heads):
        columns = pl.ds(head * HEAD_DIM, HEAD_DIM)
        query = q_ref[:, :, columns].reshape(rows, HEAD_DIM)
        scores, values = [], []
        for ref in (own_ref, other_ref):
            half = ref.shape[1] // 2
            key = ref[:, :half, columns].reshape(ref.shape[0] * half, HEAD_DIM)
            values.append(ref[:, half:, columns].reshape(ref.shape[0] * half, HEAD_DIM))
            scores.append(
                lax.dot_general(
                    query, key, (((1,), (1,)), ((), ())), preferred_element_type=jnp.float32
                )
            )
        highest = jnp.maximum(
            jnp.max(scores[0], axis=1, keepdims=True), jnp.max(scores[1], axis=1, keepdims=True)
        )
        total = jnp.zeros((rows, 1), jnp.float32)
        summed = jnp.zeros((rows, HEAD_DIM), jnp.float32)
        for score, value in zip(scores, values):
            expd = jnp.exp2((score - highest) * (SCALE * LOG2E))
            total += jnp.sum(expd, axis=1, keepdims=True)
            summed += jnp.dot(
                expd.astype(jnp.bfloat16), value, preferred_element_type=jnp.float32
            )
        out_ref[:, :, columns] = summed.astype(jnp.bfloat16).reshape(groups, tokens, HEAD_DIM)
        stats = jnp.where(lane == head, highest, stats)
        stats = jnp.where(lane == SUM_LANE + head, total, stats)
    out_ref[:, :, pl.ds(width, HEAD_DIM)] = split_pieces(stats).reshape(groups, tokens, HEAD_DIM)


def combine_kernel(part_ref, out_ref):
    groups, tokens, width = part_ref.shape
    width = width - HEAD_DIM
    heads = width // HEAD_DIM
    pieces = part_ref[:, :, pl.ds(width, HEAD_DIM)].astype(jnp.float32)
    pieces = pieces.reshape(groups * tokens, HEAD_DIM)
    stats = (
        pieces
        + pltpu.roll(pieces, HEAD_DIM - PIECE_LANES, 1)
        + pltpu.roll(pieces, HEAD_DIM - 2 * PIECE_LANES, 1)
    )
    maxima = stats.reshape(groups, tokens, HEAD_DIM)
    sums = pltpu.roll(stats, HEAD_DIM - SUM_LANE, 1).reshape(groups, tokens, HEAD_DIM)
    highest = jnp.max(maxima, axis=0, keepdims=True)
    weight = jnp.exp2((maxima - highest) * (SCALE * LOG2E))
    total = jnp.sum(weight * sums, axis=0)
    for head in range(heads):
        columns = pl.ds(head * HEAD_DIM, HEAD_DIM)
        part = part_ref[:, :, columns].astype(jnp.float32)
        summed = jnp.sum(part * weight[:, :, head : head + 1], axis=0)
        out_ref[:, columns] = (summed / total[:, head : head + 1]).astype(jnp.bfloat16)


def spread_to(block, count):
    return jnp.broadcast_to(block[None], (count, *block.shape))


def on_device(queries, keys, vals, out_weight, gate):
    parts = lax.axis_size("tp")
    rows, width = queries.shape
    head_width = width // parts
    stacked = jnp.stack([queries, keys, vals], axis=0)
    stacked = stacked.reshape(3, rows, parts, head_width).transpose(2, 0, 1, 3)
    stacked = stacked.reshape(parts, 3 * rows, head_width)
    local = lax.all_to_all(stacked, "tp", split_axis=0, concat_axis=0, tiled=True)
    local = local.reshape(parts, 3, rows, head_width).transpose(1, 0, 2, 3)
    tokens = parts * rows
    local = local.reshape(3 * tokens, head_width)
    key_value = lax.all_to_all(
        spread_to(local[tokens:], lax.axis_size(KEY_AXES)),
        KEY_AXES, split_axis=0, concat_axis=0, tiled=True,
    )
    other = lax.ppermute(key_value, "c", [(0, 1), (1, 0)])
    group = lax.all_to_all(
        spread_to(local[:tokens], lax.axis_size(QUERY_AXES)),
        QUERY_AXES, split_axis=0, concat_axis=0, tiled=True,
    )
    partial = pl.pallas_call(
        attend_kernel,
        out_shape=jax.ShapeDtypeStruct((*group.shape[:2], head_width + HEAD_DIM), jnp.bfloat16),
        name="attend",
    )(group, key_value, other)
    partial = lax.all_to_all(partial, QUERY_AXES, split_axis=0, concat_axis=0, tiled=True)
    attended = pl.pallas_call(
        combine_kernel,
        out_shape=jax.ShapeDtypeStruct((tokens, head_width), jnp.bfloat16),
        name="combine",
    )(partial)
    product = jnp.dot(
        lax.all_gather(attended, "tp", axis=1, tiled=True),
        out_weight,
        preferred_element_type=jnp.float32,
    )
    return (product * gate[None, :]).astype(jnp.bfloat16)


def solution(mesh):
    ctx = ("zl", "y", "x", "c")
    fine = Mesh(mesh.devices.reshape(3, 8, 4, 2, 4), (*ctx, "tp"))
    return jax.shard_map(
        on_device,
        mesh=fine,
        in_specs=(
            P((*ctx, "tp"), None),
            P((*ctx, "tp"), None),
            P((*ctx, "tp"), None),
            P(None, "tp"),
            P("tp"),
        ),
        out_specs=P(ctx, "tp"),
        check_vma=False,
    )
```

time: 2050 us -> 120 us (0.06)
  waiting for transfers between devices: 1830 us -> 0.01 us
  blocking collectives: 168 us -> 98.3 us
  local copies, waits for them, and re-layouts: 23.3 us -> 1.15 us
    all_gather x2 -> x0, waiting for transfers between devices: 1830 us -> none  [the longest x1 971 us: on_device(): lax.all_gather(local_vals, 'ctx', axis=0, tiled=True)]
    all_gather x1, blocking collectives: 118 us -> 13.6 us  [on_device(): lax.all_gather(attended, 'tp', axis=1, tiled=True)]
    all_to_all x3 -> x4, blocking collectives: 50 us -> 84.8 us  [the longest x1 24.6 us: on_device(): lax.all_to_all(stacked, 'tp', split_axis=0, concat_axis=0, tiled=True)]
    all_gather x2 -> x0, local copies, waits for them, and re-layouts: 21.3 us -> none  [the longest x1 10.7 us: on_device(): lax.all_gather(local_keys, 'ctx', axis=0, tiled=True)]
  transfers between devices with their start and end apart: 2 -> 1, of which waited for: 2 -> 0; matrix products, arithmetic and copies ran while one was open for 1% -> 0% of each run, Pallas kernels for 0% -> 0%
where the time goes in v1:
time: 120 us; the launch traced here: 118 us
  blocking collectives  98.3 us (82%)
  Pallas kernels  6.71 us (6%)
  starting transfers between devices  6.54 us (5%)
  matrix products  4.72 us (4%)
    all_to_all x1, blocking collectives, on_device(): lax.all_to_all(stacked, 'tp', split_axis=0, concat_axis=0, tiled=True)  24.6 us
    all_to_all x1, blocking collectives, on_device(): lax.all_to_all(spread_to(local[tokens:], lax.axis_size(KEY_AXES)), KEY_AX...  21.3 us
    all_to_all x1, blocking collectives, on_device(): lax.all_to_all(spread_to(local[:tokens], lax.axis_size(QUERY_AXES)), QUER...  20.5 us
    all_to_all x1, blocking collectives, on_device(): lax.all_to_all(partial, QUERY_AXES, split_axis=0, concat_axis=0, tiled=True)  18.5 us
    all_gather x1, blocking collectives, on_device(): lax.all_gather(attended, 'tp', axis=1, tiled=True)  13.6 us
    ppermute x1, starting transfers between devices, on_device(): other = lax.ppermute(key_value, 'c', [(0, 1), (1, 0)])  6.54 us
    dot_general x1, matrix products, on_device(): jnp.dot(lax.all_gather(attended, 'tp', axis=1, tiled=True), out_weight, p...  4.72 us
    pallas_call x1, Pallas kernels, on_device(): pl.pallas_call(attend_kernel, out_shape=jax.ShapeDtypeStruct((*group.shap...  4.71 us
  transfers between devices with their start and end apart: 1, of which 0 were waited for; matrix products, arithmetic and copies ran while one was open for 0% of the time, Pallas kernels for 0%

profile of v1, /device:TPU:1, one launch (start us, length us, event | category | flops | bytes accessed | tf_op | source)
XLA Modules:
  0.0 118.4 jit_solution(6313920269598835872)
XLA Ops:
  0.0 0.0 copy-start.2
  0.0 0.9 maximum_bitcast_fusion
  0.9 24.6 %all_to_all.20 = bf16[4,24,640]{2,1,0:T(8,128)(2,1)S(1)} all-to-all(bf16[4,24,640]{2,1,0:T(8,128)(2,1)S(1)} %maximum_bitcast_fusion), channel_id=1, replica_groups=mesh['zl'=3,'y'=8,'x'=4,'c'=2,'tp'=4] {'tp'}, dimensions={0} | all-to-all | bytes 245760 | tf_op jit(solution)/shard_map/all_to_all | solution.py:105
  25.4 0.1 broadcast_in_dim.20
  25.5 21.3 %all_to_all.21.own_ref = bf16[12,64,640]{2,1,0:T(8,128)(2,1)S(1)} all-to-all(bf16[12,64,640]{2,1,0:T(8,128)(2,1)S(1)} %broadcast_in_dim.20), channel_id=1, replica_groups=mesh['zl'=3,'y'=8,'x'=4,'c'=2,'tp'=4] {'zl','x'}, dimensions={0} | all-to-all | bytes 1966080 | tf_op jit(solution)/shard_map/all_to_all | solution.py:109
  46.8 0.0 copy-start
  46.8 6.5 %collective-permute-start = (bf16[12,64,640]{2,1,0:T(8,128)(2,1)S(1)}, bf16[12,64,640]{2,1,0:T(8,128)(2,1)S(1)}, u32[]{:S(2)}, u32[]{:S(2)}) collective-permute-start(bf16[12,64,640]{2,1,0:T(8,128)(2,1)S(1)} %all_to_all.21.own_ref), channel_id=1, source_target_pairs={{0,4},{4,0},{1,5},{5,1},{2,6},{6,2},{3,7},{7,3},{8,12},{12,8},{9,1... | collective-permute-start | bytes 2949128 | tf_op jit(solution)/shard_map/ppermute | solution.py:113
  53.4 20.5 %all_to_all.22.q_ref = bf16[8,32,640]{2,1,0:T(8,128)(2,1)} all-to-all(bf16[8,32,640]{2,1,0:T(8,128)(2,1)S(1)} %broadcast_in_dim.18), channel_id=1, replica_groups=mesh['zl'=3,'y'=8,'x'=4,'c'=2,'tp'=4] {'y'}, dimensions={0} | all-to-all | bytes 655360 | tf_op jit(solution)/shard_map/all_to_all | solution.py:114
  73.9 0.0 collective-permute-done.other_ref
  73.9 0.0 copy-done
  73.9 0.0 copy-start.1
  73.9 1.0 copy-done.1
  74.9 4.7 %attend.1 = bf16[8,32,768]{2,1,0:T(8,128)(2,1)} custom-call(bf16[8,32,640]{2,1,0:T(8,128)(2,1)} %all_to_all.22.q_ref, bf16[12,64,640]{2,1,0:T(8,128)(2,1)} %copy-done, bf16[12,64,640]{2,1,0:T(8,128)(2,1)} %copy-done.1), custom_call_target="tpu_custom_call" | custom-call | tf_op jit(solution)/shard_map/attend/pallas_call | solution.py:118
  79.6 18.5 %all_to_all.23.part_ref = bf16[8,32,768]{2,1,0:T(8,128)(2,1)} all-to-all(bf16[8,32,768]{2,1,0:T(8,128)(2,1)} %attend.1), channel_id=1, replica_groups=mesh['zl'=3,'y'=8,'x'=4,'c'=2,'tp'=4] {'y'}, dimensions={0} | all-to-all | bytes 786432 | tf_op jit(solution)/shard_map/all_to_all | solution.py:123
  98.1 2.0 %combine.1 = bf16[32,640]{1,0:T(8,128)(2,1)} custom-call(bf16[8,32,768]{2,1,0:T(8,128)(2,1)} %all_to_all.23.part_ref), custom_call_target="tpu_custom_call" | custom-call | tf_op jit(solution)/shard_map/combine/pallas_call | solution.py:124
  100.1 13.6 %all_gather.3 = bf16[32,2560]{1,0:T(8,128)(2,1)S(1)} all-gather(bf16[32,640]{1,0:T(8,128)(2,1)} %combine.1), channel_id=1, replica_groups=mesh['zl'=3,'y'=8,'x'=4,'c'=2,'tp'=4] {'tp'}, dimensions={1}, use_global_device_ids=true | all-gather | bytes 204800 | tf_op jit(solution)/shard_map/all_gather | solution.py:130
  113.7 0.0 copy-done.2
  113.7 4.7 %fusion = bf16[32,1280]{1,0:T(8,128)(2,1)} fusion(bf16[32,2560]{1,0:T(8,128)(2,1)S(1)} %all_gather.3, bf16[2560,1280]{1,0:T(8,128)(2,1)} %param.8, f32[1280]{0:T(1024)S(1)} %copy-done.2), kind=kOutput, calls=%fused_computation.1 | convolution fusion | flops 209797120 | bytes 6804480 | tf_op jit(solution)/shard_map/dot_general | solution.py:129
  (4 shorter events, 0.0 us)
Async XLA Ops:
  0.0 113.7 %copy-start.2 = (f32[1280]{0:T(1024)S(1)}, f32[1280]{0:T(1024)}, u32[]{:S(2)}) copy-start(f32[1280]{0:T(1024)} %param.9) | copy-start | bytes 15364
  46.8 27.1 %copy-start = (bf16[12,64,640]{2,1,0:T(8,128)(2,1)}, bf16[12,64,640]{2,1,0:T(8,128)(2,1)S(1)}, u32[]{:S(2)}) copy-start(bf16[12,64,640]{2,1,0:T(8,128)(2,1)S(1)} %all_to_all.21.own_ref) | copy-start | bytes 2949124
  46.8 27.1 %collective-permute-start = (bf16[12,64,640]{2,1,0:T(8,128)(2,1)S(1)}, bf16[12,64,640]{2,1,0:T(8,128)(2,1)S(1)}, u32[]{:S(2)}, u32[]{:S(2)}) collective-permute-start(bf16[12,64,640]{2,1,0:T(8,128)(2,1)S(1)} %all_to_all.21.own_ref), channel_id=1, source_target_pairs={{0,4},{4,0},{1,5},{5,1},{2,6},{6,2},{3,7},{7,3},{8,12},{12,8},{9,1... | collective-permute-start | bytes 2949128 | tf_op jit(solution)/shard_map/ppermute | solution.py:113
  73.9 1.0 copy-start.1

commit v2 on v1

--- a/solution.py
+++ b/solution.py
@@ -12,6 +12,7 @@
 KEY_AXES = ("zl", "x")
 SUM_LANE = 8
 PIECE_LANES = 16
+KERNEL_VMEM = 16 * 1024 * 1024
 
 
 def split_pieces(stats):
@@ -110,20 +111,24 @@
         spread_to(local[tokens:], lax.axis_size(KEY_AXES)),
         KEY_AXES, split_axis=0, concat_axis=0, tiled=True,
     )
+    group = lax.all_gather(local[:tokens], QUERY_AXES, axis=0, tiled=False)
+    key_value, group = lax.optimization_barrier((key_value, group))
     other = lax.ppermute(key_value, "c", [(0, 1), (1, 0)])
-    group = lax.all_to_all(
-        spread_to(local[:tokens], lax.axis_size(QUERY_AXES)),
-        QUERY_AXES, split_axis=0, concat_axis=0, tiled=True,
-    )
     partial = pl.pallas_call(
         attend_kernel,
         out_shape=jax.ShapeDtypeStruct((*group.shape[:2], head_width + HEAD_DIM), jnp.bfloat16),
+        in_specs=[pl.BlockSpec(memory_space=pltpu.VMEM)] * 3,
+        out_specs=pl.BlockSpec(memory_space=pltpu.VMEM),
+        compiler_params=pltpu.CompilerParams(vmem_limit_bytes=KERNEL_VMEM),
         name="attend",
     )(group, key_value, other)
     partial = lax.all_to_all(partial, QUERY_AXES, split_axis=0, concat_axis=0, tiled=True)
     attended = pl.pallas_call(
         combine_kernel,
         out_shape=jax.ShapeDtypeStruct((tokens, head_width), jnp.bfloat16),
+        in_specs=[pl.BlockSpec(memory_space=pltpu.VMEM)],
+        out_specs=pl.BlockSpec(memory_space=pltpu.VMEM),
+        compiler_params=pltpu.CompilerParams(vmem_limit_bytes=KERNEL_VMEM),
         name="combine",
     )(partial)
     product = jnp.dot(

time: 120 us -> 110 us (0.917)
  the two profiles are of different devices: /device:TPU:1 before, /device:TPU:2 now
where the time goes in v2:
time: 110 us; the launch traced here: 109 us
  blocking collectives  89.4 us (81%)
  starting transfers between devices  7.75 us (7%)
  matrix products  4.72 us (4%)
  Pallas kernels  2.72 us (2%)
  waiting for transfers between devices  2.53 us (2%)
  local copies, waits for them, and re-layouts  1.1 us (1%)
    all_to_all x1, blocking collectives, on_device(): lax.all_to_all(stacked, 'tp', split_axis=0, concat_axis=0, tiled=True)  26.6 us
    all_gather x1, blocking collectives, on_device(): group = lax.all_gather(local[:tokens], QUERY_AXES, axis=0, tiled=False)  26.5 us
    all_to_all x1, blocking collectives, on_device(): lax.all_to_all(partial, QUERY_AXES, split_axis=0, concat_axis=0, tiled=True)  20.3 us
    all_gather x1, blocking collectives, on_device(): lax.all_gather(attended, 'tp', axis=1, tiled=True)  16 us
    all_to_all x1, starting transfers between devices, on_device(): lax.all_to_all(spread_to(local[tokens:], lax.axis_size(KEY_AXES)), KEY_AX...  5.84 us
    dot_general x1, matrix products, on_device(): jnp.dot(lax.all_gather(attended, 'tp', axis=1, tiled=True), out_weight, p...  4.72 us
    ppermute x1, waiting for transfers between devices, on_device(): other = lax.ppermute(key_value, 'c', [(0, 1), (1, 0)])  2.53 us
    pallas_call x1, Pallas kernels, on_device(): pl.pallas_call(attend_kernel, out_shape=jax.ShapeDtypeStruct((*group.shap...  2.33 us
  transfers between devices with their start and end apart: 2, of which 1 were waited for; matrix products, arithmetic and copies ran while one was open for 0% of the time, Pallas kernels for 0%

profile of v2, /device:TPU:2, one launch (start us, length us, event | category | flops | bytes accessed | tf_op | source)
XLA Modules:
  0.0 109.1 jit_solution(15452734106801487194)
XLA Ops:
  0.0 0.0 copy-start
  0.0 0.9 maximum_bitcast_fusion
  0.9 26.6 %all_to_all.15 = bf16[4,24,640]{2,1,0:T(8,128)(2,1)S(1)} all-to-all(bf16[4,24,640]{2,1,0:T(8,128)(2,1)S(1)} %maximum_bitcast_fusion), channel_id=1, replica_groups=mesh['zl'=3,'y'=8,'x'=4,'c'=2,'tp'=4] {'tp'}, dimensions={0} | all-to-all | bytes 245760 | tf_op jit(solution)/shard_map/all_to_all | solution.py:106
  27.5 1.1 broadcast_in_dim.10
  28.5 5.8 %all-to-all-start.1 = ((bf16[12,64,640]{2,1,0:T(8,128)(2,1)}), bf16[12,64,640]{2,1,0:T(8,128)(2,1)S(1)}, u32[]{:S(2)}, u32[]{:S(2)}) async-start(bf16[12,64,640]{2,1,0:T(8,128)(2,1)} %broadcast_in_dim.10), calls=%async_computation.1 | async-start | bytes 1966080 | tf_op jit(solution)/shard_map/all_to_all | solution.py:110
  34.4 26.5 %all_gather.10.q_ref = bf16[8,32,640]{2,1,0:T(8,128)(2,1)S(1)} all-gather(bf16[1,32,640]{2,1,0:T(8,128)(2,1)S(1)} %slice_bitcast_fusion), channel_id=1, replica_groups=mesh['zl'=3,'y'=8,'x'=4,'c'=2,'tp'=4] {'y'}, dimensions={0}, use_global_device_ids=true | all-gather | bytes 368640 | tf_op jit(solution)/shard_map/all_gather | solution.py:114
  60.9 0.0 all-to-all-done.1.own_ref
  60.9 1.9 %collective-permute-start = (bf16[12,64,640]{2,1,0:T(8,128)(2,1)S(1)}, bf16[12,64,640]{2,1,0:T(8,128)(2,1)S(1)}, u32[]{:S(2)}, u32[]{:S(2)}) collective-permute-start(bf16[12,64,640]{2,1,0:T(8,128)(2,1)S(1)} %all-to-all-done.1.own_ref), channel_id=1, source_target_pairs={{0,4},{4,0},{1,5},{5,1},{2,6},{6,2},{3,7},{7,3},{8,12},{12,8},{9,1... | collective-permute-start | bytes 2949128 | tf_op jit(solution)/shard_map/ppermute | solution.py:116
  62.8 2.5 %collective-permute-done.other_ref = bf16[12,64,640]{2,1,0:T(8,128)(2,1)S(1)} collective-permute-done((bf16[12,64,640]{2,1,0:T(8,128)(2,1)S(1)}, bf16[12,64,640]{2,1,0:T(8,128)(2,1)S(1)}, u32[]{:S(2)}, u32[]{:S(2)}) %collective-permute-start) | collective-permute-done | bytes 983072 | tf_op jit(solution)/shard_map/ppermute | solution.py:116
  65.3 2.3 %attend.1 = bf16[8,32,768]{2,1,0:T(8,128)(2,1)S(1)} custom-call(bf16[8,32,640]{2,1,0:T(8,128)(2,1)S(1)} %all_gather.10.q_ref, bf16[12,64,640]{2,1,0:T(8,128)(2,1)S(1)} %all-to-all-done.1.own_ref, bf16[12,64,640]{2,1,0:T(8,128)(2,1)S(1)} %collective-permute-done.other_ref), custom_call_target="tpu_custom_call" | custom-call | tf_op jit(solution)/shard_map/attend/pallas_call | solution.py:117
  67.7 20.3 %all_to_all.16.part_ref = bf16[8,32,768]{2,1,0:T(8,128)(2,1)S(1)} all-to-all(bf16[8,32,768]{2,1,0:T(8,128)(2,1)S(1)} %attend.1), channel_id=1, replica_groups=mesh['zl'=3,'y'=8,'x'=4,'c'=2,'tp'=4] {'y'}, dimensions={0} | all-to-all | bytes 786432 | tf_op jit(solution)/shard_map/all_to_all | solution.py:125
  88.0 0.4 combine.1
  88.4 16.0 %all_gather.11 = bf16[32,2560]{1,0:T(8,128)(2,1)S(1)} all-gather(bf16[32,640]{1,0:T(8,128)(2,1)S(1)} %combine.1), channel_id=1, replica_groups=mesh['zl'=3,'y'=8,'x'=4,'c'=2,'tp'=4] {'tp'}, dimensions={1}, use_global_device_ids=true | all-gather | bytes 204800 | tf_op jit(solution)/shard_map/all_gather | solution.py:135
  104.4 0.0 copy-done
  104.4 4.7 %fusion = bf16[32,1280]{1,0:T(8,128)(2,1)} fusion(bf16[32,2560]{1,0:T(8,128)(2,1)S(1)} %all_gather.11, bf16[2560,1280]{1,0:T(8,128)(2,1)} %param.8, f32[1280]{0:T(1024)S(1)} %copy-done), kind=kOutput, calls=%fused_computation.1 | convolution fusion | flops 209797120 | bytes 6804480 | tf_op jit(solution)/shard_map/dot_general | solution.py:134
  (3 shorter events, 0.0 us)
Async XLA Ops:
  0.0 104.4 %copy-start = (f32[1280]{0:T(1024)S(1)}, f32[1280]{0:T(1024)}, u32[]{:S(2)}) copy-start(f32[1280]{0:T(1024)} %param.9) | copy-start | bytes 15364
  28.5 32.3 %all-to-all-start.1 = ((bf16[12,64,640]{2,1,0:T(8,128)(2,1)}), bf16[12,64,640]{2,1,0:T(8,128)(2,1)S(1)}, u32[]{:S(2)}, u32[]{:S(2)}) async-start(bf16[12,64,640]{2,1,0:T(8,128)(2,1)} %broadcast_in_dim.10), calls=%async_computation.1 | async-start | bytes 1966080 | tf_op jit(solution)/shard_map/all_to_all | solution.py:110
  60.9 4.5 %collective-permute-start = (bf16[12,64,640]{2,1,0:T(8,128)(2,1)S(1)}, bf16[12,64,640]{2,1,0:T(8,128)(2,1)S(1)}, u32[]{:S(2)}, u32[]{:S(2)}) collective-permute-start(bf16[12,64,640]{2,1,0:T(8,128)(2,1)S(1)} %all-to-all-done.1.own_ref), channel_id=1, source_target_pairs={{0,4},{4,0},{1,5},{5,1},{2,6},{6,2},{3,7},{7,3},{8,12},{12,8},{9,1... | collective-permute-start | bytes 2949128 | tf_op jit(solution)/shard_map/ppermute | solution.py:116

commit v3 on v2

--- a/solution.py
+++ b/solution.py
@@ -8,10 +8,12 @@
 HEAD_DIM = 128
 LOG2E = 1.4426950408889634
 SCALE = HEAD_DIM ** -0.5
-QUERY_AXES = ("y",)
-KEY_AXES = ("zl", "x")
+QUERY_AXES = ("x", "zl")
+KEY_AXES = ("y",)
 SUM_LANE = 8
 PIECE_LANES = 16
+PART_PIECES = 2
+MIX_VMEM = 59 * 1024 * 1024
 KERNEL_VMEM = 16 * 1024 * 1024
 
 
@@ -92,6 +94,27 @@
         out_ref[:, columns] = (summed / total[:, head : head + 1]).astype(jnp.bfloat16)
 
 
+def mix_kernel(attended_ref, gate_ref, weight_ref, out_ref, held_ref, semaphores):
+    parts, rows, width = attended_ref.shape
+    depth = width // PART_PIECES
+    copies = []
+    for piece in range(parts * PART_PIECES):
+        span = pl.ds(piece * depth, depth)
+        copy = pltpu.make_async_copy(weight_ref.at[span], held_ref.at[span], semaphores.at[piece])
+        copy.start()
+        copies.append(copy)
+    product = jnp.zeros(out_ref.shape, jnp.float32)
+    for piece, copy in enumerate(copies):
+        part, start = piece // PART_PIECES, piece % PART_PIECES * depth
+        copy.wait()
+        product += jnp.dot(
+            attended_ref[part, :, pl.ds(start, depth)],
+            held_ref[pl.ds(piece * depth, depth)],
+            preferred_element_type=jnp.float32,
+        )
+    out_ref[...] = (product * gate_ref[...]).astype(jnp.bfloat16)
+
+
 def spread_to(block, count):
     return jnp.broadcast_to(block[None], (count, *block.shape))
 
@@ -111,7 +134,9 @@
         spread_to(local[tokens:], lax.axis_size(KEY_AXES)),
         KEY_AXES, split_axis=0, concat_axis=0, tiled=True,
     )
-    group = lax.all_gather(local[:tokens], QUERY_AXES, axis=0, tiled=False)
+    group = local[:tokens][None]
+    for axis in reversed(QUERY_AXES):
+        group = lax.all_gather(group, axis, axis=0, tiled=True)
     key_value, group = lax.optimization_barrier((key_value, group))
     other = lax.ppermute(key_value, "c", [(0, 1), (1, 0)])
     partial = pl.pallas_call(
@@ -131,12 +156,23 @@
         compiler_params=pltpu.CompilerParams(vmem_limit_bytes=KERNEL_VMEM),
         name="combine",
     )(partial)
-    product = jnp.dot(
-        lax.all_gather(attended, "tp", axis=1, tiled=True),
-        out_weight,
-        preferred_element_type=jnp.float32,
-    )
-    return (product * gate[None, :]).astype(jnp.bfloat16)
+    parts_attended = lax.all_gather(attended, "tp", axis=0, tiled=False)
+    return pl.pallas_call(
+        mix_kernel,
+        out_shape=jax.ShapeDtypeStruct((tokens, out_weight.shape[1]), jnp.bfloat16),
+        in_specs=[
+            pl.BlockSpec(memory_space=pltpu.VMEM),
+            pl.BlockSpec(memory_space=pltpu.VMEM),
+            pl.BlockSpec(memory_space=pltpu.HBM),
+        ],
+        out_specs=pl.BlockSpec(memory_space=pltpu.VMEM),
+        scratch_shapes=[
+            pltpu.VMEM(out_weight.shape, out_weight.dtype),
+            pltpu.SemaphoreType.DMA((parts * PART_PIECES,)),
+        ],
+        compiler_params=pltpu.CompilerParams(vmem_limit_bytes=MIX_VMEM),
+        name="mix",
+    )(parts_attended, gate[None, :], out_weight)
 
 
 def solution(mesh):

time: 110 us -> 106 us (0.964)
  the two profiles are of different devices: /device:TPU:2 before, /device:TPU:8 now
where the time goes in v3:
time: 106 us; the launch traced here: 105 us
  blocking collectives  66.5 us (63%)
  waiting for transfers between devices  15.3 us (14%)
  starting transfers between devices  13.5 us (13%)
  Pallas kernels  7.87 us (7%)
  local copies, waits for them, and re-layouts  1.5 us (1%)
    all_to_all x1, blocking collectives, on_device(): lax.all_to_all(stacked, 'tp', split_axis=0, concat_axis=0, tiled=True)  26.6 us
    all_gather x2, blocking collectives, on_device(): group = lax.all_gather(group, axis, axis=0, tiled=True)  22.4 us
    all_gather x1, blocking collectives, on_device(): parts_attended = lax.all_gather(attended, 'tp', axis=0, tiled=False)  17.5 us
    all_to_all x1, waiting for transfers between devices, on_device(): lax.all_to_all(partial, QUERY_AXES, split_axis=0, concat_axis=0, tiled=True)  13.2 us
    all_to_all x1, starting transfers between devices, on_device(): lax.all_to_all(spread_to(local[tokens:], lax.axis_size(KEY_AXES)), KEY_AX...  7.55 us
    pallas_call x1, Pallas kernels, on_device(): pl.pallas_call(mix_kernel, out_shape=jax.ShapeDtypeStruct((tokens, out_we...  4.8 us
    all_to_all x1, starting transfers between devices, on_device(): lax.all_to_all(partial, QUERY_AXES, split_axis=0, concat_axis=0, tiled=True)  4.01 us
    pallas_call x1, Pallas kernels, on_device(): pl.pallas_call(attend_kernel, out_shape=jax.ShapeDtypeStruct((*group.shap...  2.56 us
  transfers between devices with their start and end apart: 3, of which 2 were waited for; matrix products, arithmetic and copies ran while one was open for 1% of the time, Pallas kernels for 0%

profile of v3, /device:TPU:8, one launch (start us, length us, event | category | flops | bytes accessed | tf_op | source)
XLA Modules:
  0.0 105.5 jit_solution(8131542708782601369)
XLA Ops:
  0.0 0.0 copy-start
  0.0 0.9 maximum_bitcast_fusion
  0.9 26.6 %all_to_all.15 = bf16[4,24,640]{2,1,0:T(8,128)(2,1)S(1)} all-to-all(bf16[4,24,640]{2,1,0:T(8,128)(2,1)S(1)} %maximum_bitcast_fusion), channel_id=1, replica_groups=mesh['zl'=3,'y'=8,'x'=4,'c'=2,'tp'=4] {'tp'}, dimensions={0} | all-to-all | bytes 245760 | tf_op jit(solution)/shard_map/all_to_all | solution.py:129
  27.5 0.9 broadcast_in_dim.15
  28.4 7.5 %all-to-all-start.1 = ((bf16[8,64,640]{2,1,0:T(8,128)(2,1)}), bf16[8,64,640]{2,1,0:T(8,128)(2,1)S(1)}, u32[]{:S(2)}, u32[]{:S(2)}) async-start(bf16[8,64,640]{2,1,0:T(8,128)(2,1)} %broadcast_in_dim.15), calls=%async_computation.1 | async-start | bytes 1310720 | tf_op jit(solution)/shard_map/all_to_all | solution.py:133
  35.9 8.7 %all_gather.12 = bf16[3,32,640]{2,1,0:T(8,128)(2,1)S(1)} all-gather(bf16[1,32,640]{2,1,0:T(8,128)(2,1)S(1)} %slice_bitcast_fusion), channel_id=1, replica_groups=mesh['zl'=3,'y'=8,'x'=4,'c'=2,'tp'=4] {'zl'}, dimensions={0}, use_global_device_ids=true | all-gather | bytes 163840 | tf_op jit(solution)/shard_map/all_gather | solution.py:139
  44.6 13.7 %all_gather.13.q_ref = bf16[12,32,640]{2,1,0:T(8,128)(2,1)S(1)} all-gather(bf16[3,32,640]{2,1,0:T(8,128)(2,1)S(1)} %all_gather.12), channel_id=1, replica_groups=mesh['zl'=3,'y'=8,'x'=4,'c'=2,'tp'=4] {'x'}, dimensions={0}, use_global_device_ids=true | all-gather | bytes 614400 | tf_op jit(solution)/shard_map/all_gather | solution.py:139
  58.3 0.0 all-to-all-done.1.own_ref
  58.3 1.9 %collective-permute-start = (bf16[8,64,640]{2,1,0:T(8,128)(2,1)S(1)}, bf16[8,64,640]{2,1,0:T(8,128)(2,1)S(1)}, u32[]{:S(2)}, u32[]{:S(2)}) collective-permute-start(bf16[8,64,640]{2,1,0:T(8,128)(2,1)S(1)} %all-to-all-done.1.own_ref), channel_id=1, source_target_pairs={{0,4},{4,0},{1,5},{5,1},{2,6},{6,2},{3,7},{7,3},{8,12},{12,8},{9,1... | collective-permute-start | bytes 1966088 | tf_op jit(solution)/shard_map/ppermute | solution.py:141
  60.2 2.1 %collective-permute-done.other_ref = bf16[8,64,640]{2,1,0:T(8,128)(2,1)S(1)} collective-permute-done((bf16[8,64,640]{2,1,0:T(8,128)(2,1)S(1)}, bf16[8,64,640]{2,1,0:T(8,128)(2,1)S(1)}, u32[]{:S(2)}, u32[]{:S(2)}) %collective-permute-start) | collective-permute-done | bytes 655392 | tf_op jit(solution)/shard_map/ppermute | solution.py:141
  62.3 2.6 %attend.1 = bf16[12,32,768]{2,1,0:T(8,128)(2,1)} custom-call(bf16[12,32,640]{2,1,0:T(8,128)(2,1)S(1)} %all_gather.13.q_ref, bf16[8,64,640]{2,1,0:T(8,128)(2,1)S(1)} %all-to-all-done.1.own_ref, bf16[8,64,640]{2,1,0:T(8,128)(2,1)S(1)} %collective-permute-done.other_ref), custom_call_target="tpu_custom_call" | custom-call | tf_op jit(solution)/shard_map/attend/pallas_call | solution.py:142
  64.8 4.0 %all-to-all-start.2 = ((bf16[12,32,768]{2,1,0:T(8,128)(2,1)}), bf16[12,32,768]{2,1,0:T(8,128)(2,1)S(1)}, u32[]{:S(2)}, u32[]{:S(2)}) async-start(bf16[12,32,768]{2,1,0:T(8,128)(2,1)} %attend.1), calls=%async_computation.2 | async-start | bytes 1179648 | tf_op jit(solution)/shard_map/all_to_all | solution.py:150
  68.9 0.0 copy-done
  68.9 0.6 broadcast_in_dim.17.gate_ref
  69.4 13.2 %all-to-all-done.2.part_ref = bf16[12,32,768]{2,1,0:T(8,128)(2,1)S(1)} async-done(((bf16[12,32,768]{2,1,0:T(8,128)(2,1)}), bf16[12,32,768]{2,1,0:T(8,128)(2,1)S(1)}, u32[]{:S(2)}, u32[]{:S(2)}) %all-to-all-start.2) | async-done | bytes 589856 | tf_op jit(solution)/shard_map/all_to_all | solution.py:150
  82.7 0.5 combine.1
  83.2 17.5 %all-gather = bf16[128,640]{1,0:T(8,128)(2,1)} all-gather(bf16[32,640]{1,0:T(8,128)(2,1)S(1)} %combine.1), channel_id=2, replica_groups=mesh['zl'=3,'y'=8,'x'=4,'c'=2,'tp'=4] {'tp'}, dimensions={0}, use_global_device_ids=true | all-gather | bytes 204800 | tf_op jit(solution)/shard_map/all_gather | solution.py:159
  100.7 4.8 %mix.1 = bf16[32,1280]{1,0:T(8,128)(2,1)} custom-call(bf16[4,32,640]{2,1,0:T(8,128)(2,1)} %bitcast.14, f32[1,1280]{1,0:T(1,128)} %broadcast_in_dim.17.gate_ref, bf16[2560,1280]{1,0:T(8,128)(2,1)} %weight_ref.1), custom_call_target="tpu_custom_call" | custom-call | tf_op jit(solution)/shard_map/mix/pallas_call | solution.py:160
  (3 shorter events, 0.0 us)
Async XLA Ops:
  0.0 68.9 %copy-start = (f32[1280]{0:T(1024)S(1)}, f32[1280]{0:T(1024)}, u32[]{:S(2)}) copy-start(f32[1280]{0:T(1024)} %param.9) | copy-start | bytes 15364
  28.4 29.9 %all-to-all-start.1 = ((bf16[8,64,640]{2,1,0:T(8,128)(2,1)}), bf16[8,64,640]{2,1,0:T(8,128)(2,1)S(1)}, u32[]{:S(2)}, u32[]{:S(2)}) async-start(bf16[8,64,640]{2,1,0:T(8,128)(2,1)} %broadcast_in_dim.15), calls=%async_computation.1 | async-start | bytes 1310720 | tf_op jit(solution)/shard_map/all_to_all | solution.py:133
  58.3 4.0 %collective-permute-start = (bf16[8,64,640]{2,1,0:T(8,128)(2,1)S(1)}, bf16[8,64,640]{2,1,0:T(8,128)(2,1)S(1)}, u32[]{:S(2)}, u32[]{:S(2)}) collective-permute-start(bf16[8,64,640]{2,1,0:T(8,128)(2,1)S(1)} %all-to-all-done.1.own_ref), channel_id=1, source_target_pairs={{0,4},{4,0},{1,5},{5,1},{2,6},{6,2},{3,7},{7,3},{8,12},{12,8},{9,1... | collective-permute-start | bytes 1966088 | tf_op jit(solution)/shard_map/ppermute | solution.py:141
  64.8 17.8 %all-to-all-start.2 = ((bf16[12,32,768]{2,1,0:T(8,128)(2,1)}), bf16[12,32,768]{2,1,0:T(8,128)(2,1)S(1)}, u32[]{:S(2)}, u32[]{:S(2)}) async-start(bf16[12,32,768]{2,1,0:T(8,128)(2,1)} %attend.1), calls=%async_computation.2 | async-start | bytes 1179648 | tf_op jit(solution)/shard_map/all_to_all | solution.py:150

commit v4 on v3

--- a/solution.py
+++ b/solution.py
@@ -8,12 +8,12 @@
 HEAD_DIM = 128
 LOG2E = 1.4426950408889634
 SCALE = HEAD_DIM ** -0.5
-QUERY_AXES = ("x", "zl")
+QUERY_AXES = ("zl", "x")
 KEY_AXES = ("y",)
 SUM_LANE = 8
 PIECE_LANES = 16
 PART_PIECES = 2
-MIX_VMEM = 59 * 1024 * 1024
+MIX_VMEM = 50 * 1024 * 1024
 KERNEL_VMEM = 16 * 1024 * 1024
 
 
@@ -71,7 +71,7 @@
     out_ref[:, :, pl.ds(width, HEAD_DIM)] = split_pieces(stats).reshape(groups, tokens, HEAD_DIM)
 
 
-def combine_kernel(part_ref, out_ref):
+def combine_kernel(part_ref, own_ref, out_ref):
     groups, tokens, width = part_ref.shape
     width = width - HEAD_DIM
     heads = width // HEAD_DIM
@@ -91,27 +91,55 @@
         columns = pl.ds(head * HEAD_DIM, HEAD_DIM)
         part = part_ref[:, :, columns].astype(jnp.float32)
         summed = jnp.sum(part * weight[:, :, head : head + 1], axis=0)
-        out_ref[:, columns] = (summed / total[:, head : head + 1]).astype(jnp.bfloat16)
-
-
-def mix_kernel(attended_ref, gate_ref, weight_ref, out_ref, held_ref, semaphores):
-    parts, rows, width = attended_ref.shape
+        attended = (summed / total[:, head : head + 1]).astype(jnp.bfloat16)
+        own_ref[0, :, columns] = attended
+        for copy in range(out_ref.shape[0]):
+            out_ref[copy, :, columns] = attended
+
+
+def start_load(weight_ref, held_ref, semaphores, part, slot):
+    width = held_ref.shape[1]
     depth = width // PART_PIECES
     copies = []
-    for piece in range(parts * PART_PIECES):
-        span = pl.ds(piece * depth, depth)
-        copy = pltpu.make_async_copy(weight_ref.at[span], held_ref.at[span], semaphores.at[piece])
+    for piece in range(PART_PIECES):
+        copy = pltpu.make_async_copy(
+            weight_ref.at[pl.ds(part * width + piece * depth, depth)],
+            held_ref.at[slot, pl.ds(piece * depth, depth)],
+            semaphores.at[slot, piece],
+        )
         copy.start()
         copies.append(copy)
-    product = jnp.zeros(out_ref.shape, jnp.float32)
+    return copies
+
+
+def mix_part(attended_ref, held_ref, copies, part, slot):
+    depth = held_ref.shape[1] // PART_PIECES
+    product = jnp.zeros((attended_ref.shape[1], held_ref.shape[2]), jnp.float32)
     for piece, copy in enumerate(copies):
-        part, start = piece // PART_PIECES, piece % PART_PIECES * depth
         copy.wait()
+        span = pl.ds(piece * depth, depth)
         product += jnp.dot(
-            attended_ref[part, :, pl.ds(start, depth)],
-            held_ref[pl.ds(piece * depth, depth)],
+            attended_ref[part, :, span],
+            held_ref[slot, span],
             preferred_element_type=jnp.float32,
         )
+    return product
+
+
+def mix_own_kernel(attended_ref, weight_ref, out_ref, held_ref, semaphores):
+    copies = start_load(weight_ref, held_ref, semaphores, lax.axis_index("tp"), 0)
+    out_ref[...] = mix_part(attended_ref, held_ref, copies, 0, 0)
+
+
+def mix_rest_kernel(attended_ref, own_ref, gate_ref, weight_ref, out_ref, held_ref, semaphores):
+    parts = attended_ref.shape[0]
+    others = [lax.rem(lax.axis_index("tp") + step, parts) for step in range(1, parts)]
+    loads = [
+        start_load(weight_ref, held_ref, semaphores, part, slot) for slot, part in enumerate(others)
+    ]
+    product = own_ref[...]
+    for slot, part in enumerate(others):
+        product += mix_part(attended_ref, held_ref, loads[slot], part, slot)
     out_ref[...] = (product * gate_ref[...]).astype(jnp.bfloat16)
 
 
@@ -148,31 +176,57 @@
         name="attend",
     )(group, key_value, other)
     partial = lax.all_to_all(partial, QUERY_AXES, split_axis=0, concat_axis=0, tiled=True)
-    attended = pl.pallas_call(
+    own, attended = pl.pallas_call(
         combine_kernel,
-        out_shape=jax.ShapeDtypeStruct((tokens, head_width), jnp.bfloat16),
+        out_shape=[
+            jax.ShapeDtypeStruct((1, tokens, head_width), jnp.bfloat16),
+            jax.ShapeDtypeStruct((parts, tokens, head_width), jnp.bfloat16),
+        ],
         in_specs=[pl.BlockSpec(memory_space=pltpu.VMEM)],
-        out_specs=pl.BlockSpec(memory_space=pltpu.VMEM),
+        out_specs=[pl.BlockSpec(memory_space=pltpu.VMEM)] * 2,
         compiler_params=pltpu.CompilerParams(vmem_limit_bytes=KERNEL_VMEM),
         name="combine",
     )(partial)
-    parts_attended = lax.all_gather(attended, "tp", axis=0, tiled=False)
-    return pl.pallas_call(
-        mix_kernel,
-        out_shape=jax.ShapeDtypeStruct((tokens, out_weight.shape[1]), jnp.bfloat16),
+    channels = out_weight.shape[1]
+    product = pl.pallas_call(
+        mix_own_kernel,
+        out_shape=jax.ShapeDtypeStruct((tokens, channels), jnp.float32),
         in_specs=[
-            pl.BlockSpec(memory_space=pltpu.VMEM),
             pl.BlockSpec(memory_space=pltpu.VMEM),
             pl.BlockSpec(memory_space=pltpu.HBM),
         ],
         out_specs=pl.BlockSpec(memory_space=pltpu.VMEM),
         scratch_shapes=[
-            pltpu.VMEM(out_weight.shape, out_weight.dtype),
-            pltpu.SemaphoreType.DMA((parts * PART_PIECES,)),
+            pltpu.VMEM((1, head_width, channels), out_weight.dtype),
+            pltpu.SemaphoreType.DMA((1, PART_PIECES)),
         ],
         compiler_params=pltpu.CompilerParams(vmem_limit_bytes=MIX_VMEM),
-        name="mix",
-    )(parts_attended, gate[None, :], out_weight)
+        cost_estimate=pl.CostEstimate(
+            flops=2 * tokens * head_width * channels,
+            bytes_accessed=head_width * channels * 2,
+            transcendentals=0,
+        ),
+        name="mix_own",
+    )(own, out_weight)
+    attended = lax.all_to_all(attended, "tp", split_axis=0, concat_axis=0, tiled=True)
+    attended, product = lax.optimization_barrier((attended, product))
+    return pl.pallas_call(
+        mix_rest_kernel,
+        out_shape=jax.ShapeDtypeStruct((tokens, channels), jnp.bfloat16),
+        in_specs=[
+            pl.BlockSpec(memory_space=pltpu.VMEM),
+            pl.BlockSpec(memory_space=pltpu.VMEM),
+            pl.BlockSpec(memory_space=pltpu.VMEM),
+            pl.BlockSpec(memory_space=pltpu.HBM),
+        ],
+        out_specs=pl.BlockSpec(memory_space=pltpu.VMEM),
+        scratch_shapes=[
+            pltpu.VMEM((parts - 1, head_width, channels), out_weight.dtype),
+            pltpu.SemaphoreType.DMA((parts - 1, PART_PIECES)),
+        ],
+        compiler_params=pltpu.CompilerParams(vmem_limit_bytes=MIX_VMEM),
+        name="mix_rest",
+    )(attended, product, gate[None, :], out_weight)
 
 
 def solution(mesh):

time: 106 us -> 106 us (level)
  the two profiles are of different devices: /device:TPU:8 before, /device:TPU:40 now
where the time goes in v4:
time: 106 us; the launch traced here: 105 us
  blocking collectives  67.4 us (64%)
  starting transfers between devices  15.6 us (15%)
  waiting for transfers between devices  12.2 us (12%)
  Pallas kernels  8.31 us (8%)
    all_to_all x1, blocking collectives, on_device(): lax.all_to_all(stacked, 'tp', split_axis=0, concat_axis=0, tiled=True)  26.6 us
    all_gather x2, blocking collectives, on_device(): group = lax.all_gather(group, axis, axis=0, tiled=True)  22.8 us
    all_to_all x1, blocking collectives, on_device(): lax.all_to_all(partial, QUERY_AXES, split_axis=0, concat_axis=0, tiled=True)  18 us
    all_to_all x1, waiting for transfers between devices, on_device(): lax.all_to_all(attended, 'tp', split_axis=0, concat_axis=0, tiled=True)  10.1 us
    all_to_all x1, starting transfers between devices, on_device(): lax.all_to_all(spread_to(local[tokens:], lax.axis_size(KEY_AXES)), KEY_AX...  7.09 us
    all_to_all x1, starting transfers between devices, on_device(): lax.all_to_all(attended, 'tp', split_axis=0, concat_axis=0, tiled=True)  6.58 us
    pallas_call x1, Pallas kernels, on_device(): pl.pallas_call(mix_rest_kernel, out_shape=jax.ShapeDtypeStruct((tokens, c...  3.54 us
  transfers between devices with their start and end apart: 3, of which 2 were waited for; matrix products, arithmetic and copies ran while one was open for 0% of the time, Pallas kernels for 2%

profile of v4, /device:TPU:40, one launch (start us, length us, event | category | flops | bytes accessed | tf_op | source)
XLA Modules:
  0.0 105.3 jit_solution(18007130657089203438)
XLA Ops:
  0.0 0.0 copy-start
  0.0 0.9 maximum_bitcast_fusion
  0.9 26.6 %all_to_all.20 = bf16[4,24,640]{2,1,0:T(8,128)(2,1)S(1)} all-to-all(bf16[4,24,640]{2,1,0:T(8,128)(2,1)S(1)} %maximum_bitcast_fusion), channel_id=1, replica_groups=mesh['zl'=3,'y'=8,'x'=4,'c'=2,'tp'=4] {'tp'}, dimensions={0} | all-to-all | bytes 245760 | tf_op jit(solution)/shard_map/all_to_all | solution.py:157
  27.5 0.9 broadcast_in_dim.15
  28.4 7.1 %all-to-all-start.1 = ((bf16[8,64,640]{2,1,0:T(8,128)(2,1)}), bf16[8,64,640]{2,1,0:T(8,128)(2,1)S(1)}, u32[]{:S(2)}, u32[]{:S(2)}) async-start(bf16[8,64,640]{2,1,0:T(8,128)(2,1)} %broadcast_in_dim.15), calls=%async_computation.1 | async-start | bytes 1310720 | tf_op jit(solution)/shard_map/all_to_all | solution.py:161
  35.5 12.5 %all_gather.6 = bf16[4,32,640]{2,1,0:T(8,128)(2,1)S(1)} all-gather(bf16[1,32,640]{2,1,0:T(8,128)(2,1)S(1)} %slice_bitcast_fusion), channel_id=1, replica_groups=mesh['zl'=3,'y'=8,'x'=4,'c'=2,'tp'=4] {'x'}, dimensions={0}, use_global_device_ids=true | all-gather | bytes 204800 | tf_op jit(solution)/shard_map/all_gather | solution.py:167
  48.0 10.3 %all_gather.7.q_ref = bf16[12,32,640]{2,1,0:T(8,128)(2,1)S(1)} all-gather(bf16[4,32,640]{2,1,0:T(8,128)(2,1)S(1)} %all_gather.6), channel_id=1, replica_groups=mesh['zl'=3,'y'=8,'x'=4,'c'=2,'tp'=4] {'zl'}, dimensions={0}, use_global_device_ids=true | all-gather | bytes 655360 | tf_op jit(solution)/shard_map/all_gather | solution.py:167
  58.3 0.0 all-to-all-done.1.own_ref
  58.3 1.9 %collective-permute-start = (bf16[8,64,640]{2,1,0:T(8,128)(2,1)S(1)}, bf16[8,64,640]{2,1,0:T(8,128)(2,1)S(1)}, u32[]{:S(2)}, u32[]{:S(2)}) collective-permute-start(bf16[8,64,640]{2,1,0:T(8,128)(2,1)S(1)} %all-to-all-done.1.own_ref), channel_id=1, source_target_pairs={{0,4},{4,0},{1,5},{5,1},{2,6},{6,2},{3,7},{7,3},{8,12},{12,8},{9,1... | collective-permute-start | bytes 1966088 | tf_op jit(solution)/shard_map/ppermute | solution.py:169
  60.2 2.1 %collective-permute-done.other_ref = bf16[8,64,640]{2,1,0:T(8,128)(2,1)S(1)} collective-permute-done((bf16[8,64,640]{2,1,0:T(8,128)(2,1)S(1)}, bf16[8,64,640]{2,1,0:T(8,128)(2,1)S(1)}, u32[]{:S(2)}, u32[]{:S(2)}) %collective-permute-start) | collective-permute-done | bytes 655392 | tf_op jit(solution)/shard_map/ppermute | solution.py:169
  62.2 1.7 %attend.1 = bf16[12,32,768]{2,1,0:T(8,128)(2,1)S(1)} custom-call(bf16[12,32,640]{2,1,0:T(8,128)(2,1)S(1)} %all_gather.7.q_ref, bf16[8,64,640]{2,1,0:T(8,128)(2,1)S(1)} %all-to-all-done.1.own_ref, bf16[8,64,640]{2,1,0:T(8,128)(2,1)S(1)} %collective-permute-done.other_ref), custom_call_target="tpu_custom_call" | custom-call | tf_op jit(solution)/shard_map/attend/pallas_call | solution.py:170
  64.0 18.0 %all_to_all.21.part_ref = bf16[12,32,768]{2,1,0:T(8,128)(2,1)S(1)} all-to-all(bf16[12,32,768]{2,1,0:T(8,128)(2,1)S(1)} %attend.1), channel_id=1, replica_groups=mesh['zl'=3,'y'=8,'x'=4,'c'=2,'tp'=4] {'zl','x'}, dimensions={0} | all-to-all | bytes 1179648 | tf_op jit(solution)/shard_map/all_to_all | solution.py:178
  82.0 1.2 %combine.1 = (bf16[1,32,640]{2,1,0:T(8,128)(2,1)S(1)}, bf16[4,32,640]{2,1,0:T(8,128)(2,1)}) custom-call(bf16[12,32,768]{2,1,0:T(8,128)(2,1)S(1)} %all_to_all.21.part_ref), custom_call_target="tpu_custom_call" | custom-call | tf_op jit(solution)/shard_map/combine/pallas_call | solution.py:179
  83.2 6.6 %all-to-all-start.3 = ((bf16[4,32,640]{2,1,0:T(8,128)(2,1)}), bf16[4,32,640]{2,1,0:T(8,128)(2,1)S(1)}, u32[]{:S(2)}, u32[]{:S(2)}) async-start(bf16[4,32,640]{2,1,0:T(8,128)(2,1)} %get-tuple-element.13), calls=%async_computation.3 | async-start | bytes 327680 | tf_op jit(solution)/shard_map/all_to_all | solution.py:211
  89.8 0.0 copy-done
  89.8 1.8 %mix_own.1.own_ref = f32[32,1280]{1,0:T(8,128)S(1)} custom-call(bf16[1,32,640]{2,1,0:T(8,128)(2,1)S(1)} %get-tuple-element.14.attended_ref, bf16[2560,1280]{1,0:T(8,128)(2,1)} %weight_ref.3), custom_call_target="tpu_custom_call" | custom-call | flops 52428800 | bytes 1638400 | tf_op jit(solution)/shard_map/mix_own/pallas_call | solution.py:191
  91.6 10.1 %all-to-all-done.3.attended_ref = bf16[4,32,640]{2,1,0:T(8,128)(2,1)S(1)} async-done(((bf16[4,32,640]{2,1,0:T(8,128)(2,1)}), bf16[4,32,640]{2,1,0:T(8,128)(2,1)S(1)}, u32[]{:S(2)}, u32[]{:S(2)}) %all-to-all-start.3) | async-done | bytes 163872 | tf_op jit(solution)/shard_map/all_to_all | solution.py:211
  101.7 3.5 %mix_rest.1 = bf16[32,1280]{1,0:T(8,128)(2,1)} custom-call(bf16[4,32,640]{2,1,0:T(8,128)(2,1)S(1)} %all-to-all-done.3.attended_ref, f32[32,1280]{1,0:T(8,128)S(1)} %mix_own.1.own_ref, f32[1,1280]{1,0:T(1,128)S(1)} %broadcast_in_dim.17.gate_ref, bf16[2560,1280]{1,0:T(8,128)(2,1)} %weight_ref.3), custom_call_target="tpu_custom_call" | custom-call | tf_op jit(solution)/shard_map/mix_rest/pallas_call | solution.py:213
  (4 shorter events, 0.0 us)
Async XLA Ops:
  0.0 89.8 %copy-start = (f32[1280]{0:T(1024)S(1)}, f32[1280]{0:T(1024)}, u32[]{:S(2)}) copy-start(f32[1280]{0:T(1024)} %param.9) | copy-start | bytes 15364
  28.4 29.9 %all-to-all-start.1 = ((bf16[8,64,640]{2,1,0:T(8,128)(2,1)}), bf16[8,64,640]{2,1,0:T(8,128)(2,1)S(1)}, u32[]{:S(2)}, u32[]{:S(2)}) async-start(bf16[8,64,640]{2,1,0:T(8,128)(2,1)} %broadcast_in_dim.15), calls=%async_computation.1 | async-start | bytes 1310720 | tf_op jit(solution)/shard_map/all_to_all | solution.py:161
  58.3 4.0 %collective-permute-start = (bf16[8,64,640]{2,1,0:T(8,128)(2,1)S(1)}, bf16[8,64,640]{2,1,0:T(8,128)(2,1)S(1)}, u32[]{:S(2)}, u32[]{:S(2)}) collective-permute-start(bf16[8,64,640]{2,1,0:T(8,128)(2,1)S(1)} %all-to-all-done.1.own_ref), channel_id=1, source_target_pairs={{0,4},{4,0},{1,5},{5,1},{2,6},{6,2},{3,7},{7,3},{8,12},{12,8},{9,1... | collective-permute-start | bytes 1966088 | tf_op jit(solution)/shard_map/ppermute | solution.py:169
  83.2 18.5 %all-to-all-start.3 = ((bf16[4,32,640]{2,1,0:T(8,128)(2,1)}), bf16[4,32,640]{2,1,0:T(8,128)(2,1)S(1)}, u32[]{:S(2)}, u32[]{:S(2)}) async-start(bf16[4,32,640]{2,1,0:T(8,128)(2,1)} %get-tuple-element.13), calls=%async_computation.3 | async-start | bytes 327680 | tf_op jit(solution)/shard_map/all_to_all | solution.py:211

commit v5 on v2

--- a/solution.py
+++ b/solution.py
@@ -1,3 +1,5 @@
+import functools
+
 import jax
 import jax.numpy as jnp
 from jax import lax
@@ -8,10 +10,12 @@
 HEAD_DIM = 128
 LOG2E = 1.4426950408889634
 SCALE = HEAD_DIM ** -0.5
-QUERY_AXES = ("y",)
-KEY_AXES = ("zl", "x")
+QUERY_AXES = ("zl", "x")
+KEY_AXES = ("y",)
 SUM_LANE = 8
 PIECE_LANES = 16
+PART_PIECES = 2
+MIX_VMEM = 50 * 1024 * 1024
 KERNEL_VMEM = 16 * 1024 * 1024
 
 
@@ -89,7 +93,80 @@
         columns = pl.ds(head * HEAD_DIM, HEAD_DIM)
         part = part_ref[:, :, columns].astype(jnp.float32)
         summed = jnp.sum(part * weight[:, :, head : head + 1], axis=0)
-        out_ref[:, columns] = (summed / total[:, head : head + 1]).astype(jnp.bfloat16)
+        attended = (summed / total[:, head : head + 1]).astype(jnp.bfloat16)
+        out_ref[:, columns] = attended
+
+
+def start_load(weight_ref, held_ref, semaphores, part, slot):
+    width = held_ref.shape[1]
+    depth = width // PART_PIECES
+    copies = []
+    for piece in range(PART_PIECES):
+        copy = pltpu.make_async_copy(
+            weight_ref.at[pl.ds(part * width + piece * depth, depth)],
+            held_ref.at[slot, pl.ds(piece * depth, depth)],
+            semaphores.at[slot, piece],
+        )
+        copy.start()
+        copies.append(copy)
+    return copies
+
+
+def mix_part(attended_ref, held_ref, copies, slot):
+    depth = held_ref.shape[1] // PART_PIECES
+    product = jnp.zeros((attended_ref.shape[0], held_ref.shape[2]), jnp.float32)
+    for piece, copy in enumerate(copies):
+        copy.wait()
+        span = pl.ds(piece * depth, depth)
+        product += jnp.dot(
+            attended_ref[:, span],
+            held_ref[slot, span],
+            preferred_element_type=jnp.float32,
+        )
+    return product
+
+
+def mix_kernel(steps, *refs):
+    count = len(steps)
+    attended_refs, (weight_ref, *more, out_ref, held_ref, semaphores) = refs[:count], refs[count:]
+    parts = weight_ref.shape[0] // held_ref.shape[1]
+    loads = [
+        start_load(
+            weight_ref, held_ref, semaphores, lax.rem(lax.axis_index("tp") + step, parts), slot
+        )
+        for slot, step in enumerate(steps)
+    ]
+    product = more[0][...] if more else jnp.zeros(out_ref.shape, jnp.float32)
+    for slot, attended_ref in enumerate(attended_refs):
+        product += mix_part(attended_ref, held_ref, loads[slot], slot)
+    if len(more) > 1:
+        product *= more[1][...]
+    out_ref[...] = product.astype(out_ref.dtype)
+
+
+def mix(steps, attended, weight, more, dtype):
+    tokens, width = attended[0].shape
+    channels = weight.shape[1]
+    in_vmem = pl.BlockSpec(memory_space=pltpu.VMEM)
+    return pl.pallas_call(
+        functools.partial(mix_kernel, steps),
+        out_shape=jax.ShapeDtypeStruct((tokens, channels), dtype),
+        in_specs=[in_vmem] * len(steps)
+        + [pl.BlockSpec(memory_space=pltpu.HBM)]
+        + [in_vmem] * len(more),
+        out_specs=in_vmem,
+        scratch_shapes=[
+            pltpu.VMEM((len(steps), width, channels), weight.dtype),
+            pltpu.SemaphoreType.DMA((len(steps), PART_PIECES)),
+        ],
+        compiler_params=pltpu.CompilerParams(vmem_limit_bytes=MIX_VMEM),
+        cost_estimate=pl.CostEstimate(
+            flops=2 * len(steps) * tokens * width * channels,
+            bytes_accessed=2 * len(steps) * width * channels,
+            transcendentals=0,
+        ),
+        name="mix",
+    )(*attended, weight, *more)
 
 
 def spread_to(block, count):
@@ -131,12 +208,15 @@
         compiler_params=pltpu.CompilerParams(vmem_limit_bytes=KERNEL_VMEM),
         name="combine",
     )(partial)
-    product = jnp.dot(
-        lax.all_gather(attended, "tp", axis=1, tiled=True),
-        out_weight,
-        preferred_element_type=jnp.float32,
-    )
-    return (product * gate[None, :]).astype(jnp.bfloat16)
+
+    def from_ahead(step):
+        pairs = [(place, (place - step) % parts) for place in range(parts)]
+        return lax.ppermute(attended, "tp", pairs)
+
+    arrived = {step: from_ahead(step) for step in (2, 1, 3)}
+    product = mix((0,), [attended], out_weight, [], jnp.float32)
+    product = mix((1, 3), [arrived[1], arrived[3]], out_weight, [product], jnp.float32)
+    return mix((2,), [arrived[2]], out_weight, [product, gate[None, :]], jnp.bfloat16)
 
 
 def solution(mesh):

time: 110 us -> 115 us (1.045)
  the two profiles are of different devices: /device:TPU:2 before, /device:TPU:8 now
where the time goes in v5:
time: 115 us
  blocking collectives  73.8 us (64%)
  starting transfers between devices  28 us (24%)
  Pallas kernels  8.97 us (8%)
  waiting for transfers between devices  2.07 us (2%)
    all_gather x1, blocking collectives, on_device(): group = lax.all_gather(local[:tokens], QUERY_AXES, axis=0, tiled=False)  30.7 us
    all_to_all x1, blocking collectives, on_device(): lax.all_to_all(stacked, 'tp', split_axis=0, concat_axis=0, tiled=True)  26.6 us
    ppermute x3, starting transfers between devices, from_ahead(): return lax.ppermute(attended, 'tp', pairs)  18.5 us
    all_to_all x1, blocking collectives, on_device(): lax.all_to_all(partial, QUERY_AXES, split_axis=0, concat_axis=0, tiled=True)  16.5 us
    all_to_all x1, starting transfers between devices, on_device(): lax.all_to_all(spread_to(local[tokens:], lax.axis_size(KEY_AXES)), KEY_AX...  7.55 us
    pallas_call x3, Pallas kernels, mix(): pl.pallas_call(functools.partial(mix_kernel, steps), out_shape=jax.ShapeD...  6.72 us
  transfers between devices with their start and end apart: 5, of which 1 were waited for; matrix products, arithmetic and copies ran while one was open for 0% of the time, Pallas kernels for 4%

profile of v5, /device:TPU:8, one launch (start us, length us, event | category | flops | bytes accessed | tf_op | source)
XLA Modules:
  0.0 114.8 jit_solution(14691133282979619405)
XLA Ops:
  0.0 0.0 copy-start
  0.0 0.9 maximum_bitcast_fusion
  0.9 26.6 %all_to_all.15 = bf16[4,24,640]{2,1,0:T(8,128)(2,1)S(1)} all-to-all(bf16[4,24,640]{2,1,0:T(8,128)(2,1)S(1)} %maximum_bitcast_fusion), channel_id=1, replica_groups=mesh['zl'=3,'y'=8,'x'=4,'c'=2,'tp'=4] {'tp'}, dimensions={0} | all-to-all | bytes 245760 | tf_op jit(solution)/shard_map/all_to_all | solution.py:183
  27.5 0.9 broadcast_in_dim.12
  28.4 7.5 %all-to-all-start.1 = ((bf16[8,64,640]{2,1,0:T(8,128)(2,1)}), bf16[8,64,640]{2,1,0:T(8,128)(2,1)S(1)}, u32[]{:S(2)}, u32[]{:S(2)}) async-start(bf16[8,64,640]{2,1,0:T(8,128)(2,1)} %broadcast_in_dim.12), calls=%async_computation.1 | async-start | bytes 1310720 | tf_op jit(solution)/shard_map/all_to_all | solution.py:187
  35.9 30.7 %all_gather.7.q_ref = bf16[12,32,640]{2,1,0:T(8,128)(2,1)S(1)} all-gather(bf16[1,32,640]{2,1,0:T(8,128)(2,1)S(1)} %slice_bitcast_fusion), channel_id=1, replica_groups=mesh['zl'=3,'y'=8,'x'=4,'c'=2,'tp'=4] {'zl','x'}, dimensions={0}, use_global_device_ids=true | all-gather | bytes 532480 | tf_op jit(solution)/shard_map/all_gather | solution.py:191
  66.6 0.0 all-to-all-done.1.own_ref
  66.6 1.9 %collective-permute-start = (bf16[8,64,640]{2,1,0:T(8,128)(2,1)S(1)}, bf16[8,64,640]{2,1,0:T(8,128)(2,1)S(1)}, u32[]{:S(2)}, u32[]{:S(2)}) collective-permute-start(bf16[8,64,640]{2,1,0:T(8,128)(2,1)S(1)} %all-to-all-done.1.own_ref), channel_id=1, source_target_pairs={{0,4},{4,0},{1,5},{5,1},{2,6},{6,2},{3,7},{7,3},{8,12},{12,8},{9,1... | collective-permute-start | bytes 1966088 | tf_op jit(solution)/shard_map/ppermute | solution.py:193
  68.6 2.1 %collective-permute-done.other_ref = bf16[8,64,640]{2,1,0:T(8,128)(2,1)S(1)} collective-permute-done((bf16[8,64,640]{2,1,0:T(8,128)(2,1)S(1)}, bf16[8,64,640]{2,1,0:T(8,128)(2,1)S(1)}, u32[]{:S(2)}, u32[]{:S(2)}) %collective-permute-start) | collective-permute-done | bytes 655392 | tf_op jit(solution)/shard_map/ppermute | solution.py:193
  70.6 1.7 %attend.1 = bf16[12,32,768]{2,1,0:T(8,128)(2,1)S(1)} custom-call(bf16[12,32,640]{2,1,0:T(8,128)(2,1)S(1)} %all_gather.7.q_ref, bf16[8,64,640]{2,1,0:T(8,128)(2,1)S(1)} %all-to-all-done.1.own_ref, bf16[8,64,640]{2,1,0:T(8,128)(2,1)S(1)} %collective-permute-done.other_ref), custom_call_target="tpu_custom_call" | custom-call | tf_op jit(solution)/shard_map/attend/pallas_call | solution.py:194
  72.4 16.5 %all_to_all.16.part_ref = bf16[12,32,768]{2,1,0:T(8,128)(2,1)S(1)} all-to-all(bf16[12,32,768]{2,1,0:T(8,128)(2,1)S(1)} %attend.1), channel_id=1, replica_groups=mesh['zl'=3,'y'=8,'x'=4,'c'=2,'tp'=4] {'zl','x'}, dimensions={0} | all-to-all | bytes 1179648 | tf_op jit(solution)/shard_map/all_to_all | solution.py:202
  88.9 0.5 combine.1.refs_0_
  89.4 2.8 %collective-permute-start.2 = (bf16[32,640]{1,0:T(8,128)(2,1)S(1)}, bf16[32,640]{1,0:T(8,128)(2,1)S(1)}, u32[]{:S(2)}, u32[]{:S(2)}) collective-permute-start(bf16[32,640]{1,0:T(8,128)(2,1)S(1)} %combine.1.refs_0_), channel_id=1, source_target_pairs={{0,3},{1,0},{2,1},{3,2},{4,7},{5,4},{6,5},{7,6},{8,11},{9,8},{10,9... | collective-permute-start | bytes 122888 | tf_op jit(solution)/shard_map/ppermute | solution.py:214
  92.2 7.2 %collective-permute-start.3 = (bf16[32,640]{1,0:T(8,128)(2,1)S(1)}, bf16[32,640]{1,0:T(8,128)(2,1)S(1)}, u32[]{:S(2)}, u32[]{:S(2)}) collective-permute-start(bf16[32,640]{1,0:T(8,128)(2,1)S(1)} %combine.1.refs_0_), channel_id=1, source_target_pairs={{0,1},{1,2},{2,3},{3,0},{4,5},{5,6},{6,7},{7,4},{8,9},{9,10},{10,1... | collective-permute-start | bytes 122888 | tf_op jit(solution)/shard_map/ppermute | solution.py:214
  99.4 8.6 %collective-permute-start.1 = (bf16[32,640]{1,0:T(8,128)(2,1)S(1)}, bf16[32,640]{1,0:T(8,128)(2,1)S(1)}, u32[]{:S(2)}, u32[]{:S(2)}) collective-permute-start(bf16[32,640]{1,0:T(8,128)(2,1)S(1)} %combine.1.refs_0_), channel_id=1, source_target_pairs={{0,2},{1,3},{2,0},{3,1},{4,6},{5,7},{6,4},{7,5},{8,10},{9,11},{10,... | collective-permute-start | bytes 122888 | tf_op jit(solution)/shard_map/ppermute | solution.py:214
  108.0 0.0 copy-done
  108.0 1.8 %mix.3.refs_3_ = f32[32,1280]{1,0:T(8,128)S(1)} custom-call(bf16[32,640]{1,0:T(8,128)(2,1)S(1)} %combine.1.refs_0_, bf16[2560,1280]{1,0:T(8,128)(2,1)} %refs_1_.3), custom_call_target="tpu_custom_call" | custom-call | flops 52428800 | bytes 1638400 | tf_op jit(solution)/shard_map/mix/pallas_call | solution.py:151
  109.8 0.0 collective-permute-done.2.refs_0_
  109.8 0.0 collective-permute-done.3.refs_1_
  109.9 2.4 %mix.4.refs_2_ = f32[32,1280]{1,0:T(8,128)S(1)} custom-call(bf16[32,640]{1,0:T(8,128)(2,1)S(1)} %collective-permute-done.2.refs_0_, bf16[32,640]{1,0:T(8,128)(2,1)S(1)} %collective-permute-done.3.refs_1_, bf16[2560,1280]{1,0:T(8,128)(2,1)} %refs_1_.3, f32[32,1280]{1,0:T(8,128)S(1)} %mix.3.refs_3_), custom_call_target="tpu_custom_call" | custom-call | flops 104857600 | bytes 3276800 | tf_op jit(solution)/shard_map/mix/pallas_call | solution.py:151
  112.3 0.0 collective-permute-done.1.refs_0_
  112.3 2.5 %mix.5 = bf16[32,1280]{1,0:T(8,128)(2,1)} custom-call(bf16[32,640]{1,0:T(8,128)(2,1)S(1)} %collective-permute-done.1.refs_0_, bf16[2560,1280]{1,0:T(8,128)(2,1)} %refs_1_.3, f32[32,1280]{1,0:T(8,128)S(1)} %mix.4.refs_2_, f32[1,1280]{1,0:T(1,128)S(1)} %broadcast_in_dim.13.refs_3_), custom_call_target="tpu_custom_call" | custom-call | flops 52428800 | bytes 1638400 | tf_op jit(solution)/shard_map/mix/pallas_call | solution.py:151
  (4 shorter events, 0.0 us)
Async XLA Ops:
  0.0 108.0 %copy-start = (f32[1280]{0:T(1024)S(1)}, f32[1280]{0:T(1024)}, u32[]{:S(2)}) copy-start(f32[1280]{0:T(1024)} %param.9) | copy-start | bytes 15364
  28.4 38.3 %all-to-all-start.1 = ((bf16[8,64,640]{2,1,0:T(8,128)(2,1)}), bf16[8,64,640]{2,1,0:T(8,128)(2,1)S(1)}, u32[]{:S(2)}, u32[]{:S(2)}) async-start(bf16[8,64,640]{2,1,0:T(8,128)(2,1)} %broadcast_in_dim.12), calls=%async_computation.1 | async-start | bytes 1310720 | tf_op jit(solution)/shard_map/all_to_all | solution.py:187
  66.6 4.0 %collective-permute-start = (bf16[8,64,640]{2,1,0:T(8,128)(2,1)S(1)}, bf16[8,64,640]{2,1,0:T(8,128)(2,1)S(1)}, u32[]{:S(2)}, u32[]{:S(2)}) collective-permute-start(bf16[8,64,640]{2,1,0:T(8,128)(2,1)S(1)} %all-to-all-done.1.own_ref), channel_id=1, source_target_pairs={{0,4},{4,0},{1,5},{5,1},{2,6},{6,2},{3,7},{7,3},{8,12},{12,8},{9,1... | collective-permute-start | bytes 1966088 | tf_op jit(solution)/shard_map/ppermute | solution.py:193
  89.4 20.4 %collective-permute-start.2 = (bf16[32,640]{1,0:T(8,128)(2,1)S(1)}, bf16[32,640]{1,0:T(8,128)(2,1)S(1)}, u32[]{:S(2)}, u32[]{:S(2)}) collective-permute-start(bf16[32,640]{1,0:T(8,128)(2,1)S(1)} %combine.1.refs_0_), channel_id=1, source_target_pairs={{0,3},{1,0},{2,1},{3,2},{4,7},{5,4},{6,5},{7,6},{8,11},{9,8},{10,9... | collective-permute-start | bytes 122888 | tf_op jit(solution)/shard_map/ppermute | solution.py:214
  92.2 17.7 %collective-permute-start.3 = (bf16[32,640]{1,0:T(8,128)(2,1)S(1)}, bf16[32,640]{1,0:T(8,128)(2,1)S(1)}, u32[]{:S(2)}, u32[]{:S(2)}) collective-permute-start(bf16[32,640]{1,0:T(8,128)(2,1)S(1)} %combine.1.refs_0_), channel_id=1, source_target_pairs={{0,1},{1,2},{2,3},{3,0},{4,5},{5,6},{6,7},{7,4},{8,9},{9,10},{10,1... | collective-permute-start | bytes 122888 | tf_op jit(solution)/shard_map/ppermute | solution.py:214
  99.4 12.9 %collective-permute-start.1 = (bf16[32,640]{1,0:T(8,128)(2,1)S(1)}, bf16[32,640]{1,0:T(8,128)(2,1)S(1)}, u32[]{:S(2)}, u32[]{:S(2)}) collective-permute-start(bf16[32,640]{1,0:T(8,128)(2,1)S(1)} %combine.1.refs_0_), channel_id=1, source_target_pairs={{0,2},{1,3},{2,0},{3,1},{4,6},{5,7},{6,4},{7,5},{8,10},{9,11},{10,... | collective-permute-start | bytes 122888 | tf_op jit(solution)/shard_map/ppermute | solution.py:214

commit v6 on v3

v6 whole, which is shorter than its diff:
```python
import jax
import jax.numpy as jnp
from jax import lax
from jax.experimental import pallas as pl
from jax.experimental.pallas import tpu as pltpu
from jax.sharding import Mesh, PartitionSpec as P

HEAD_DIM = 128
LOG2E = 1.4426950408889634
SCALE = HEAD_DIM ** -0.5
HEAD_AXES = ("zl", "c", "tp")
QUERY_AXES = ("x",)
KEY_AXES = ("y",)
PIECE_LANES = 8
KERNEL_VMEM = 16 * 1024 * 1024
MIX_VMEM = 50 * 1024 * 1024
IN_VMEM = pl.BlockSpec(memory_space=pltpu.VMEM)


def split_pieces(stats):
    high = stats.astype(jnp.bfloat16).astype(jnp.float32)
    rest = stats - high
    middle = rest.astype(jnp.bfloat16).astype(jnp.float32)
    low = rest - middle
    lane = lax.broadcasted_iota(jnp.int32, stats.shape, 1)
    spread = jnp.where(
        lane < PIECE_LANES,
        high,
        jnp.where(
            lane < 2 * PIECE_LANES,
            pltpu.roll(middle, PIECE_LANES, 1),
            pltpu.roll(low, 2 * PIECE_LANES, 1),
        ),
    )
    return spread.astype(jnp.bfloat16)


def attend_kernel(q_ref, key_value_ref, out_ref):
    groups, tokens, width = q_ref.shape
    count = key_value_ref.shape[0] * tokens
    key = key_value_ref[:, 0].reshape(count, width)
    value = key_value_ref[:, 1].reshape(count, width)
    lane = lax.broadcasted_iota(jnp.int32, (tokens, HEAD_DIM), 1)
    for group in range(groups):
        score = lax.dot_general(
            q_ref[group], key, (((1,), (1,)), ((), ())), preferred_element_type=jnp.float32
        )
        highest = jnp.max(score, axis=1, keepdims=True)
        expd = jnp.exp2((score - highest) * (SCALE * LOG2E))
        total = jnp.sum(expd, axis=1, keepdims=True)
        summed = jnp.dot(expd.astype(jnp.bfloat16), value, preferred_element_type=jnp.float32)
        out_ref[group, :, pl.ds(0, width)] = summed.astype(jnp.bfloat16)
        stats = jnp.where(lane == 0, highest, jnp.where(lane == 1, total, 0.0))
        out_ref[group, :, pl.ds(width, HEAD_DIM)] = split_pieces(stats)


def combine_kernel(part_ref, out_ref):
    groups, tokens, _ = part_ref.shape
    copies, rows, width = out_ref.shape
    pieces = part_ref[:, :, pl.ds(width, HEAD_DIM)].astype(jnp.float32)
    pieces = pieces.reshape(groups * tokens, HEAD_DIM)
    stats = (
        pieces
        + pltpu.roll(pieces, HEAD_DIM - PIECE_LANES, 1)
        + pltpu.roll(pieces, HEAD_DIM - 2 * PIECE_LANES, 1)
    ).reshape(groups, tokens, HEAD_DIM)
    maxima, sums = stats[:, :, 0:1], stats[:, :, 1:2]
    weight = jnp.exp2((maxima - jnp.max(maxima, axis=0, keepdims=True)) * (SCALE * LOG2E))
    total = jnp.sum(weight * sums, axis=0)
    summed = jnp.sum(part_ref[:, :, pl.ds(0, width)].astype(jnp.float32) * weight, axis=0)
    attended = (summed / total).astype(jnp.bfloat16)
    repeats = copies * rows // tokens
    for block in range(tokens // rows):
        for repeat in range(repeats):
            out_ref[block * repeats + repeat] = attended[block * rows : (block + 1) * rows]


def mix_kernel(attended_ref, gate_ref, weight_ref, out_ref, held_ref, semaphores):
    heads = weight_ref.shape[0] // HEAD_DIM
    pieces = semaphores.shape[0]
    span = heads // pieces
    copies = []
    for piece in range(pieces):
        rows = pl.ds(piece * span * HEAD_DIM, span * HEAD_DIM)
        copy = pltpu.make_async_copy(weight_ref.at[rows], held_ref.at[rows], semaphores.at[piece])
        copy.start()
        copies.append(copy)
    product = jnp.zeros(out_ref.shape, jnp.float32)
    for piece, copy in enumerate(copies):
        first = piece * span
        block = jnp.concatenate(
            [attended_ref[head] for head in range(first, first + span)], axis=1
        )
        copy.wait()
        product += jnp.dot(
            block,
            held_ref[pl.ds(first * HEAD_DIM, span * HEAD_DIM)],
            preferred_element_type=jnp.float32,
        )
    out_ref[...] = (product * gate_ref[...]).astype(jnp.bfloat16)


def exchange(blocks, axes):
    return lax.all_to_all(blocks, axes, split_axis=0, concat_axis=0, tiled=True)


def spread_to(block, count):
    return jnp.broadcast_to(block[None], (count, *block.shape))


def on_device(queries, keys, vals, out_weight, gate):
    slots = lax.axis_size(HEAD_AXES)
    rows, width = queries.shape
    heads = width // HEAD_DIM
    tokens = slots * rows
    own_tokens = lax.axis_size("tp") * rows
    stacked = jnp.stack([queries, keys, vals], axis=0).reshape(3, rows, heads, HEAD_DIM)
    stacked = stacked.transpose(2, 0, 1, 3).reshape(heads, 3 * rows, HEAD_DIM)
    stacked = jnp.pad(stacked, ((0, slots - heads), (0, 0), (0, 0)))
    local = exchange(stacked, HEAD_AXES)
    local = local.reshape(slots, 3, rows, HEAD_DIM).transpose(1, 0, 2, 3)
    local = local.reshape(3, tokens, HEAD_DIM)
    key_value = exchange(spread_to(local[1:], lax.axis_size(KEY_AXES)), KEY_AXES)
    group = lax.all_gather(local[0], QUERY_AXES, axis=0, tiled=False)
    key_value, group = lax.optimization_barrier((key_value, group))
    partial = pl.pallas_call(
        attend_kernel,
        out_shape=jax.ShapeDtypeStruct((*group.shape[:2], 2 * HEAD_DIM), jnp.bfloat16),
        in_specs=[IN_VMEM] * 2,
        out_specs=IN_VMEM,
        compiler_params=pltpu.CompilerParams(vmem_limit_bytes=KERNEL_VMEM),
        name="attend",
    )(group, key_value)
    partial = exchange(partial, QUERY_AXES)
    attended = pl.pallas_call(
        combine_kernel,
        out_shape=jax.ShapeDtypeStruct((slots, own_tokens, HEAD_DIM), jnp.bfloat16),
        in_specs=[IN_VMEM],
        out_specs=IN_VMEM,
        compiler_params=pltpu.CompilerParams(vmem_limit_bytes=KERNEL_VMEM),
        name="combine",
    )(partial)
    attended = exchange(attended, HEAD_AXES)
    return pl.pallas_call(
        mix_kernel,
        out_shape=jax.ShapeDtypeStruct((own_tokens, out_weight.shape[1]), jnp.bfloat16),
        in_specs=[IN_VMEM, IN_VMEM, pl.BlockSpec(memory_space=pltpu.HBM)],
        out_specs=IN_VMEM,
        scratch_shapes=[
            pltpu.VMEM(out_weight.shape, out_weight.dtype),
            pltpu.SemaphoreType.DMA((heads // 2,)),
        ],
        compiler_params=pltpu.CompilerParams(vmem_limit_bytes=MIX_VMEM),
        name="mix",
    )(attended, gate[None, :], out_weight)


def solution(mesh):
    ctx = ("zl", "y", "x", "c")
    fine = Mesh(mesh.devices.reshape(3, 8, 4, 2, 4), (*ctx, "tp"))
    return jax.shard_map(
        on_device,
        mesh=fine,
        in_specs=(
            P((*ctx, "tp"), None),
            P((*ctx, "tp"), None),
            P((*ctx, "tp"), None),
            P(None, "tp"),
            P("tp"),
        ),
        out_specs=P(ctx, "tp"),
        check_vma=False,
    )
```

time: 106 us -> 99.1 us (0.935)
  the two profiles are of different devices: /device:TPU:8 before, /device:TPU:1 now
where the time goes in v6:
time: 99.1 us; the launch traced here: 98.8 us
  blocking collectives  48.7 us (49%)
  waiting for transfers between devices  26.4 us (27%)
  starting transfers between devices  14.4 us (15%)
  Pallas kernels  7.3 us (7%)
  local copies, waits for them, and re-layouts  1.08 us (1%)
    all_to_all x2, blocking collectives, exchange(): return lax.all_to_all(blocks, axes, split_axis=0, concat_axis=0, tiled=True)  38.8 us
    all_to_all x2, waiting for transfers between devices, exchange(): return lax.all_to_all(blocks, axes, split_axis=0, concat_axis=0, tiled=True)  26.4 us
    all_to_all x2, starting transfers between devices, exchange(): return lax.all_to_all(blocks, axes, split_axis=0, concat_axis=0, tiled=True)  14.4 us
    all_gather x1, blocking collectives, on_device(): group = lax.all_gather(local[0], QUERY_AXES, axis=0, tiled=False)  9.88 us
    pallas_call x1, Pallas kernels, on_device(): pl.pallas_call(mix_kernel, out_shape=jax.ShapeDtypeStruct((own_tokens, ou...  3.82 us
    pallas_call x1, Pallas kernels, on_device(): pl.pallas_call(attend_kernel, out_shape=jax.ShapeDtypeStruct((*group.shap...  2.38 us
  transfers between devices with their start and end apart: 2, of which 2 were waited for; matrix products, arithmetic and copies ran while one was open for 0% of the time, Pallas kernels for 0%

profile of v6, /device:TPU:1, one launch (start us, length us, event | category | flops | bytes accessed | tf_op | source)
XLA Modules:
  0.0 98.8 jit_solution(12453616300012620448)
XLA Ops:
  0.0 0.0 copy-start
  0.0 0.9 maximum_bitcast_fusion
  0.9 28.8 %all_to_all.20 = bf16[24,24,128]{2,1,0:T(8,128)(2,1)S(1)} all-to-all(bf16[24,24,128]{2,1,0:T(8,128)(2,1)S(1)} %pad.4), channel_id=1, replica_groups=mesh['zl'=3,'y'=8,'x'=4,'c'=2,'tp'=4] {'zl','c','tp'}, dimensions={0} | all-to-all | bytes 294912 | tf_op jit(solution)/shard_map/all_to_all | solution.py:104
  29.7 1.0 %broadcast_in_dim.12 = bf16[8,2,192,128]{3,2,1,0:T(8,128)(2,1)} broadcast(bf16[2,192,128]{2,1,0:T(8,128)(2,1)S(1)} %copy_bitcast_fusion), dimensions={1,2,3} | broadcast | bytes 884736 | tf_op jit(solution)/shard_map/broadcast_in_dim | solution.py:108
  30.7 6.8 %all-to-all-start.1 = ((bf16[8,2,192,128]{3,2,1,0:T(8,128)(2,1)}), bf16[8,2,192,128]{3,2,1,0:T(8,128)(2,1)S(1)}, u32[]{:S(2)}, u32[]{:S(2)}) async-start(bf16[8,2,192,128]{3,2,1,0:T(8,128)(2,1)} %broadcast_in_dim.12), calls=%async_computation.1 | async-start | bytes 1572864 | tf_op jit(solution)/shard_map/all_to_all | solution.py:104
  37.6 9.9 %all_gather.3.q_ref = bf16[4,192,128]{2,1,0:T(8,128)(2,1)S(1)} all-gather(bf16[1,192,128]{2,1,0:T(8,128)(2,1)S(1)} %slice_bitcast_fusion), channel_id=1, replica_groups=mesh['zl'=3,'y'=8,'x'=4,'c'=2,'tp'=4] {'x'}, dimensions={0}, use_global_device_ids=true | all-gather | bytes 245760 | tf_op jit(solution)/shard_map/all_gather | solution.py:124
  47.5 12.5 %all-to-all-done.1.key_value_ref = bf16[8,2,192,128]{3,2,1,0:T(8,128)(2,1)S(1)} async-done(((bf16[8,2,192,128]{3,2,1,0:T(8,128)(2,1)}), bf16[8,2,192,128]{3,2,1,0:T(8,128)(2,1)S(1)}, u32[]{:S(2)}, u32[]{:S(2)}) %all-to-all-start.1) | async-done | bytes 786464 | tf_op jit(solution)/shard_map/all_to_all | solution.py:104
  60.0 2.4 %attend.1 = bf16[4,192,256]{2,1,0:T(8,128)(2,1)S(1)} custom-call(bf16[4,192,128]{2,1,0:T(8,128)(2,1)S(1)} %all_gather.3.q_ref, bf16[8,2,192,128]{3,2,1,0:T(8,128)(2,1)S(1)} %all-to-all-done.1.key_value_ref), custom_call_target="tpu_custom_call" | custom-call | tf_op jit(solution)/shard_map/attend/pallas_call | solution.py:126
  62.4 10.0 %all_to_all.21.part_ref = bf16[4,192,256]{2,1,0:T(8,128)(2,1)S(1)} all-to-all(bf16[4,192,256]{2,1,0:T(8,128)(2,1)S(1)} %attend.1), channel_id=1, replica_groups=mesh['zl'=3,'y'=8,'x'=4,'c'=2,'tp'=4] {'x'}, dimensions={0} | all-to-all | bytes 786432 | tf_op jit(solution)/shard_map/all_to_all | solution.py:104
  72.4 1.1 %combine.1 = bf16[24,32,128]{2,1,0:T(8,128)(2,1)} custom-call(bf16[4,192,256]{2,1,0:T(8,128)(2,1)S(1)} %all_to_all.21.part_ref), custom_call_target="tpu_custom_call" | custom-call | tf_op jit(solution)/shard_map/combine/pallas_call | solution.py:135
  73.5 7.5 %all-to-all-start.3 = ((bf16[24,32,128]{2,1,0:T(8,128)(2,1)}), bf16[24,32,128]{2,1,0:T(8,128)(2,1)S(1)}, u32[]{:S(2)}, u32[]{:S(2)}) async-start(bf16[24,32,128]{2,1,0:T(8,128)(2,1)} %combine.1), calls=%async_computation.3 | async-start | bytes 393216 | tf_op jit(solution)/shard_map/all_to_all | solution.py:104
  81.1 0.0 copy-done
  81.1 13.8 %all-to-all-done.3.attended_ref = bf16[24,32,128]{2,1,0:T(8,128)(2,1)S(1)} async-done(((bf16[24,32,128]{2,1,0:T(8,128)(2,1)}), bf16[24,32,128]{2,1,0:T(8,128)(2,1)S(1)}, u32[]{:S(2)}, u32[]{:S(2)}) %all-to-all-start.3) | async-done | bytes 196640 | tf_op jit(solution)/shard_map/all_to_all | solution.py:104
  94.9 3.8 %mix.1 = bf16[32,1280]{1,0:T(8,128)(2,1)} custom-call(bf16[24,32,128]{2,1,0:T(8,128)(2,1)S(1)} %all-to-all-done.3.attended_ref, f32[1,1280]{1,0:T(1,128)S(1)} %broadcast_in_dim.13.gate_ref, bf16[2560,1280]{1,0:T(8,128)(2,1)} %weight_ref.1), custom_call_target="tpu_custom_call" | custom-call | tf_op jit(solution)/shard_map/mix/pallas_call | solution.py:144
  (4 shorter events, 0.0 us)
Async XLA Ops:
  0.0 81.1 %copy-start = (f32[1280]{0:T(1024)S(1)}, f32[1280]{0:T(1024)}, u32[]{:S(2)}) copy-start(f32[1280]{0:T(1024)} %param.9) | copy-start | bytes 15364
  30.7 29.2 %all-to-all-start.1 = ((bf16[8,2,192,128]{3,2,1,0:T(8,128)(2,1)}), bf16[8,2,192,128]{3,2,1,0:T(8,128)(2,1)S(1)}, u32[]{:S(2)}, u32[]{:S(2)}) async-start(bf16[8,2,192,128]{3,2,1,0:T(8,128)(2,1)} %broadcast_in_dim.12), calls=%async_computation.1 | async-start | bytes 1572864 | tf_op jit(solution)/shard_map/all_to_all | solution.py:104
  73.5 21.4 %all-to-all-start.3 = ((bf16[24,32,128]{2,1,0:T(8,128)(2,1)}), bf16[24,32,128]{2,1,0:T(8,128)(2,1)S(1)}, u32[]{:S(2)}, u32[]{:S(2)}) async-start(bf16[24,32,128]{2,1,0:T(8,128)(2,1)} %combine.1), calls=%async_computation.3 | async-start | bytes 393216 | tf_op jit(solution)/shard_map/all_to_all | solution.py:104

commit v7 on v6

--- a/solution.py
+++ b/solution.py
@@ -9,30 +9,46 @@
 LOG2E = 1.4426950408889634
 SCALE = HEAD_DIM ** -0.5
 HEAD_AXES = ("zl", "c", "tp")
-QUERY_AXES = ("x",)
-KEY_AXES = ("y",)
-PIECE_LANES = 8
+QUERY_AXES = ("y",)
+KEY_AXES = ("x",)
+STATS = 2
+STAT_LANES = 8
+STAT_ROWS = 16
 KERNEL_VMEM = 16 * 1024 * 1024
 MIX_VMEM = 50 * 1024 * 1024
 IN_VMEM = pl.BlockSpec(memory_space=pltpu.VMEM)
 
 
-def split_pieces(stats):
+def pack_stats(highest, total):
+    tokens = highest.shape[0]
+    lane = lax.broadcasted_iota(jnp.int32, (tokens, HEAD_DIM), 1)
+    stats = jnp.where(lane == 0, highest, jnp.where(lane == 1, total, 0.0))
     high = stats.astype(jnp.bfloat16).astype(jnp.float32)
     rest = stats - high
     middle = rest.astype(jnp.bfloat16).astype(jnp.float32)
     low = rest - middle
-    lane = lax.broadcasted_iota(jnp.int32, stats.shape, 1)
-    spread = jnp.where(
-        lane < PIECE_LANES,
-        high,
-        jnp.where(
-            lane < 2 * PIECE_LANES,
-            pltpu.roll(middle, PIECE_LANES, 1),
-            pltpu.roll(low, 2 * PIECE_LANES, 1),
-        ),
+    pieces = high + pltpu.roll(middle, STATS, 1) + pltpu.roll(low, 2 * STATS, 1)
+    filler = jnp.zeros((2 * HEAD_DIM - tokens, HEAD_DIM), jnp.float32)
+    rows = jnp.concatenate([pieces, filler], axis=0).T[:STAT_LANES]
+    return jnp.concatenate([rows[:, :HEAD_DIM], rows[:, HEAD_DIM:]], axis=0).astype(jnp.bfloat16)
+
+
+def unpack_stats(packed, tokens):
+    groups = packed.shape[0]
+    rows = packed.astype(jnp.float32)
+    filler = jnp.zeros((HEAD_DIM - groups * STAT_LANES, HEAD_DIM), jnp.float32)
+    halves = [
+        jnp.concatenate(
+            [rows[group, half : half + STAT_LANES] for group in range(groups)] + [filler], axis=0
+        )
+        for half in (0, STAT_LANES)
+    ]
+    pieces = jnp.concatenate([half.T for half in halves], axis=0)[:tokens]
+    return (
+        pieces
+        + pltpu.roll(pieces, HEAD_DIM - STATS, 1)
+        + pltpu.roll(pieces, HEAD_DIM - 2 * STATS, 1)
     )
-    return spread.astype(jnp.bfloat16)
 
 
 def attend_kernel(q_ref, key_value_ref, out_ref):
@@ -40,7 +56,6 @@
     count = key_value_ref.shape[0] * tokens
     key = key_value_ref[:, 0].reshape(count, width)
     value = key_value_ref[:, 1].reshape(count, width)
-    lane = lax.broadcasted_iota(jnp.int32, (tokens, HEAD_DIM), 1)
     for group in range(groups):
         score = lax.dot_general(
             q_ref[group], key, (((1,), (1,)), ((), ())), preferred_element_type=jnp.float32
@@ -49,25 +64,26 @@
         expd = jnp.exp2((score - highest) * (SCALE * LOG2E))
         total = jnp.sum(expd, axis=1, keepdims=True)
         summed = jnp.dot(expd.astype(jnp.bfloat16), value, preferred_element_type=jnp.float32)
-        out_ref[group, :, pl.ds(0, width)] = summed.astype(jnp.bfloat16)
-        stats = jnp.where(lane == 0, highest, jnp.where(lane == 1, total, 0.0))
-        out_ref[group, :, pl.ds(width, HEAD_DIM)] = split_pieces(stats)
+        out_ref[group, pl.ds(0, tokens)] = summed.astype(jnp.bfloat16)
+        out_ref[group, pl.ds(tokens, STAT_ROWS)] = pack_stats(highest, total)
 
 
 def combine_kernel(part_ref, out_ref):
-    groups, tokens, _ = part_ref.shape
-    copies, rows, width = out_ref.shape
-    pieces = part_ref[:, :, pl.ds(width, HEAD_DIM)].astype(jnp.float32)
-    pieces = pieces.reshape(groups * tokens, HEAD_DIM)
-    stats = (
-        pieces
-        + pltpu.roll(pieces, HEAD_DIM - PIECE_LANES, 1)
-        + pltpu.roll(pieces, HEAD_DIM - 2 * PIECE_LANES, 1)
-    ).reshape(groups, tokens, HEAD_DIM)
-    maxima, sums = stats[:, :, 0:1], stats[:, :, 1:2]
-    weight = jnp.exp2((maxima - jnp.max(maxima, axis=0, keepdims=True)) * (SCALE * LOG2E))
-    total = jnp.sum(weight * sums, axis=0)
-    summed = jnp.sum(part_ref[:, :, pl.ds(0, width)].astype(jnp.float32) * weight, axis=0)
+    groups = part_ref.shape[0]
+    tokens = part_ref.shape[1] - STAT_ROWS
+    copies, rows, _ = out_ref.shape
+    stats = unpack_stats(part_ref[:, pl.ds(tokens, STAT_ROWS)], tokens)
+    lane = lax.broadcasted_iota(jnp.int32, stats.shape, 1)
+    is_maximum = (lane % STAT_LANES == 0) & (lane < groups * STAT_LANES)
+    highest = jnp.max(jnp.where(is_maximum, stats, -jnp.inf), axis=1, keepdims=True)
+    weight = jnp.where(is_maximum, jnp.exp2((stats - highest) * (SCALE * LOG2E)), 0.0)
+    sums = jnp.where(is_maximum, pltpu.roll(stats, HEAD_DIM - 1, 1), 0.0)
+    total = jnp.sum(weight * sums, axis=1, keepdims=True)
+    summed = jnp.zeros(stats.shape, jnp.float32)
+    for group in range(groups):
+        at = group * STAT_LANES
+        part = part_ref[group, pl.ds(0, tokens)].astype(jnp.float32)
+        summed += part * weight[:, at : at + 1]
     attended = (summed / total).astype(jnp.bfloat16)
     repeats = copies * rows // tokens
     for block in range(tokens // rows):
@@ -120,12 +136,15 @@
     local = exchange(stacked, HEAD_AXES)
     local = local.reshape(slots, 3, rows, HEAD_DIM).transpose(1, 0, 2, 3)
     local = local.reshape(3, tokens, HEAD_DIM)
-    key_value = exchange(spread_to(local[1:], lax.axis_size(KEY_AXES)), KEY_AXES)
-    group = lax.all_gather(local[0], QUERY_AXES, axis=0, tiled=False)
-    key_value, group = lax.optimization_barrier((key_value, group))
+    group = exchange(spread_to(local[0], lax.axis_size(QUERY_AXES)), QUERY_AXES)
+    key_value = lax.all_gather(local[1:], KEY_AXES, axis=0, tiled=False)
+    gate_row = gate[None, :]
+    key_value, group, gate_row = lax.optimization_barrier((key_value, group, gate_row))
     partial = pl.pallas_call(
         attend_kernel,
-        out_shape=jax.ShapeDtypeStruct((*group.shape[:2], 2 * HEAD_DIM), jnp.bfloat16),
+        out_shape=jax.ShapeDtypeStruct(
+            (group.shape[0], tokens + STAT_ROWS, HEAD_DIM), jnp.bfloat16
+        ),
         in_specs=[IN_VMEM] * 2,
         out_specs=IN_VMEM,
         compiler_params=pltpu.CompilerParams(vmem_limit_bytes=KERNEL_VMEM),
@@ -152,7 +171,7 @@
         ],
         compiler_params=pltpu.CompilerParams(vmem_limit_bytes=MIX_VMEM),
         name="mix",
-    )(attended, gate[None, :], out_weight)
+    )(attended, gate_row, out_weight)
 
 
 def solution(mesh):

time: 99.1 us -> 98.3 us (level)
  blocking collectives: 48.7 us -> 78.9 us
  waiting for transfers between devices: 26.4 us -> 1.42 us
  starting transfers between devices: 14.4 us -> 6.82 us
  Pallas kernels: 7.3 us -> 8.4 us
    all_to_all x2 -> x3, blocking collectives: 38.8 us -> 68.6 us  [exchange(): return lax.all_to_all(blocks, axes, split_axis=0, concat_axis=0, tiled=True)]
    all_to_all x2 -> x1, waiting for transfers between devices: 26.4 us -> 1.42 us  [exchange(): return lax.all_to_all(blocks, axes, split_axis=0, concat_axis=0, tiled=True)]
    all_to_all x2 -> x1, starting transfers between devices: 14.4 us -> 6.82 us  [exchange(): return lax.all_to_all(blocks, axes, split_axis=0, concat_axis=0, tiled=True)]
    pallas_call x1, Pallas kernels: 2.38 us -> 3.62 us  [on_device(): pl.pallas_call(attend_kernel, out_shape=jax.ShapeDtypeStruct((group.shape...]
  transfers between devices with their start and end apart: 2 -> 1, of which waited for: 2 -> 1; matrix products, arithmetic and copies ran while one was open for 0% -> 1% of each run, Pallas kernels for 0% -> 0%
where the time goes in v7:
time: 98.3 us; the launch traced here: 97.9 us
  blocking collectives  78.9 us (80%)
  Pallas kernels  8.4 us (9%)
  starting transfers between devices  6.82 us (7%)
  local copies, waits for them, and re-layouts  1.52 us (2%)
  waiting for transfers between devices  1.42 us (1%)
    all_to_all x3, blocking collectives, exchange(): return lax.all_to_all(blocks, axes, split_axis=0, concat_axis=0, tiled=True)  68.6 us
    all_gather x1, blocking collectives, on_device(): key_value = lax.all_gather(local[1:], KEY_AXES, axis=0, tiled=False)  10.3 us
    all_to_all x1, starting transfers between devices, exchange(): return lax.all_to_all(blocks, axes, split_axis=0, concat_axis=0, tiled=True)  6.82 us
    pallas_call x1, Pallas kernels, on_device(): pl.pallas_call(mix_kernel, out_shape=jax.ShapeDtypeStruct((own_tokens, ou...  3.82 us
    pallas_call x1, Pallas kernels, on_device(): pl.pallas_call(attend_kernel, out_shape=jax.ShapeDtypeStruct((group.shape...  3.62 us
  transfers between devices with their start and end apart: 1, of which 1 were waited for; matrix products, arithmetic and copies ran while one was open for 1% of the time, Pallas kernels for 0%

profile of v7, /device:TPU:1, one launch (start us, length us, event | category | flops | bytes accessed | tf_op | source)
XLA Modules:
  0.0 97.9 jit_solution(4047196362493988167)
XLA Ops:
  0.0 0.8 maximum_bitcast_fusion
  0.9 28.8 %all_to_all.20 = bf16[24,24,128]{2,1,0:T(8,128)(2,1)S(1)} all-to-all(bf16[24,24,128]{2,1,0:T(8,128)(2,1)S(1)} %pad.4), channel_id=1, replica_groups=mesh['zl'=3,'y'=8,'x'=4,'c'=2,'tp'=4] {'zl','c','tp'}, dimensions={0} | all-to-all | bytes 294912 | tf_op jit(solution)/shard_map/all_to_all | solution.py:120
  29.7 0.8 broadcast_in_dim.11
  30.5 6.8 %all-to-all-start.1 = ((bf16[8,192,128]{2,1,0:T(8,128)(2,1)}), bf16[8,192,128]{2,1,0:T(8,128)(2,1)S(1)}, u32[]{:S(2)}, u32[]{:S(2)}) async-start(bf16[8,192,128]{2,1,0:T(8,128)(2,1)} %broadcast_in_dim.11), calls=%async_computation.1 | async-start | bytes 786432 | tf_op jit(solution)/shard_map/all_to_all | solution.py:120
  37.3 0.7 broadcast_in_dim.12.gate_ref
  38.0 10.3 %all_gather.7.key_value_ref = bf16[4,2,192,128]{3,2,1,0:T(8,128)(2,1)S(1)} all-gather(bf16[1,2,192,128]{3,2,1,0:T(8,128)(2,1)S(1)} %copy_bitcast_fusion), channel_id=1, replica_groups=mesh['zl'=3,'y'=8,'x'=4,'c'=2,'tp'=4] {'x'}, dimensions={0}, use_global_device_ids=true | all-gather | bytes 491520 | tf_op jit(solution)/shard_map/all_gather | solution.py:140
  48.3 1.4 %all-to-all-done.1.q_ref = bf16[8,192,128]{2,1,0:T(8,128)(2,1)S(1)} async-done(((bf16[8,192,128]{2,1,0:T(8,128)(2,1)}), bf16[8,192,128]{2,1,0:T(8,128)(2,1)S(1)}, u32[]{:S(2)}, u32[]{:S(2)}) %all-to-all-start.1) | async-done | bytes 393248 | tf_op jit(solution)/shard_map/all_to_all | solution.py:120
  49.7 3.6 %attend.1 = bf16[8,208,128]{2,1,0:T(8,128)(2,1)S(1)} custom-call(bf16[8,192,128]{2,1,0:T(8,128)(2,1)S(1)} %all-to-all-done.1.q_ref, bf16[4,2,192,128]{3,2,1,0:T(8,128)(2,1)S(1)} %all_gather.7.key_value_ref), custom_call_target="tpu_custom_call" | custom-call | tf_op jit(solution)/shard_map/attend/pallas_call | solution.py:143
  53.3 16.5 %all_to_all.21.part_ref = bf16[8,208,128]{2,1,0:T(8,128)(2,1)S(1)} all-to-all(bf16[8,208,128]{2,1,0:T(8,128)(2,1)S(1)} %attend.1), channel_id=1, replica_groups=mesh['zl'=3,'y'=8,'x'=4,'c'=2,'tp'=4] {'y'}, dimensions={0} | all-to-all | bytes 851968 | tf_op jit(solution)/shard_map/all_to_all | solution.py:120
  69.8 1.0 combine.1
  70.8 23.3 %all_to_all.22.attended_ref = bf16[24,32,128]{2,1,0:T(8,128)(2,1)S(1)} all-to-all(bf16[24,32,128]{2,1,0:T(8,128)(2,1)S(1)} %combine.1), channel_id=1, replica_groups=mesh['zl'=3,'y'=8,'x'=4,'c'=2,'tp'=4] {'zl','c','tp'}, dimensions={0} | all-to-all | bytes 393216 | tf_op jit(solution)/shard_map/all_to_all | solution.py:120
  94.1 3.8 %mix.1 = bf16[32,1280]{1,0:T(8,128)(2,1)} custom-call(bf16[24,32,128]{2,1,0:T(8,128)(2,1)S(1)} %all_to_all.22.attended_ref, f32[1,1280]{1,0:T(1,128)S(1)} %broadcast_in_dim.12.gate_ref, bf16[2560,1280]{1,0:T(8,128)(2,1)} %weight_ref.1), custom_call_target="tpu_custom_call" | custom-call | tf_op jit(solution)/shard_map/mix/pallas_call | solution.py:163
  (3 shorter events, 0.0 us)
Async XLA Ops:
  30.5 19.2 %all-to-all-start.1 = ((bf16[8,192,128]{2,1,0:T(8,128)(2,1)}), bf16[8,192,128]{2,1,0:T(8,128)(2,1)S(1)}, u32[]{:S(2)}, u32[]{:S(2)}) async-start(bf16[8,192,128]{2,1,0:T(8,128)(2,1)} %broadcast_in_dim.11), calls=%async_computation.1 | async-start | bytes 786432 | tf_op jit(solution)/shard_map/all_to_all | solution.py:120

commit v8 on v7

--- a/solution.py
+++ b/solution.py
@@ -14,23 +14,32 @@
 STATS = 2
 STAT_LANES = 8
 STAT_ROWS = 16
+GROUP_STEP = 2
 KERNEL_VMEM = 16 * 1024 * 1024
 MIX_VMEM = 50 * 1024 * 1024
 IN_VMEM = pl.BlockSpec(memory_space=pltpu.VMEM)
 
 
-def pack_stats(highest, total):
-    tokens = highest.shape[0]
+def pack_stats(columns):
+    tokens = columns[0][0].shape[0]
     lane = lax.broadcasted_iota(jnp.int32, (tokens, HEAD_DIM), 1)
-    stats = jnp.where(lane == 0, highest, jnp.where(lane == 1, total, 0.0))
+    stats = jnp.zeros((tokens, HEAD_DIM), jnp.float32)
+    for group, values in enumerate(columns):
+        for place, value in enumerate(values):
+            stats = jnp.where(lane == group * STAT_LANES + place, value, stats)
     high = stats.astype(jnp.bfloat16).astype(jnp.float32)
     rest = stats - high
     middle = rest.astype(jnp.bfloat16).astype(jnp.float32)
     low = rest - middle
     pieces = high + pltpu.roll(middle, STATS, 1) + pltpu.roll(low, 2 * STATS, 1)
     filler = jnp.zeros((2 * HEAD_DIM - tokens, HEAD_DIM), jnp.float32)
-    rows = jnp.concatenate([pieces, filler], axis=0).T[:STAT_LANES]
-    return jnp.concatenate([rows[:, :HEAD_DIM], rows[:, HEAD_DIM:]], axis=0).astype(jnp.bfloat16)
+    rows = jnp.concatenate([pieces, filler], axis=0).T
+    packed = []
+    for group in range(len(columns)):
+        own = rows[group * STAT_LANES : (group + 1) * STAT_LANES]
+        both = jnp.concatenate([own[:, :HEAD_DIM], own[:, HEAD_DIM:]], axis=0)
+        packed.append(both.astype(jnp.bfloat16))
+    return packed
 
 
 def unpack_stats(packed, tokens):
@@ -51,21 +60,38 @@
     )
 
 
+def split_kernel(local_ref, query_ref, key_value_ref):
+    slots = local_ref.shape[0]
+    rows = local_ref.shape[1] // 3
+    query = local_ref[:, pl.ds(0, rows)].reshape(slots * rows, HEAD_DIM)
+    for copy in range(query_ref.shape[0]):
+        query_ref[copy] = query
+    for place in range(2):
+        block = local_ref[:, pl.ds((place + 1) * rows, rows)]
+        key_value_ref[place] = block.reshape(slots * rows, HEAD_DIM)
+
+
 def attend_kernel(q_ref, key_value_ref, out_ref):
     groups, tokens, width = q_ref.shape
     count = key_value_ref.shape[0] * tokens
     key = key_value_ref[:, 0].reshape(count, width)
     value = key_value_ref[:, 1].reshape(count, width)
-    for group in range(groups):
+    columns = []
+    for group in range(0, groups, GROUP_STEP):
+        query = q_ref[pl.ds(group, GROUP_STEP)].reshape(GROUP_STEP * tokens, width)
         score = lax.dot_general(
-            q_ref[group], key, (((1,), (1,)), ((), ())), preferred_element_type=jnp.float32
+            query, key, (((1,), (1,)), ((), ())), preferred_element_type=jnp.float32
         )
         highest = jnp.max(score, axis=1, keepdims=True)
         expd = jnp.exp2((score - highest) * (SCALE * LOG2E))
         total = jnp.sum(expd, axis=1, keepdims=True)
         summed = jnp.dot(expd.astype(jnp.bfloat16), value, preferred_element_type=jnp.float32)
-        out_ref[group, pl.ds(0, tokens)] = summed.astype(jnp.bfloat16)
-        out_ref[group, pl.ds(tokens, STAT_ROWS)] = pack_stats(highest, total)
+        for step in range(GROUP_STEP):
+            rows = slice(step * tokens, (step + 1) * tokens)
+            out_ref[group + step, pl.ds(0, tokens)] = summed[rows].astype(jnp.bfloat16)
+            columns.append((highest[rows], total[rows]))
+    for group, packed in enumerate(pack_stats(columns)):
+        out_ref[group, pl.ds(tokens, STAT_ROWS)] = packed
 
 
 def combine_kernel(part_ref, out_ref):
@@ -113,15 +139,11 @@
             held_ref[pl.ds(first * HEAD_DIM, span * HEAD_DIM)],
             preferred_element_type=jnp.float32,
         )
-    out_ref[...] = (product * gate_ref[...]).astype(jnp.bfloat16)
+    out_ref[...] = (product * gate_ref[...][None, :]).astype(jnp.bfloat16)
 
 
 def exchange(blocks, axes):
     return lax.all_to_all(blocks, axes, split_axis=0, concat_axis=0, tiled=True)
-
-
-def spread_to(block, count):
-    return jnp.broadcast_to(block[None], (count, *block.shape))
 
 
 def on_device(queries, keys, vals, out_weight, gate):
@@ -133,13 +155,20 @@
     stacked = jnp.stack([queries, keys, vals], axis=0).reshape(3, rows, heads, HEAD_DIM)
     stacked = stacked.transpose(2, 0, 1, 3).reshape(heads, 3 * rows, HEAD_DIM)
     stacked = jnp.pad(stacked, ((0, slots - heads), (0, 0), (0, 0)))
-    local = exchange(stacked, HEAD_AXES)
-    local = local.reshape(slots, 3, rows, HEAD_DIM).transpose(1, 0, 2, 3)
-    local = local.reshape(3, tokens, HEAD_DIM)
-    group = exchange(spread_to(local[0], lax.axis_size(QUERY_AXES)), QUERY_AXES)
-    key_value = lax.all_gather(local[1:], KEY_AXES, axis=0, tiled=False)
-    gate_row = gate[None, :]
-    key_value, group, gate_row = lax.optimization_barrier((key_value, group, gate_row))
+    query_copies, own_key_value = pl.pallas_call(
+        split_kernel,
+        out_shape=[
+            jax.ShapeDtypeStruct((lax.axis_size(QUERY_AXES), tokens, HEAD_DIM), jnp.bfloat16),
+            jax.ShapeDtypeStruct((2, tokens, HEAD_DIM), jnp.bfloat16),
+        ],
+        in_specs=[IN_VMEM],
+        out_specs=[IN_VMEM] * 2,
+        compiler_params=pltpu.CompilerParams(vmem_limit_bytes=KERNEL_VMEM),
+        name="split",
+    )(exchange(stacked, HEAD_AXES))
+    group = exchange(query_copies, QUERY_AXES)
+    key_value = lax.all_gather(own_key_value, KEY_AXES, axis=0, tiled=False)
+    key_value, group = lax.optimization_barrier((key_value, group))
     partial = pl.pallas_call(
         attend_kernel,
         out_shape=jax.ShapeDtypeStruct(
@@ -171,7 +200,7 @@
         ],
         compiler_params=pltpu.CompilerParams(vmem_limit_bytes=MIX_VMEM),
         name="mix",
-    )(attended, gate_row, out_weight)
+    )(attended, gate, out_weight)
 
 
 def solution(mesh):

time: 98.3 us -> 96.6 us (0.983)
    pallas_call x1, Pallas kernels: 3.62 us -> 1.92 us  [on_device(): pl.pallas_call(attend_kernel, out_shape=jax.ShapeDtypeStruct((group.shape...]
    broadcast_in_dim x3 -> x0, local copies, waits for them, and re-layouts: 1.5 us -> none  [the longest x2 0.8 us: spread_to(): return jnp.broadcast_to(block[None], (count, *block.shape))]
  transfers between devices with their start and end apart: 1 -> 1, of which waited for: 1 -> 1; matrix products, arithmetic and copies ran while one was open for 1% -> 0% of each run, Pallas kernels for 0% -> 0%
where the time goes in v8:
time: 96.6 us; the launch traced here: 96.2 us
  blocking collectives  78.1 us (81%)
  Pallas kernels  7.52 us (8%)
  starting transfers between devices  6.82 us (7%)
  waiting for transfers between devices  2.14 us (2%)
    all_to_all x3, blocking collectives, exchange(): return lax.all_to_all(blocks, axes, split_axis=0, concat_axis=0, tiled=True)  67.9 us
    all_gather x1, blocking collectives, on_device(): key_value = lax.all_gather(own_key_value, KEY_AXES, axis=0, tiled=False)  10.3 us
    all_to_all x1, starting transfers between devices, exchange(): return lax.all_to_all(blocks, axes, split_axis=0, concat_axis=0, tiled=True)  6.82 us
    pallas_call x1, Pallas kernels, on_device(): pl.pallas_call(mix_kernel, out_shape=jax.ShapeDtypeStruct((own_tokens, ou...  3.82 us
    all_to_all x1, waiting for transfers between devices, exchange(): return lax.all_to_all(blocks, axes, split_axis=0, concat_axis=0, tiled=True)  2.14 us
  transfers between devices with their start and end apart: 1, of which 1 were waited for; matrix products, arithmetic and copies ran while one was open for 0% of the time, Pallas kernels for 0%

profile of v8, /device:TPU:1, one launch (start us, length us, event | category | flops | bytes accessed | tf_op | source)
XLA Modules:
  0.0 96.2 jit_solution(9536573178831623928)
XLA Ops:
  0.0 0.8 maximum_bitcast_fusion
  0.9 28.8 %all_to_all.20.local_ref = bf16[24,24,128]{2,1,0:T(8,128)(2,1)S(1)} all-to-all(bf16[24,24,128]{2,1,0:T(8,128)(2,1)S(1)} %pad.4), channel_id=1, replica_groups=mesh['zl'=3,'y'=8,'x'=4,'c'=2,'tp'=4] {'zl','c','tp'}, dimensions={0} | all-to-all | bytes 294912 | tf_op jit(solution)/shard_map/all_to_all | solution.py:146
  29.7 0.8 split.1
  30.5 6.8 %all-to-all-start.1 = ((bf16[8,192,128]{2,1,0:T(8,128)(2,1)}), bf16[8,192,128]{2,1,0:T(8,128)(2,1)S(1)}, u32[]{:S(2)}, u32[]{:S(2)}) async-start(bf16[8,192,128]{2,1,0:T(8,128)(2,1)} %get-tuple-element.10), calls=%async_computation.1 | async-start | bytes 786432 | tf_op jit(solution)/shard_map/all_to_all | solution.py:146
  37.3 10.3 %all-gather = bf16[8,192,128]{2,1,0:T(8,128)(2,1)S(1)} all-gather(bf16[2,192,128]{2,1,0:T(8,128)(2,1)S(1)} %get-tuple-element.9), channel_id=2, replica_groups=mesh['zl'=3,'y'=8,'x'=4,'c'=2,'tp'=4] {'x'}, dimensions={0}, use_global_device_ids=true | all-gather | bytes 491520 | tf_op jit(solution)/shard_map/all_gather | solution.py:170
  47.6 2.1 %all-to-all-done.1.q_ref = bf16[8,192,128]{2,1,0:T(8,128)(2,1)S(1)} async-done(((bf16[8,192,128]{2,1,0:T(8,128)(2,1)}), bf16[8,192,128]{2,1,0:T(8,128)(2,1)S(1)}, u32[]{:S(2)}, u32[]{:S(2)}) %all-to-all-start.1) | async-done | bytes 393248 | tf_op jit(solution)/shard_map/all_to_all | solution.py:146
  49.7 1.9 %attend.1 = bf16[8,208,128]{2,1,0:T(8,128)(2,1)S(1)} custom-call(bf16[8,192,128]{2,1,0:T(8,128)(2,1)S(1)} %all-to-all-done.1.q_ref, bf16[4,2,192,128]{3,2,1,0:T(8,128)(2,1)S(1)} %bitcast.14), custom_call_target="tpu_custom_call" | custom-call | tf_op jit(solution)/shard_map/attend/pallas_call | solution.py:172
  51.7 15.8 %all_to_all.21.part_ref = bf16[8,208,128]{2,1,0:T(8,128)(2,1)S(1)} all-to-all(bf16[8,208,128]{2,1,0:T(8,128)(2,1)S(1)} %attend.1), channel_id=1, replica_groups=mesh['zl'=3,'y'=8,'x'=4,'c'=2,'tp'=4] {'y'}, dimensions={0} | all-to-all | bytes 851968 | tf_op jit(solution)/shard_map/all_to_all | solution.py:146
  67.4 1.0 %combine.1 = bf16[24,32,128]{2,1,0:T(8,128)(2,1)S(1)} custom-call(bf16[8,208,128]{2,1,0:T(8,128)(2,1)S(1)} %all_to_all.21.part_ref), custom_call_target="tpu_custom_call" | custom-call | tf_op jit(solution)/shard_map/combine/pallas_call | solution.py:183
  68.4 23.3 %all_to_all.22.attended_ref = bf16[24,32,128]{2,1,0:T(8,128)(2,1)S(1)} all-to-all(bf16[24,32,128]{2,1,0:T(8,128)(2,1)S(1)} %combine.1), channel_id=1, replica_groups=mesh['zl'=3,'y'=8,'x'=4,'c'=2,'tp'=4] {'zl','c','tp'}, dimensions={0} | all-to-all | bytes 393216 | tf_op jit(solution)/shard_map/all_to_all | solution.py:146
  91.7 0.0 copy-start
  91.7 0.7 copy-done
  92.4 3.8 %mix.1 = bf16[32,1280]{1,0:T(8,128)(2,1)} custom-call(bf16[24,32,128]{2,1,0:T(8,128)(2,1)S(1)} %all_to_all.22.attended_ref, f32[1280]{0:T(1024)S(1)} %copy-done, bf16[2560,1280]{1,0:T(8,128)(2,1)} %weight_ref.1), custom_call_target="tpu_custom_call" | custom-call | tf_op jit(solution)/shard_map/mix/pallas_call | solution.py:192
  (1 shorter events, 0.0 us)
Async XLA Ops:
  30.5 19.2 %all-to-all-start.1 = ((bf16[8,192,128]{2,1,0:T(8,128)(2,1)}), bf16[8,192,128]{2,1,0:T(8,128)(2,1)S(1)}, u32[]{:S(2)}, u32[]{:S(2)}) async-start(bf16[8,192,128]{2,1,0:T(8,128)(2,1)} %get-tuple-element.10), calls=%async_computation.1 | async-start | bytes 786432 | tf_op jit(solution)/shard_map/all_to_all | solution.py:146
  91.7 0.7 copy-start

commit v9 on v8

--- a/solution.py
+++ b/solution.py
@@ -10,7 +10,8 @@
 SCALE = HEAD_DIM ** -0.5
 HEAD_AXES = ("zl", "c", "tp")
 QUERY_AXES = ("y",)
-KEY_AXES = ("x",)
+KEY_AXIS = "x"
+KEY_PAIRS = ([[0, 1], [2, 3]], [[1, 2], [3, 0]])
 STATS = 2
 STAT_LANES = 8
 STAT_ROWS = 16
@@ -167,7 +168,11 @@
         name="split",
     )(exchange(stacked, HEAD_AXES))
     group = exchange(query_copies, QUERY_AXES)
-    key_value = lax.all_gather(own_key_value, KEY_AXES, axis=0, tiled=False)
+    key_value = own_key_value[None]
+    for pairs in KEY_PAIRS:
+        key_value = lax.all_gather(
+            key_value, KEY_AXIS, axis=0, tiled=True, axis_index_groups=pairs
+        )
     key_value, group = lax.optimization_barrier((key_value, group))
     partial = pl.pallas_call(
         attend_kernel,

time: 96.6 us -> 97.9 us (1.013)
  blocking collectives: 78.1 us -> 80 us
    all_to_all x3, blocking collectives: 67.9 us -> 69.2 us  [exchange(): return lax.all_to_all(blocks, axes, split_axis=0, concat_axis=0, tiled=True)]
    all_gather x1 -> x2, blocking collectives: 10.3 us -> 10.8 us  [on_device(): lax.all_gather(key_value, KEY_AXIS, axis=0, tiled=True, axis_index_groups...]
where the time goes in v9:
time: 97.9 us; the launch traced here: 97.5 us
  blocking collectives  80 us (82%)
  Pallas kernels  7.52 us (8%)
  starting transfers between devices  6.82 us (7%)
  waiting for transfers between devices  1.59 us (2%)
    all_to_all x3, blocking collectives, exchange(): return lax.all_to_all(blocks, axes, split_axis=0, concat_axis=0, tiled=True)  69.2 us
    all_gather x2, blocking collectives, on_device(): lax.all_gather(key_value, KEY_AXIS, axis=0, tiled=True, axis_index_groups...  10.8 us
    all_to_all x1, starting transfers between devices, exchange(): return lax.all_to_all(blocks, axes, split_axis=0, concat_axis=0, tiled=True)  6.82 us
    pallas_call x1, Pallas kernels, on_device(): pl.pallas_call(mix_kernel, out_shape=jax.ShapeDtypeStruct((own_tokens, ou...  3.82 us
  transfers between devices with their start and end apart: 1, of which 1 were waited for; matrix products, arithmetic and copies ran while one was open for 0% of the time, Pallas kernels for 0%

profile of v9, /device:TPU:1, one launch (start us, length us, event | category | flops | bytes accessed | tf_op | source)
XLA Modules:
  0.0 97.5 jit_solution(15983685706181487822)
XLA Ops:
  0.0 0.8 maximum_bitcast_fusion
  0.9 28.8 %all_to_all.20.local_ref = bf16[24,24,128]{2,1,0:T(8,128)(2,1)S(1)} all-to-all(bf16[24,24,128]{2,1,0:T(8,128)(2,1)S(1)} %pad.4), channel_id=1, replica_groups=mesh['zl'=3,'y'=8,'x'=4,'c'=2,'tp'=4] {'zl','c','tp'}, dimensions={0} | all-to-all | bytes 294912 | tf_op jit(solution)/shard_map/all_to_all | solution.py:147
  29.7 0.8 split.1
  30.5 6.8 %all-to-all-start.1 = ((bf16[8,192,128]{2,1,0:T(8,128)(2,1)}), bf16[8,192,128]{2,1,0:T(8,128)(2,1)S(1)}, u32[]{:S(2)}, u32[]{:S(2)}) async-start(bf16[8,192,128]{2,1,0:T(8,128)(2,1)} %get-tuple-element.10), calls=%async_computation.1 | async-start | bytes 786432 | tf_op jit(solution)/shard_map/all_to_all | solution.py:147
  37.3 4.1 %all-gather = bf16[4,192,128]{2,1,0:T(8,128)(2,1)S(1)} all-gather(bf16[2,192,128]{2,1,0:T(8,128)(2,1)S(1)} %get-tuple-element.9), channel_id=2, replica_groups={{0,8},{16,24},{1,9},{17,25},{2,10},{18,26},{3,11},{19,27},{4,12},{20,28..., dimensions={0}, use_global_device_ids=true | all-gather | bytes 294912 | tf_op jit(solution)/shard_map/all_gather | solution.py:173
  41.4 6.7 %all_gather.7.key_value_ref = bf16[4,2,192,128]{3,2,1,0:T(8,128)(2,1)S(1)} all-gather(bf16[2,2,192,128]{3,2,1,0:T(8,128)(2,1)S(1)} %bitcast.14), channel_id=1, replica_groups={{8,16},{24,0},{9,17},{25,1},{10,18},{26,2},{11,19},{27,3},{12,20},{28,4..., dimensions={0}, use_global_device_ids=true | all-gather | bytes 589824 | tf_op jit(solution)/shard_map/all_gather | solution.py:173
  48.1 1.6 %all-to-all-done.1.q_ref = bf16[8,192,128]{2,1,0:T(8,128)(2,1)S(1)} async-done(((bf16[8,192,128]{2,1,0:T(8,128)(2,1)}), bf16[8,192,128]{2,1,0:T(8,128)(2,1)S(1)}, u32[]{:S(2)}, u32[]{:S(2)}) %all-to-all-start.1) | async-done | bytes 393248 | tf_op jit(solution)/shard_map/all_to_all | solution.py:147
  49.7 1.9 %attend.1 = bf16[8,208,128]{2,1,0:T(8,128)(2,1)S(1)} custom-call(bf16[8,192,128]{2,1,0:T(8,128)(2,1)S(1)} %all-to-all-done.1.q_ref, bf16[4,2,192,128]{3,2,1,0:T(8,128)(2,1)S(1)} %all_gather.7.key_value_ref), custom_call_target="tpu_custom_call" | custom-call | tf_op jit(solution)/shard_map/attend/pallas_call | solution.py:177
  51.7 16.0 %all_to_all.21.part_ref = bf16[8,208,128]{2,1,0:T(8,128)(2,1)S(1)} all-to-all(bf16[8,208,128]{2,1,0:T(8,128)(2,1)S(1)} %attend.1), channel_id=1, replica_groups=mesh['zl'=3,'y'=8,'x'=4,'c'=2,'tp'=4] {'y'}, dimensions={0} | all-to-all | bytes 851968 | tf_op jit(solution)/shard_map/all_to_all | solution.py:147
  67.6 1.0 combine.1
  68.6 24.4 %all_to_all.22.attended_ref = bf16[24,32,128]{2,1,0:T(8,128)(2,1)S(1)} all-to-all(bf16[24,32,128]{2,1,0:T(8,128)(2,1)S(1)} %combine.1), channel_id=1, replica_groups=mesh['zl'=3,'y'=8,'x'=4,'c'=2,'tp'=4] {'zl','c','tp'}, dimensions={0} | all-to-all | bytes 393216 | tf_op jit(solution)/shard_map/all_to_all | solution.py:147
  93.0 0.0 copy-start
  93.0 0.7 copy-done
  93.7 3.8 %mix.1 = bf16[32,1280]{1,0:T(8,128)(2,1)} custom-call(bf16[24,32,128]{2,1,0:T(8,128)(2,1)S(1)} %all_to_all.22.attended_ref, f32[1280]{0:T(1024)S(1)} %copy-done, bf16[2560,1280]{1,0:T(8,128)(2,1)} %weight_ref.1), custom_call_target="tpu_custom_call" | custom-call | tf_op jit(solution)/shard_map/mix/pallas_call | solution.py:197
  (1 shorter events, 0.0 us)
Async XLA Ops:
  30.5 19.2 %all-to-all-start.1 = ((bf16[8,192,128]{2,1,0:T(8,128)(2,1)}), bf16[8,192,128]{2,1,0:T(8,128)(2,1)S(1)}, u32[]{:S(2)}, u32[]{:S(2)}) async-start(bf16[8,192,128]{2,1,0:T(8,128)(2,1)} %get-tuple-element.10), calls=%async_computation.1 | async-start | bytes 786432 | tf_op jit(solution)/shard_map/all_to_all | solution.py:147
  93.0 0.7 copy-start

commit v10 on v8

--- a/solution.py
+++ b/solution.py
@@ -8,13 +8,13 @@
 HEAD_DIM = 128
 LOG2E = 1.4426950408889634
 SCALE = HEAD_DIM ** -0.5
-HEAD_AXES = ("zl", "c", "tp")
+HEAD_AXES = ("zl", "tp")
 QUERY_AXES = ("y",)
-KEY_AXES = ("x",)
+KEY_AXES = ("x", "c")
 STATS = 2
 STAT_LANES = 8
 STAT_ROWS = 16
-GROUP_STEP = 2
+GROUP_STEP = 4
 KERNEL_VMEM = 16 * 1024 * 1024
 MIX_VMEM = 50 * 1024 * 1024
 IN_VMEM = pl.BlockSpec(memory_space=pltpu.VMEM)
@@ -62,42 +62,52 @@
 
 def split_kernel(local_ref, query_ref, key_value_ref):
     slots = local_ref.shape[0]
-    rows = local_ref.shape[1] // 3
-    query = local_ref[:, pl.ds(0, rows)].reshape(slots * rows, HEAD_DIM)
-    for copy in range(query_ref.shape[0]):
-        query_ref[copy] = query
-    for place in range(2):
-        block = local_ref[:, pl.ds((place + 1) * rows, rows)]
-        key_value_ref[place] = block.reshape(slots * rows, HEAD_DIM)
+    heads, tokens = key_value_ref.shape[1:3]
+    rows = tokens // slots
+    for head in range(heads):
+        for place in range(3):
+            span = pl.ds((head * 3 + place) * rows, rows)
+            block = local_ref[:, span].reshape(tokens, HEAD_DIM)
+            if place:
+                key_value_ref[place - 1, head] = block
+                continue
+            for copy in range(query_ref.shape[0]):
+                query_ref[copy, head] = block
 
 
 def attend_kernel(q_ref, key_value_ref, out_ref):
-    groups, tokens, width = q_ref.shape
+    groups, heads, tokens, width = q_ref.shape
     count = key_value_ref.shape[0] * tokens
-    key = key_value_ref[:, 0].reshape(count, width)
-    value = key_value_ref[:, 1].reshape(count, width)
-    columns = []
-    for group in range(0, groups, GROUP_STEP):
-        query = q_ref[pl.ds(group, GROUP_STEP)].reshape(GROUP_STEP * tokens, width)
-        score = lax.dot_general(
-            query, key, (((1,), (1,)), ((), ())), preferred_element_type=jnp.float32
-        )
-        highest = jnp.max(score, axis=1, keepdims=True)
-        expd = jnp.exp2((score - highest) * (SCALE * LOG2E))
-        total = jnp.sum(expd, axis=1, keepdims=True)
-        summed = jnp.dot(expd.astype(jnp.bfloat16), value, preferred_element_type=jnp.float32)
-        for step in range(GROUP_STEP):
-            rows = slice(step * tokens, (step + 1) * tokens)
-            out_ref[group + step, pl.ds(0, tokens)] = summed[rows].astype(jnp.bfloat16)
-            columns.append((highest[rows], total[rows]))
+    columns = [[None] * heads for _ in range(groups)]
+    for head in range(heads):
+        key = key_value_ref[:, 0, head].reshape(count, width)
+        value = key_value_ref[:, 1, head].reshape(count, width)
+        for group in range(0, groups, GROUP_STEP):
+            query = q_ref[pl.ds(group, GROUP_STEP), head].reshape(GROUP_STEP * tokens, width)
+            score = lax.dot_general(
+                query, key, (((1,), (1,)), ((), ())), preferred_element_type=jnp.float32
+            )
+            highest = jnp.max(score, axis=1, keepdims=True)
+            expd = jnp.exp2((score - highest) * (SCALE * LOG2E))
+            total = jnp.sum(expd, axis=1, keepdims=True)
+            summed = jnp.dot(expd.astype(jnp.bfloat16), value, preferred_element_type=jnp.float32)
+            for step in range(GROUP_STEP):
+                rows = slice(step * tokens, (step + 1) * tokens)
+                out_ref[group + step, pl.ds(head * tokens, tokens)] = summed[rows].astype(
+                    jnp.bfloat16
+                )
+                columns[group + step][head] = (highest[rows], total[rows])
+    columns = [
+        [jnp.concatenate(values, axis=0) for values in zip(*by_head)] for by_head in columns
+    ]
     for group, packed in enumerate(pack_stats(columns)):
-        out_ref[group, pl.ds(tokens, STAT_ROWS)] = packed
+        out_ref[group, pl.ds(heads * tokens, STAT_ROWS)] = packed
 
 
 def combine_kernel(part_ref, out_ref):
     groups = part_ref.shape[0]
     tokens = part_ref.shape[1] - STAT_ROWS
-    copies, rows, _ = out_ref.shape
+    slots, heads, rows, _ = out_ref.shape
     stats = unpack_stats(part_ref[:, pl.ds(tokens, STAT_ROWS)], tokens)
     lane = lax.broadcasted_iota(jnp.int32, stats.shape, 1)
     is_maximum = (lane % STAT_LANES == 0) & (lane < groups * STAT_LANES)
@@ -111,13 +121,15 @@
         part = part_ref[group, pl.ds(0, tokens)].astype(jnp.float32)
         summed += part * weight[:, at : at + 1]
     attended = (summed / total).astype(jnp.bfloat16)
-    repeats = copies * rows // tokens
-    for block in range(tokens // rows):
-        for repeat in range(repeats):
-            out_ref[block * repeats + repeat] = attended[block * rows : (block + 1) * rows]
+    blocks = tokens // heads // rows
+    for slot in range(slots):
+        for head in range(heads):
+            start = (head * blocks + slot * blocks // slots) * rows
+            out_ref[slot, head] = attended[start : start + rows]
 
 
 def mix_kernel(attended_ref, gate_ref, weight_ref, out_ref, held_ref, semaphores):
+    held = attended_ref.shape[1]
     heads = weight_ref.shape[0] // HEAD_DIM
     pieces = semaphores.shape[0]
     span = heads // pieces
@@ -131,7 +143,8 @@
     for piece, copy in enumerate(copies):
         first = piece * span
         block = jnp.concatenate(
-            [attended_ref[head] for head in range(first, first + span)], axis=1
+            [attended_ref[head // held, head % held] for head in range(first, first + span)],
+            axis=1,
         )
         copy.wait()
         product += jnp.dot(
@@ -150,16 +163,20 @@
     slots = lax.axis_size(HEAD_AXES)
     rows, width = queries.shape
     heads = width // HEAD_DIM
+    held = -(-heads // slots)
     tokens = slots * rows
     own_tokens = lax.axis_size("tp") * rows
     stacked = jnp.stack([queries, keys, vals], axis=0).reshape(3, rows, heads, HEAD_DIM)
     stacked = stacked.transpose(2, 0, 1, 3).reshape(heads, 3 * rows, HEAD_DIM)
-    stacked = jnp.pad(stacked, ((0, slots - heads), (0, 0), (0, 0)))
+    stacked = jnp.pad(stacked, ((0, slots * held - heads), (0, 0), (0, 0)))
+    stacked = stacked.reshape(slots, held * 3 * rows, HEAD_DIM)
     query_copies, own_key_value = pl.pallas_call(
         split_kernel,
         out_shape=[
-            jax.ShapeDtypeStruct((lax.axis_size(QUERY_AXES), tokens, HEAD_DIM), jnp.bfloat16),
-            jax.ShapeDtypeStruct((2, tokens, HEAD_DIM), jnp.bfloat16),
+            jax.ShapeDtypeStruct(
+                (lax.axis_size(QUERY_AXES), held, tokens, HEAD_DIM), jnp.bfloat16
+            ),
+            jax.ShapeDtypeStruct((2, held, tokens, HEAD_DIM), jnp.bfloat16),
         ],
         in_specs=[IN_VMEM],
         out_specs=[IN_VMEM] * 2,
@@ -172,7 +189,7 @@
     partial = pl.pallas_call(
         attend_kernel,
         out_shape=jax.ShapeDtypeStruct(
-            (group.shape[0], tokens + STAT_ROWS, HEAD_DIM), jnp.bfloat16
+            (group.shape[0], held * tokens + STAT_ROWS, HEAD_DIM), jnp.bfloat16
         ),
         in_specs=[IN_VMEM] * 2,
         out_specs=IN_VMEM,
@@ -182,7 +199,7 @@
     partial = exchange(partial, QUERY_AXES)
     attended = pl.pallas_call(
         combine_kernel,
-        out_shape=jax.ShapeDtypeStruct((slots, own_tokens, HEAD_DIM), jnp.bfloat16),
+        out_shape=jax.ShapeDtypeStruct((slots, held, own_tokens, HEAD_DIM), jnp.bfloat16),
         in_specs=[IN_VMEM],
         out_specs=IN_VMEM,
         compiler_params=pltpu.CompilerParams(vmem_limit_bytes=KERNEL_VMEM),

time: 96.6 us -> 100 us (1.035)
  Pallas kernels: 7.52 us -> 9.98 us
  blocking collectives: 78.1 us -> 80.4 us
  waiting for transfers between devices: 2.14 us -> 0.01 us
    all_gather x1, blocking collectives: 10.3 us -> 17.2 us  [on_device(): key_value = lax.all_gather(own_key_value, KEY_AXES, axis=0, tiled=False)]
    all_to_all x3, blocking collectives: 67.9 us -> 63.2 us  [exchange(): return lax.all_to_all(blocks, axes, split_axis=0, concat_axis=0, tiled=True)]
    pallas_call x1, Pallas kernels: 1.92 us -> 4.37 us  [on_device(): pl.pallas_call(attend_kernel, out_shape=jax.ShapeDtypeStruct((group.shape...]
    all_to_all x1, waiting for transfers between devices: 2.14 us -> 0.01 us  [exchange(): return lax.all_to_all(blocks, axes, split_axis=0, concat_axis=0, tiled=True)]
  transfers between devices with their start and end apart: 1 -> 1, of which waited for: 1 -> 0; matrix products, arithmetic and copies ran while one was open for 0% -> 0% of each run, Pallas kernels for 0% -> 0%
where the time goes in v10:
time: 100 us; the launch traced here: 98.8 us
  blocking collectives  80.4 us (80%)
  Pallas kernels  9.98 us (10%)
  starting transfers between devices  6.82 us (7%)
    all_to_all x3, blocking collectives, exchange(): return lax.all_to_all(blocks, axes, split_axis=0, concat_axis=0, tiled=True)  63.2 us
    all_gather x1, blocking collectives, on_device(): key_value = lax.all_gather(own_key_value, KEY_AXES, axis=0, tiled=False)  17.2 us
    all_to_all x1, starting transfers between devices, exchange(): return lax.all_to_all(blocks, axes, split_axis=0, concat_axis=0, tiled=True)  6.82 us
    pallas_call x1, Pallas kernels, on_device(): pl.pallas_call(attend_kernel, out_shape=jax.ShapeDtypeStruct((group.shape...  4.37 us
    pallas_call x1, Pallas kernels, on_device(): pl.pallas_call(mix_kernel, out_shape=jax.ShapeDtypeStruct((own_tokens, ou...  3.82 us
  transfers between devices with their start and end apart: 1, of which 0 were waited for; matrix products, arithmetic and copies ran while one was open for 0% of the time, Pallas kernels for 0%

profile of v10, /device:TPU:1, one launch (start us, length us, event | category | flops | bytes accessed | tf_op | source)
XLA Modules:
  0.0 98.8 jit_solution(13174820454168001236)
XLA Ops:
  0.0 0.8 copy_bitcast_fusion
  0.9 25.5 %all_to_all.20.local_ref = bf16[12,48,128]{2,1,0:T(8,128)(2,1)S(1)} all-to-all(bf16[12,48,128]{2,1,0:T(8,128)(2,1)S(1)} %bitcast.11), channel_id=1, replica_groups=mesh['zl'=3,'y'=8,'x'=4,'c'=2,'tp'=4] {'zl','tp'}, dimensions={0} | all-to-all | bytes 294912 | tf_op jit(solution)/shard_map/all_to_all | solution.py:159
  26.4 0.8 split.1
  27.2 6.8 %all-to-all-start.1 = ((bf16[8,2,96,128]{3,2,1,0:T(8,128)(2,1)}), bf16[8,2,96,128]{3,2,1,0:T(8,128)(2,1)S(1)}, u32[]{:S(2)}, u32[]{:S(2)}) async-start(bf16[8,2,96,128]{3,2,1,0:T(8,128)(2,1)} %get-tuple-element.10), calls=%async_computation.1 | async-start | bytes 786432 | tf_op jit(solution)/shard_map/all_to_all | solution.py:159
  34.0 17.2 %all-gather = bf16[16,2,96,128]{3,2,1,0:T(8,128)(2,1)S(1)} all-gather(bf16[2,2,96,128]{3,2,1,0:T(8,128)(2,1)S(1)} %get-tuple-element.9), channel_id=2, replica_groups=mesh['zl'=3,'y'=8,'x'=4,'c'=2,'tp'=4] {'x','c'}, dimensions={0}, use_global_device_ids=true | all-gather | bytes 884736 | tf_op jit(solution)/shard_map/all_gather | solution.py:187
  51.3 0.0 all-to-all-done.1.q_ref
  51.3 4.4 %attend.1 = bf16[8,208,128]{2,1,0:T(8,128)(2,1)S(1)} custom-call(bf16[8,2,96,128]{3,2,1,0:T(8,128)(2,1)S(1)} %all-to-all-done.1.q_ref, bf16[8,2,2,96,128]{4,3,2,1,0:T(8,128)(2,1)S(1)} %bitcast.10), custom_call_target="tpu_custom_call" | custom-call | tf_op jit(solution)/shard_map/attend/pallas_call | solution.py:189
  55.7 22.5 %all_to_all.21.part_ref = bf16[8,208,128]{2,1,0:T(8,128)(2,1)S(1)} all-to-all(bf16[8,208,128]{2,1,0:T(8,128)(2,1)S(1)} %attend.1), channel_id=1, replica_groups=mesh['zl'=3,'y'=8,'x'=4,'c'=2,'tp'=4] {'y'}, dimensions={0} | all-to-all | bytes 851968 | tf_op jit(solution)/shard_map/all_to_all | solution.py:159
  78.2 1.0 combine.1
  79.1 15.2 %all_to_all.22.attended_ref = bf16[12,2,32,128]{3,2,1,0:T(8,128)(2,1)S(1)} all-to-all(bf16[12,2,32,128]{3,2,1,0:T(8,128)(2,1)S(1)} %combine.1), channel_id=1, replica_groups=mesh['zl'=3,'y'=8,'x'=4,'c'=2,'tp'=4] {'zl','tp'}, dimensions={0} | all-to-all | bytes 393216 | tf_op jit(solution)/shard_map/all_to_all | solution.py:159
  94.3 0.0 copy-start
  94.3 0.7 copy-done
  95.0 3.8 %mix.1 = bf16[32,1280]{1,0:T(8,128)(2,1)} custom-call(bf16[12,2,32,128]{3,2,1,0:T(8,128)(2,1)S(1)} %all_to_all.22.attended_ref, f32[1280]{0:T(1024)S(1)} %copy-done, bf16[2560,1280]{1,0:T(8,128)(2,1)} %weight_ref.1), custom_call_target="tpu_custom_call" | custom-call | tf_op jit(solution)/shard_map/mix/pallas_call | solution.py:209
  (1 shorter events, 0.0 us)
Async XLA Ops:
  27.2 24.1 %all-to-all-start.1 = ((bf16[8,2,96,128]{3,2,1,0:T(8,128)(2,1)}), bf16[8,2,96,128]{3,2,1,0:T(8,128)(2,1)S(1)}, u32[]{:S(2)}, u32[]{:S(2)}) async-start(bf16[8,2,96,128]{3,2,1,0:T(8,128)(2,1)} %get-tuple-element.10), calls=%async_computation.1 | async-start | bytes 786432 | tf_op jit(solution)/shard_map/all_to_all | solution.py:159
  94.3 0.7 copy-start

commit v11 on v8

--- a/solution.py
+++ b/solution.py
@@ -15,6 +15,7 @@
 STAT_LANES = 8
 STAT_ROWS = 16
 GROUP_STEP = 2
+EARLY_HEADS = 10
 KERNEL_VMEM = 16 * 1024 * 1024
 MIX_VMEM = 50 * 1024 * 1024
 IN_VMEM = pl.BlockSpec(memory_space=pltpu.VMEM)
@@ -117,29 +118,44 @@
             out_ref[block * repeats + repeat] = attended[block * rows : (block + 1) * rows]
 
 
-def mix_kernel(attended_ref, gate_ref, weight_ref, out_ref, held_ref, semaphores):
-    heads = weight_ref.shape[0] // HEAD_DIM
-    pieces = semaphores.shape[0]
-    span = heads // pieces
+def load_rows(weight_ref, held_ref, semaphores, first):
+    rows = held_ref.shape[0] // semaphores.shape[0]
     copies = []
-    for piece in range(pieces):
-        rows = pl.ds(piece * span * HEAD_DIM, span * HEAD_DIM)
-        copy = pltpu.make_async_copy(weight_ref.at[rows], held_ref.at[rows], semaphores.at[piece])
+    for piece in range(semaphores.shape[0]):
+        copy = pltpu.make_async_copy(
+            weight_ref.at[pl.ds(first + piece * rows, rows)],
+            held_ref.at[pl.ds(piece * rows, rows)],
+            semaphores.at[piece],
+        )
         copy.start()
         copies.append(copy)
-    product = jnp.zeros(out_ref.shape, jnp.float32)
+    return copies
+
+
+def fetch_kernel(weight_ref, gate_ref, held_ref, row_ref, semaphores):
+    copies = load_rows(weight_ref, held_ref, semaphores, 0)
+    row_ref[...] = gate_ref[...][None, :]
+    for copy in copies:
+        copy.wait()
+
+
+def mix_kernel(attended_ref, row_ref, first_ref, weight_ref, out_ref, held_ref, semaphores):
+    early = first_ref.shape[0] // HEAD_DIM
+    copies = load_rows(weight_ref, held_ref, semaphores, first_ref.shape[0])
+    span = held_ref.shape[0] // HEAD_DIM // len(copies)
+
+    def product_of(first, count, rows):
+        block = jnp.concatenate(
+            [attended_ref[head] for head in range(first, first + count)], axis=1
+        )
+        return jnp.dot(block, rows, preferred_element_type=jnp.float32)
+
+    product = product_of(0, early, first_ref[...])
     for piece, copy in enumerate(copies):
-        first = piece * span
-        block = jnp.concatenate(
-            [attended_ref[head] for head in range(first, first + span)], axis=1
-        )
         copy.wait()
-        product += jnp.dot(
-            block,
-            held_ref[pl.ds(first * HEAD_DIM, span * HEAD_DIM)],
-            preferred_element_type=jnp.float32,
-        )
-    out_ref[...] = (product * gate_ref[...][None, :]).astype(jnp.bfloat16)
+        rows = held_ref[pl.ds(piece * span * HEAD_DIM, span * HEAD_DIM)]
+        product += product_of(early + piece * span, span, rows)
+    out_ref[...] = (product * row_ref[...]).astype(jnp.bfloat16)
 
 
 def exchange(blocks, axes):
@@ -188,19 +204,39 @@
         compiler_params=pltpu.CompilerParams(vmem_limit_bytes=KERNEL_VMEM),
         name="combine",
     )(partial)
+    channels = out_weight.shape[1]
+    attended, weight = lax.optimization_barrier((attended, out_weight))
+    in_hbm = pl.BlockSpec(memory_space=pltpu.HBM)
+    first, row = pl.pallas_call(
+        fetch_kernel,
+        out_shape=[
+            jax.ShapeDtypeStruct((EARLY_HEADS * HEAD_DIM, channels), weight.dtype),
+            jax.ShapeDtypeStruct((1, channels), gate.dtype),
+        ],
+        in_specs=[in_hbm, IN_VMEM],
+        out_specs=[IN_VMEM] * 2,
+        scratch_shapes=[pltpu.SemaphoreType.DMA((EARLY_HEADS // 2,))],
+        compiler_params=pltpu.CompilerParams(vmem_limit_bytes=MIX_VMEM),
+        cost_estimate=pl.CostEstimate(
+            flops=0, bytes_accessed=4 * EARLY_HEADS * HEAD_DIM * channels, transcendentals=0
+        ),
+        name="fetch",
+    )(weight, gate)
     attended = exchange(attended, HEAD_AXES)
+    attended, first, row = lax.optimization_barrier((attended, first, row))
+    late = heads - EARLY_HEADS
     return pl.pallas_call(
         mix_kernel,
-        out_shape=jax.ShapeDtypeStruct((own_tokens, out_weight.shape[1]), jnp.bfloat16),
-        in_specs=[IN_VMEM, IN_VMEM, pl.BlockSpec(memory_space=pltpu.HBM)],
+        out_shape=jax.ShapeDtypeStruct((own_tokens, channels), jnp.bfloat16),
+        in_specs=[IN_VMEM, IN_VMEM, IN_VMEM, in_hbm],
         out_specs=IN_VMEM,
         scratch_shapes=[
-            pltpu.VMEM(out_weight.shape, out_weight.dtype),
-            pltpu.SemaphoreType.DMA((heads // 2,)),
+            pltpu.VMEM((late * HEAD_DIM, channels), out_weight.dtype),
+            pltpu.SemaphoreType.DMA((late // 2,)),
         ],
         compiler_params=pltpu.CompilerParams(vmem_limit_bytes=MIX_VMEM),
         name="mix",
-    )(attended, gate, out_weight)
+    )(attended, row, first, weight)
 
 
 def solution(mesh):

time: 96.6 us -> 96.1 us (level)
  blocking collectives: 78.1 us -> 54.9 us
  waiting for transfers between devices: 2.14 us -> 13.4 us
  starting transfers between devices: 6.82 us -> 16.4 us
  Pallas kernels: 7.52 us -> 9.38 us
    all_to_all x3 -> x2, blocking collectives: 67.9 us -> 44.6 us  [exchange(): return lax.all_to_all(blocks, axes, split_axis=0, concat_axis=0, tiled=True)]
    all_to_all x1 -> x2, waiting for transfers between devices: 2.14 us -> 13.4 us  [exchange(): return lax.all_to_all(blocks, axes, split_axis=0, concat_axis=0, tiled=True)]
    all_to_all x1 -> x2, starting transfers between devices: 6.82 us -> 16.4 us  [exchange(): return lax.all_to_all(blocks, axes, split_axis=0, concat_axis=0, tiled=True)]
    pallas_call x1 -> x2, Pallas kernels: 3.82 us -> 5 us  [the longest x1 3.08 us: on_device(): pl.pallas_call(mix_kernel, out_shape=jax.ShapeDtypeStruct((own_tokens, ch...]
  transfers between devices with their start and end apart: 1 -> 2, of which waited for: 1 -> 2; matrix products, arithmetic and copies ran while one was open for 0% -> 0% of each run, Pallas kernels for 0% -> 2%
where the time goes in v11:
time: 96.1 us; the launch traced here: 95.7 us
  blocking collectives  54.9 us (57%)
  starting transfers between devices  16.4 us (17%)
  waiting for transfers between devices  13.4 us (14%)
  Pallas kernels  9.38 us (10%)
    all_to_all x2, blocking collectives, exchange(): return lax.all_to_all(blocks, axes, split_axis=0, concat_axis=0, tiled=True)  44.6 us
    all_to_all x2, starting transfers between devices, exchange(): return lax.all_to_all(blocks, axes, split_axis=0, concat_axis=0, tiled=True)  16.4 us
    all_to_all x2, waiting for transfers between devices, exchange(): return lax.all_to_all(blocks, axes, split_axis=0, concat_axis=0, tiled=True)  13.4 us
    all_gather x1, blocking collectives, on_device(): key_value = lax.all_gather(own_key_value, KEY_AXES, axis=0, tiled=False)  10.3 us
    pallas_call x1, Pallas kernels, on_device(): pl.pallas_call(mix_kernel, out_shape=jax.ShapeDtypeStruct((own_tokens, ch...  3.08 us
  transfers between devices with their start and end apart: 2, of which 2 were waited for; matrix products, arithmetic and copies ran while one was open for 0% of the time, Pallas kernels for 2%

profile of v11, /device:TPU:1, one launch (start us, length us, event | category | flops | bytes accessed | tf_op | source)
XLA Modules:
  0.0 95.7 jit_solution(1205847978356882567)
XLA Ops:
  0.0 0.8 maximum_bitcast_fusion
  0.9 28.8 %all_to_all.20.local_ref = bf16[24,24,128]{2,1,0:T(8,128)(2,1)S(1)} all-to-all(bf16[24,24,128]{2,1,0:T(8,128)(2,1)S(1)} %pad.4), channel_id=1, replica_groups=mesh['zl'=3,'y'=8,'x'=4,'c'=2,'tp'=4] {'zl','c','tp'}, dimensions={0} | all-to-all | bytes 294912 | tf_op jit(solution)/shard_map/all_to_all | solution.py:162
  29.7 0.8 split.1
  30.5 6.8 %all-to-all-start.1 = ((bf16[8,192,128]{2,1,0:T(8,128)(2,1)}), bf16[8,192,128]{2,1,0:T(8,128)(2,1)S(1)}, u32[]{:S(2)}, u32[]{:S(2)}) async-start(bf16[8,192,128]{2,1,0:T(8,128)(2,1)} %get-tuple-element.17), calls=%async_computation.1 | async-start | bytes 786432 | tf_op jit(solution)/shard_map/all_to_all | solution.py:162
  37.3 10.3 %all-gather = bf16[8,192,128]{2,1,0:T(8,128)(2,1)S(1)} all-gather(bf16[2,192,128]{2,1,0:T(8,128)(2,1)S(1)} %get-tuple-element.16), channel_id=2, replica_groups=mesh['zl'=3,'y'=8,'x'=4,'c'=2,'tp'=4] {'x'}, dimensions={0}, use_global_device_ids=true | all-gather | bytes 491520 | tf_op jit(solution)/shard_map/all_gather | solution.py:186
  47.6 2.1 %all-to-all-done.1.q_ref = bf16[8,192,128]{2,1,0:T(8,128)(2,1)S(1)} async-done(((bf16[8,192,128]{2,1,0:T(8,128)(2,1)}), bf16[8,192,128]{2,1,0:T(8,128)(2,1)S(1)}, u32[]{:S(2)}, u32[]{:S(2)}) %all-to-all-start.1) | async-done | bytes 393248 | tf_op jit(solution)/shard_map/all_to_all | solution.py:162
  49.7 1.9 %attend.1 = bf16[8,208,128]{2,1,0:T(8,128)(2,1)S(1)} custom-call(bf16[8,192,128]{2,1,0:T(8,128)(2,1)S(1)} %all-to-all-done.1.q_ref, bf16[4,2,192,128]{3,2,1,0:T(8,128)(2,1)S(1)} %bitcast.14), custom_call_target="tpu_custom_call" | custom-call | tf_op jit(solution)/shard_map/attend/pallas_call | solution.py:188
  51.7 15.8 %all_to_all.21.part_ref = bf16[8,208,128]{2,1,0:T(8,128)(2,1)S(1)} all-to-all(bf16[8,208,128]{2,1,0:T(8,128)(2,1)S(1)} %attend.1), channel_id=1, replica_groups=mesh['zl'=3,'y'=8,'x'=4,'c'=2,'tp'=4] {'y'}, dimensions={0} | all-to-all | bytes 851968 | tf_op jit(solution)/shard_map/all_to_all | solution.py:162
  67.4 1.6 %combine.1 = bf16[24,32,128]{2,1,0:T(8,128)(2,1)} custom-call(bf16[8,208,128]{2,1,0:T(8,128)(2,1)S(1)} %all_to_all.21.part_ref), custom_call_target="tpu_custom_call" | custom-call | tf_op jit(solution)/shard_map/combine/pallas_call | solution.py:199
  69.1 9.6 %all-to-all-start.3 = ((bf16[24,32,128]{2,1,0:T(8,128)(2,1)}), bf16[24,32,128]{2,1,0:T(8,128)(2,1)S(1)}, u32[]{:S(2)}, u32[]{:S(2)}) async-start(bf16[24,32,128]{2,1,0:T(8,128)(2,1)} %combine.1), calls=%async_computation.3 | async-start | bytes 393216 | tf_op jit(solution)/shard_map/all_to_all | solution.py:162
  78.7 0.0 copy-start
  78.7 0.7 copy-done
  79.4 1.9 %fetch.1 = (bf16[1280,1280]{1,0:T(8,128)(2,1)S(1)}, f32[1,1280]{1,0:T(1,128)S(1)}) custom-call(bf16[2560,1280]{1,0:T(8,128)(2,1)} %weight_ref.1, f32[1280]{0:T(1024)S(1)} %copy-done), custom_call_target="tpu_custom_call" | custom-call | bytes 6553600 | tf_op jit(solution)/shard_map/fetch/pallas_call | solution.py:210
  81.3 11.2 %all-to-all-done.3.attended_ref = bf16[24,32,128]{2,1,0:T(8,128)(2,1)S(1)} async-done(((bf16[24,32,128]{2,1,0:T(8,128)(2,1)}), bf16[24,32,128]{2,1,0:T(8,128)(2,1)S(1)}, u32[]{:S(2)}, u32[]{:S(2)}) %all-to-all-start.3) | async-done | bytes 196640 | tf_op jit(solution)/shard_map/all_to_all | solution.py:162
  92.6 3.1 %mix.1 = bf16[32,1280]{1,0:T(8,128)(2,1)} custom-call(bf16[24,32,128]{2,1,0:T(8,128)(2,1)S(1)} %all-to-all-done.3.attended_ref, f32[1,1280]{1,0:T(1,128)S(1)} %get-tuple-element.25.row_ref, bf16[1280,1280]{1,0:T(8,128)(2,1)S(1)} %get-tuple-element.26.first_ref, bf16[2560,1280]{1,0:T(8,128)(2,1)} %weight_ref.1), custom_call_target="tpu_custom_call" | custom-call | tf_op jit(solution)/shard_map/mix/pallas_call | solution.py:228
  (1 shorter events, 0.0 us)
Async XLA Ops:
  30.5 19.2 %all-to-all-start.1 = ((bf16[8,192,128]{2,1,0:T(8,128)(2,1)}), bf16[8,192,128]{2,1,0:T(8,128)(2,1)S(1)}, u32[]{:S(2)}, u32[]{:S(2)}) async-start(bf16[8,192,128]{2,1,0:T(8,128)(2,1)} %get-tuple-element.17), calls=%async_computation.1 | async-start | bytes 786432 | tf_op jit(solution)/shard_map/all_to_all | solution.py:162
  69.1 23.5 %all-to-all-start.3 = ((bf16[24,32,128]{2,1,0:T(8,128)(2,1)}), bf16[24,32,128]{2,1,0:T(8,128)(2,1)S(1)}, u32[]{:S(2)}, u32[]{:S(2)}) async-start(bf16[24,32,128]{2,1,0:T(8,128)(2,1)} %combine.1), calls=%async_computation.3 | async-start | bytes 393216 | tf_op jit(solution)/shard_map/all_to_all | solution.py:162
  78.7 0.7 copy-start

commit v12 on v11

--- a/solution.py
+++ b/solution.py
@@ -9,12 +9,12 @@
 LOG2E = 1.4426950408889634
 SCALE = HEAD_DIM ** -0.5
 HEAD_AXES = ("zl", "c", "tp")
-QUERY_AXES = ("y",)
-KEY_AXES = ("x",)
+QUERY_AXES = ("x",)
+KEY_AXES = ("y",)
 STATS = 2
 STAT_LANES = 8
 STAT_ROWS = 16
-GROUP_STEP = 2
+GROUP_STEP = 1
 EARLY_HEADS = 10
 KERNEL_VMEM = 16 * 1024 * 1024
 MIX_VMEM = 50 * 1024 * 1024
@@ -64,12 +64,11 @@
 def split_kernel(local_ref, query_ref, key_value_ref):
     slots = local_ref.shape[0]
     rows = local_ref.shape[1] // 3
-    query = local_ref[:, pl.ds(0, rows)].reshape(slots * rows, HEAD_DIM)
-    for copy in range(query_ref.shape[0]):
-        query_ref[copy] = query
+    query_ref[...] = local_ref[:, pl.ds(0, rows)].reshape(slots * rows, HEAD_DIM)
     for place in range(2):
-        block = local_ref[:, pl.ds((place + 1) * rows, rows)]
-        key_value_ref[place] = block.reshape(slots * rows, HEAD_DIM)
+        block = local_ref[:, pl.ds((place + 1) * rows, rows)].reshape(slots * rows, HEAD_DIM)
+        for copy in range(key_value_ref.shape[0]):
+            key_value_ref[copy, place] = block
 
 
 def attend_kernel(q_ref, key_value_ref, out_ref):
@@ -171,19 +170,19 @@
     stacked = jnp.stack([queries, keys, vals], axis=0).reshape(3, rows, heads, HEAD_DIM)
     stacked = stacked.transpose(2, 0, 1, 3).reshape(heads, 3 * rows, HEAD_DIM)
     stacked = jnp.pad(stacked, ((0, slots - heads), (0, 0), (0, 0)))
-    query_copies, own_key_value = pl.pallas_call(
+    own_query, key_value_copies = pl.pallas_call(
         split_kernel,
         out_shape=[
-            jax.ShapeDtypeStruct((lax.axis_size(QUERY_AXES), tokens, HEAD_DIM), jnp.bfloat16),
-            jax.ShapeDtypeStruct((2, tokens, HEAD_DIM), jnp.bfloat16),
+            jax.ShapeDtypeStruct((tokens, HEAD_DIM), jnp.bfloat16),
+            jax.ShapeDtypeStruct((lax.axis_size(KEY_AXES), 2, tokens, HEAD_DIM), jnp.bfloat16),
         ],
         in_specs=[IN_VMEM],
         out_specs=[IN_VMEM] * 2,
         compiler_params=pltpu.CompilerParams(vmem_limit_bytes=KERNEL_VMEM),
         name="split",
     )(exchange(stacked, HEAD_AXES))
-    group = exchange(query_copies, QUERY_AXES)
-    key_value = lax.all_gather(own_key_value, KEY_AXES, axis=0, tiled=False)
+    key_value = exchange(key_value_copies, KEY_AXES)
+    group = lax.all_gather(own_query, QUERY_AXES, axis=0, tiled=False)
     key_value, group = lax.optimization_barrier((key_value, group))
     partial = pl.pallas_call(
         attend_kernel,

time: 96.1 us -> 96.9 us (level)
  waiting for transfers between devices: 13.4 us -> 23.8 us
  blocking collectives: 54.9 us -> 47.7 us
  starting transfers between devices: 16.4 us -> 13.5 us
    all_to_all x2, waiting for transfers between devices: 13.4 us -> 23.8 us  [exchange(): return lax.all_to_all(blocks, axes, split_axis=0, concat_axis=0, tiled=True)]
    all_to_all x2, blocking collectives: 44.6 us -> 37.9 us  [exchange(): return lax.all_to_all(blocks, axes, split_axis=0, concat_axis=0, tiled=True)]
    all_to_all x2, starting transfers between devices: 16.4 us -> 13.5 us  [exchange(): return lax.all_to_all(blocks, axes, split_axis=0, concat_axis=0, tiled=True)]
where the time goes in v12:
time: 96.9 us; the launch traced here: 96.5 us
  blocking collectives  47.7 us (49%)
  waiting for transfers between devices  23.8 us (25%)
  starting transfers between devices  13.5 us (14%)
  Pallas kernels  9.82 us (10%)
    all_to_all x2, blocking collectives, exchange(): return lax.all_to_all(blocks, axes, split_axis=0, concat_axis=0, tiled=True)  37.9 us
    all_to_all x2, waiting for transfers between devices, exchange(): return lax.all_to_all(blocks, axes, split_axis=0, concat_axis=0, tiled=True)  23.8 us
    all_to_all x2, starting transfers between devices, exchange(): return lax.all_to_all(blocks, axes, split_axis=0, concat_axis=0, tiled=True)  13.5 us
    all_gather x1, blocking collectives, on_device(): group = lax.all_gather(own_query, QUERY_AXES, axis=0, tiled=False)  9.87 us
    pallas_call x1, Pallas kernels, on_device(): pl.pallas_call(mix_kernel, out_shape=jax.ShapeDtypeStruct((own_tokens, ch...  3.08 us
    pallas_call x1, Pallas kernels, on_device(): pl.pallas_call(attend_kernel, out_shape=jax.ShapeDtypeStruct((group.shape...  2.28 us
  transfers between devices with their start and end apart: 2, of which 2 were waited for; matrix products, arithmetic and copies ran while one was open for 0% of the time, Pallas kernels for 2%

profile of v12, /device:TPU:1, one launch (start us, length us, event | category | flops | bytes accessed | tf_op | source)
XLA Modules:
  0.0 96.5 jit_solution(10640248587681810246)
XLA Ops:
  0.0 0.8 maximum_bitcast_fusion
  0.9 28.8 %all_to_all.20.local_ref = bf16[24,24,128]{2,1,0:T(8,128)(2,1)S(1)} all-to-all(bf16[24,24,128]{2,1,0:T(8,128)(2,1)S(1)} %pad.4), channel_id=1, replica_groups=mesh['zl'=3,'y'=8,'x'=4,'c'=2,'tp'=4] {'zl','c','tp'}, dimensions={0} | all-to-all | bytes 294912 | tf_op jit(solution)/shard_map/all_to_all | solution.py:161
  29.7 1.0 %split.1 = (bf16[192,128]{1,0:T(8,128)(2,1)S(1)}, bf16[8,2,192,128]{3,2,1,0:T(8,128)(2,1)}) custom-call(bf16[24,24,128]{2,1,0:T(8,128)(2,1)S(1)} %all_to_all.20.local_ref), custom_call_target="tpu_custom_call" | custom-call | tf_op jit(solution)/shard_map/split/pallas_call | solution.py:173
  30.7 6.8 %all-to-all-start.1 = ((bf16[8,2,192,128]{3,2,1,0:T(8,128)(2,1)}), bf16[8,2,192,128]{3,2,1,0:T(8,128)(2,1)S(1)}, u32[]{:S(2)}, u32[]{:S(2)}) async-start(bf16[8,2,192,128]{3,2,1,0:T(8,128)(2,1)} %get-tuple-element.16), calls=%async_computation.1 | async-start | bytes 1572864 | tf_op jit(solution)/shard_map/all_to_all | solution.py:161
  37.5 9.9 %all-gather = bf16[768,128]{1,0:T(8,128)(2,1)S(1)} all-gather(bf16[192,128]{1,0:T(8,128)(2,1)S(1)} %get-tuple-element.17), channel_id=2, replica_groups=mesh['zl'=3,'y'=8,'x'=4,'c'=2,'tp'=4] {'x'}, dimensions={0}, use_global_device_ids=true | all-gather | bytes 245760 | tf_op jit(solution)/shard_map/all_gather | solution.py:185
  47.4 12.5 %all-to-all-done.1.key_value_ref = bf16[8,2,192,128]{3,2,1,0:T(8,128)(2,1)S(1)} async-done(((bf16[8,2,192,128]{3,2,1,0:T(8,128)(2,1)}), bf16[8,2,192,128]{3,2,1,0:T(8,128)(2,1)S(1)}, u32[]{:S(2)}, u32[]{:S(2)}) %all-to-all-start.1) | async-done | bytes 786464 | tf_op jit(solution)/shard_map/all_to_all | solution.py:161
  59.9 2.3 %attend.1 = bf16[4,208,128]{2,1,0:T(8,128)(2,1)S(1)} custom-call(bf16[4,192,128]{2,1,0:T(8,128)(2,1)S(1)} %bitcast.14, bf16[8,2,192,128]{3,2,1,0:T(8,128)(2,1)S(1)} %all-to-all-done.1.key_value_ref), custom_call_target="tpu_custom_call" | custom-call | tf_op jit(solution)/shard_map/attend/pallas_call | solution.py:187
  62.2 9.1 %all_to_all.21.part_ref = bf16[4,208,128]{2,1,0:T(8,128)(2,1)S(1)} all-to-all(bf16[4,208,128]{2,1,0:T(8,128)(2,1)S(1)} %attend.1), channel_id=1, replica_groups=mesh['zl'=3,'y'=8,'x'=4,'c'=2,'tp'=4] {'x'}, dimensions={0} | all-to-all | bytes 425984 | tf_op jit(solution)/shard_map/all_to_all | solution.py:161
  71.3 1.5 %combine.1 = bf16[24,32,128]{2,1,0:T(8,128)(2,1)} custom-call(bf16[4,208,128]{2,1,0:T(8,128)(2,1)S(1)} %all_to_all.21.part_ref), custom_call_target="tpu_custom_call" | custom-call | tf_op jit(solution)/shard_map/combine/pallas_call | solution.py:198
  72.8 6.7 %all-to-all-start.3 = ((bf16[24,32,128]{2,1,0:T(8,128)(2,1)}), bf16[24,32,128]{2,1,0:T(8,128)(2,1)S(1)}, u32[]{:S(2)}, u32[]{:S(2)}) async-start(bf16[24,32,128]{2,1,0:T(8,128)(2,1)} %combine.1), calls=%async_computation.3 | async-start | bytes 393216 | tf_op jit(solution)/shard_map/all_to_all | solution.py:161
  79.5 0.0 copy-start
  79.5 0.7 copy-done
  80.2 1.9 %fetch.1 = (bf16[1280,1280]{1,0:T(8,128)(2,1)S(1)}, f32[1,1280]{1,0:T(1,128)S(1)}) custom-call(bf16[2560,1280]{1,0:T(8,128)(2,1)} %weight_ref.1, f32[1280]{0:T(1024)S(1)} %copy-done), custom_call_target="tpu_custom_call" | custom-call | bytes 6553600 | tf_op jit(solution)/shard_map/fetch/pallas_call | solution.py:209
  82.1 11.3 %all-to-all-done.3.attended_ref = bf16[24,32,128]{2,1,0:T(8,128)(2,1)S(1)} async-done(((bf16[24,32,128]{2,1,0:T(8,128)(2,1)}), bf16[24,32,128]{2,1,0:T(8,128)(2,1)S(1)}, u32[]{:S(2)}, u32[]{:S(2)}) %all-to-all-start.3) | async-done | bytes 196640 | tf_op jit(solution)/shard_map/all_to_all | solution.py:161
  93.4 3.1 %mix.1 = bf16[32,1280]{1,0:T(8,128)(2,1)} custom-call(bf16[24,32,128]{2,1,0:T(8,128)(2,1)S(1)} %all-to-all-done.3.attended_ref, f32[1,1280]{1,0:T(1,128)S(1)} %get-tuple-element.25.row_ref, bf16[1280,1280]{1,0:T(8,128)(2,1)S(1)} %get-tuple-element.26.first_ref, bf16[2560,1280]{1,0:T(8,128)(2,1)} %weight_ref.1), custom_call_target="tpu_custom_call" | custom-call | tf_op jit(solution)/shard_map/mix/pallas_call | solution.py:227
  (1 shorter events, 0.0 us)
Async XLA Ops:
  30.7 29.2 %all-to-all-start.1 = ((bf16[8,2,192,128]{3,2,1,0:T(8,128)(2,1)}), bf16[8,2,192,128]{3,2,1,0:T(8,128)(2,1)S(1)}, u32[]{:S(2)}, u32[]{:S(2)}) async-start(bf16[8,2,192,128]{3,2,1,0:T(8,128)(2,1)} %get-tuple-element.16), calls=%async_computation.1 | async-start | bytes 1572864 | tf_op jit(solution)/shard_map/all_to_all | solution.py:161
  72.8 20.6 %all-to-all-start.3 = ((bf16[24,32,128]{2,1,0:T(8,128)(2,1)}), bf16[24,32,128]{2,1,0:T(8,128)(2,1)S(1)}, u32[]{:S(2)}, u32[]{:S(2)}) async-start(bf16[24,32,128]{2,1,0:T(8,128)(2,1)} %combine.1), calls=%async_computation.3 | async-start | bytes 393216 | tf_op jit(solution)/shard_map/all_to_all | solution.py:161
  79.5 0.7 copy-start

commit v13 on v12

--- a/solution.py
+++ b/solution.py
@@ -15,7 +15,7 @@
 STAT_LANES = 8
 STAT_ROWS = 16
 GROUP_STEP = 1
-EARLY_HEADS = 10
+EARLY_HEADS = 6
 KERNEL_VMEM = 16 * 1024 * 1024
 MIX_VMEM = 50 * 1024 * 1024
 IN_VMEM = pl.BlockSpec(memory_space=pltpu.VMEM)
@@ -181,9 +181,27 @@
         compiler_params=pltpu.CompilerParams(vmem_limit_bytes=KERNEL_VMEM),
         name="split",
     )(exchange(stacked, HEAD_AXES))
+    channels = out_weight.shape[1]
+    key_value_copies, weight = lax.optimization_barrier((key_value_copies, out_weight))
+    in_hbm = pl.BlockSpec(memory_space=pltpu.HBM)
+    first, row = pl.pallas_call(
+        fetch_kernel,
+        out_shape=[
+            jax.ShapeDtypeStruct((EARLY_HEADS * HEAD_DIM, channels), weight.dtype),
+            jax.ShapeDtypeStruct((1, channels), gate.dtype),
+        ],
+        in_specs=[in_hbm, IN_VMEM],
+        out_specs=[IN_VMEM] * 2,
+        scratch_shapes=[pltpu.SemaphoreType.DMA((EARLY_HEADS // 2,))],
+        compiler_params=pltpu.CompilerParams(vmem_limit_bytes=MIX_VMEM),
+        cost_estimate=pl.CostEstimate(
+            flops=0, bytes_accessed=4 * EARLY_HEADS * HEAD_DIM * channels, transcendentals=0
+        ),
+        name="fetch",
+    )(weight, gate)
     key_value = exchange(key_value_copies, KEY_AXES)
     group = lax.all_gather(own_query, QUERY_AXES, axis=0, tiled=False)
-    key_value, group = lax.optimization_barrier((key_value, group))
+    key_value, group, first, row = lax.optimization_barrier((key_value, group, first, row))
     partial = pl.pallas_call(
         attend_kernel,
         out_shape=jax.ShapeDtypeStruct(
@@ -203,26 +221,7 @@
         compiler_params=pltpu.CompilerParams(vmem_limit_bytes=KERNEL_VMEM),
         name="combine",
     )(partial)
-    channels = out_weight.shape[1]
-    attended, weight = lax.optimization_barrier((attended, out_weight))
-    in_hbm = pl.BlockSpec(memory_space=pltpu.HBM)
-    first, row = pl.pallas_call(
-        fetch_kernel,
-        out_shape=[
-            jax.ShapeDtypeStruct((EARLY_HEADS * HEAD_DIM, channels), weight.dtype),
-            jax.ShapeDtypeStruct((1, channels), gate.dtype),
-        ],
-        in_specs=[in_hbm, IN_VMEM],
-        out_specs=[IN_VMEM] * 2,
-        scratch_shapes=[pltpu.SemaphoreType.DMA((EARLY_HEADS // 2,))],
-        compiler_params=pltpu.CompilerParams(vmem_limit_bytes=MIX_VMEM),
-        cost_estimate=pl.CostEstimate(
-            flops=0, bytes_accessed=4 * EARLY_HEADS * HEAD_DIM * channels, transcendentals=0
-        ),
-        name="fetch",
-    )(weight, gate)
     attended = exchange(attended, HEAD_AXES)
-    attended, first, row = lax.optimization_barrier((attended, first, row))
     late = heads - EARLY_HEADS
     return pl.pallas_call(
         mix_kernel,

time: 96.9 us -> 96.1 us (level)
  blocking collectives: 47.7 us -> 68.4 us
  waiting for transfers between devices: 23.8 us -> 10 us
  starting transfers between devices: 13.5 us -> 6.82 us
  Pallas kernels: 9.82 us -> 8.84 us
    all_to_all x2 -> x3, blocking collectives: 37.9 us -> 58.2 us  [exchange(): return lax.all_to_all(blocks, axes, split_axis=0, concat_axis=0, tiled=True)]
    all_to_all x2 -> x1, waiting for transfers between devices: 23.8 us -> 10 us  [exchange(): return lax.all_to_all(blocks, axes, split_axis=0, concat_axis=0, tiled=True)]
    all_to_all x2 -> x1, starting transfers between devices: 13.5 us -> 6.82 us  [exchange(): return lax.all_to_all(blocks, axes, split_axis=0, concat_axis=0, tiled=True)]
  transfers between devices with their start and end apart: 2 -> 1, of which waited for: 2 -> 1; matrix products, arithmetic and copies ran while one was open for 0% -> 0% of each run, Pallas kernels for 2% -> 2%
where the time goes in v13:
time: 96.1 us; the launch traced here: 95.7 us
  blocking collectives  68.4 us (71%)
  waiting for transfers between devices  10 us (10%)
  Pallas kernels  8.84 us (9%)
  starting transfers between devices  6.82 us (7%)
    all_to_all x3, blocking collectives, exchange(): return lax.all_to_all(blocks, axes, split_axis=0, concat_axis=0, tiled=True)  58.2 us
    all_gather x1, blocking collectives, on_device(): group = lax.all_gather(own_query, QUERY_AXES, axis=0, tiled=False)  10.2 us
    all_to_all x1, waiting for transfers between devices, exchange(): return lax.all_to_all(blocks, axes, split_axis=0, concat_axis=0, tiled=True)  10 us
    all_to_all x1, starting transfers between devices, exchange(): return lax.all_to_all(blocks, axes, split_axis=0, concat_axis=0, tiled=True)  6.82 us
    pallas_call x1, Pallas kernels, on_device(): pl.pallas_call(mix_kernel, out_shape=jax.ShapeDtypeStruct((own_tokens, ch...  3.21 us
    pallas_call x1, Pallas kernels, on_device(): pl.pallas_call(attend_kernel, out_shape=jax.ShapeDtypeStruct((group.shape...  2.27 us
  transfers between devices with their start and end apart: 1, of which 1 were waited for; matrix products, arithmetic and copies ran while one was open for 0% of the time, Pallas kernels for 2%

profile of v13, /device:TPU:1, one launch (start us, length us, event | category | flops | bytes accessed | tf_op | source)
XLA Modules:
  0.0 95.7 jit_solution(1832373547128825119)
XLA Ops:
  0.0 0.8 maximum_bitcast_fusion
  0.9 28.8 %all_to_all.20.local_ref = bf16[24,24,128]{2,1,0:T(8,128)(2,1)S(1)} all-to-all(bf16[24,24,128]{2,1,0:T(8,128)(2,1)S(1)} %pad.4), channel_id=1, replica_groups=mesh['zl'=3,'y'=8,'x'=4,'c'=2,'tp'=4] {'zl','c','tp'}, dimensions={0} | all-to-all | bytes 294912 | tf_op jit(solution)/shard_map/all_to_all | solution.py:161
  29.7 1.0 %split.1 = (bf16[192,128]{1,0:T(8,128)(2,1)S(1)}, bf16[8,2,192,128]{3,2,1,0:T(8,128)(2,1)}) custom-call(bf16[24,24,128]{2,1,0:T(8,128)(2,1)S(1)} %all_to_all.20.local_ref), custom_call_target="tpu_custom_call" | custom-call | tf_op jit(solution)/shard_map/split/pallas_call | solution.py:173
  30.7 6.8 %all-to-all-start.1 = ((bf16[8,2,192,128]{3,2,1,0:T(8,128)(2,1)}), bf16[8,2,192,128]{3,2,1,0:T(8,128)(2,1)S(1)}, u32[]{:S(2)}, u32[]{:S(2)}) async-start(bf16[8,2,192,128]{3,2,1,0:T(8,128)(2,1)} %get-tuple-element.16), calls=%async_computation.1 | async-start | bytes 1572864 | tf_op jit(solution)/shard_map/all_to_all | solution.py:161
  37.5 0.0 copy-start
  37.5 0.7 copy-done
  38.2 1.5 %fetch.1 = (bf16[768,1280]{1,0:T(8,128)(2,1)S(1)}, f32[1,1280]{1,0:T(1,128)S(1)}) custom-call(bf16[2560,1280]{1,0:T(8,128)(2,1)} %weight_ref.1, f32[1280]{0:T(1024)S(1)} %copy-done), custom_call_target="tpu_custom_call" | custom-call | bytes 3932160 | tf_op jit(solution)/shard_map/fetch/pallas_call | solution.py:187
  39.7 10.2 %all-gather = bf16[768,128]{1,0:T(8,128)(2,1)S(1)} all-gather(bf16[192,128]{1,0:T(8,128)(2,1)S(1)} %get-tuple-element.17), channel_id=2, replica_groups=mesh['zl'=3,'y'=8,'x'=4,'c'=2,'tp'=4] {'x'}, dimensions={0}, use_global_device_ids=true | all-gather | bytes 245760 | tf_op jit(solution)/shard_map/all_gather | solution.py:203
  49.9 10.0 %all-to-all-done.1.key_value_ref = bf16[8,2,192,128]{3,2,1,0:T(8,128)(2,1)S(1)} async-done(((bf16[8,2,192,128]{3,2,1,0:T(8,128)(2,1)}), bf16[8,2,192,128]{3,2,1,0:T(8,128)(2,1)S(1)}, u32[]{:S(2)}, u32[]{:S(2)}) %all-to-all-start.1) | async-done | bytes 786464 | tf_op jit(solution)/shard_map/all_to_all | solution.py:161
  59.9 2.3 %attend.1 = bf16[4,208,128]{2,1,0:T(8,128)(2,1)S(1)} custom-call(bf16[4,192,128]{2,1,0:T(8,128)(2,1)S(1)} %bitcast.14, bf16[8,2,192,128]{3,2,1,0:T(8,128)(2,1)S(1)} %all-to-all-done.1.key_value_ref), custom_call_target="tpu_custom_call" | custom-call | tf_op jit(solution)/shard_map/attend/pallas_call | solution.py:205
  62.2 9.1 %all_to_all.21.part_ref = bf16[4,208,128]{2,1,0:T(8,128)(2,1)S(1)} all-to-all(bf16[4,208,128]{2,1,0:T(8,128)(2,1)S(1)} %attend.1), channel_id=1, replica_groups=mesh['zl'=3,'y'=8,'x'=4,'c'=2,'tp'=4] {'x'}, dimensions={0} | all-to-all | bytes 425984 | tf_op jit(solution)/shard_map/all_to_all | solution.py:161
  71.3 0.9 combine.1
  72.1 20.3 %all_to_all.22.attended_ref = bf16[24,32,128]{2,1,0:T(8,128)(2,1)S(1)} all-to-all(bf16[24,32,128]{2,1,0:T(8,128)(2,1)S(1)} %combine.1), channel_id=1, replica_groups=mesh['zl'=3,'y'=8,'x'=4,'c'=2,'tp'=4] {'zl','c','tp'}, dimensions={0} | all-to-all | bytes 393216 | tf_op jit(solution)/shard_map/all_to_all | solution.py:161
  92.5 3.2 %mix.1 = bf16[32,1280]{1,0:T(8,128)(2,1)} custom-call(bf16[24,32,128]{2,1,0:T(8,128)(2,1)S(1)} %all_to_all.22.attended_ref, f32[1,1280]{1,0:T(1,128)S(1)} %get-tuple-element.23.row_ref, bf16[768,1280]{1,0:T(8,128)(2,1)S(1)} %get-tuple-element.24.first_ref, bf16[2560,1280]{1,0:T(8,128)(2,1)} %weight_ref.1), custom_call_target="tpu_custom_call" | custom-call | tf_op jit(solution)/shard_map/mix/pallas_call | solution.py:226
  (1 shorter events, 0.0 us)
Async XLA Ops:
  30.7 29.2 %all-to-all-start.1 = ((bf16[8,2,192,128]{3,2,1,0:T(8,128)(2,1)}), bf16[8,2,192,128]{3,2,1,0:T(8,128)(2,1)S(1)}, u32[]{:S(2)}, u32[]{:S(2)}) async-start(bf16[8,2,192,128]{3,2,1,0:T(8,128)(2,1)} %get-tuple-element.16), calls=%async_computation.1 | async-start | bytes 1572864 | tf_op jit(solution)/shard_map/all_to_all | solution.py:161
  37.5 0.7 copy-start

commit v14 on v13

--- a/solution.py
+++ b/solution.py
@@ -1,5 +1,8 @@
+import math
+
 import jax
 import jax.numpy as jnp
+import numpy as np
 from jax import lax
 from jax.experimental import pallas as pl
 from jax.experimental.pallas import tpu as pltpu
@@ -8,6 +11,7 @@
 HEAD_DIM = 128
 LOG2E = 1.4426950408889634
 SCALE = HEAD_DIM ** -0.5
+AXES = ("zl", "y", "x", "c", "tp")
 HEAD_AXES = ("zl", "c", "tp")
 QUERY_AXES = ("x",)
 KEY_AXES = ("y",)
@@ -157,8 +161,19 @@
     out_ref[...] = (product * row_ref[...]).astype(jnp.bfloat16)
 
 
+def listed_groups(axes):
+    sizes = [lax.axis_size(axis) for axis in AXES]
+    places = np.arange(math.prod(sizes)).reshape(sizes)
+    inner = [AXES.index(axis) for axis in axes]
+    outer = [place for place in range(len(AXES)) if place not in inner]
+    members = math.prod(sizes[place] for place in inner)
+    return places.transpose(outer + inner).reshape(-1, members).tolist()
+
+
 def exchange(blocks, axes):
-    return lax.all_to_all(blocks, axes, split_axis=0, concat_axis=0, tiled=True)
+    return lax.all_to_all(
+        blocks, AXES, split_axis=0, concat_axis=0, axis_index_groups=listed_groups(axes), tiled=True
+    )
 
 
 def on_device(queries, keys, vals, out_weight, gate):

time: 96.1 us -> 96.1 us (level)
  no operation moved by 1% of the time
where the time goes in v14:
time: 96.1 us; the launch traced here: 95.7 us
  blocking collectives  68.4 us (71%)
  waiting for transfers between devices  10 us (10%)
  Pallas kernels  8.84 us (9%)
  starting transfers between devices  6.82 us (7%)
    all_to_all x3, blocking collectives, exchange(): lax.all_to_all(blocks, AXES, split_axis=0, concat_axis=0, axis_index_grou...  58.2 us
    all_gather x1, blocking collectives, on_device(): group = lax.all_gather(own_query, QUERY_AXES, axis=0, tiled=False)  10.2 us
    all_to_all x1, waiting for transfers between devices, exchange(): lax.all_to_all(blocks, AXES, split_axis=0, concat_axis=0, axis_index_grou...  10 us
    all_to_all x1, starting transfers between devices, exchange(): lax.all_to_all(blocks, AXES, split_axis=0, concat_axis=0, axis_index_grou...  6.82 us
    pallas_call x1, Pallas kernels, on_device(): pl.pallas_call(mix_kernel, out_shape=jax.ShapeDtypeStruct((own_tokens, ch...  3.21 us
    pallas_call x1, Pallas kernels, on_device(): pl.pallas_call(attend_kernel, out_shape=jax.ShapeDtypeStruct((group.shape...  2.27 us
  transfers between devices with their start and end apart: 1, of which 1 were waited for; matrix products, arithmetic and copies ran while one was open for 0% of the time, Pallas kernels for 2%

profile of v14, /device:TPU:1, one launch (start us, length us, event | category | flops | bytes accessed | tf_op | source)
XLA Modules:
  0.0 95.7 jit_solution(1832373547128825119)
XLA Ops:
  0.0 0.8 maximum_bitcast_fusion
  0.9 28.8 %all_to_all.20.local_ref = bf16[24,24,128]{2,1,0:T(8,128)(2,1)S(1)} all-to-all(bf16[24,24,128]{2,1,0:T(8,128)(2,1)S(1)} %pad.4), channel_id=1, replica_groups={{0,1,2,3,4,5,6,7,256,257,258,259,260,261,262,263,512,513,514,515,516,51..., dimensions={0} | all-to-all | bytes 294912 | tf_op jit(solution)/shard_map/all_to_all | solution.py:174
  29.7 1.0 %split.1 = (bf16[192,128]{1,0:T(8,128)(2,1)S(1)}, bf16[8,2,192,128]{3,2,1,0:T(8,128)(2,1)}) custom-call(bf16[24,24,128]{2,1,0:T(8,128)(2,1)S(1)} %all_to_all.20.local_ref), custom_call_target="tpu_custom_call" | custom-call | tf_op jit(solution)/shard_map/split/pallas_call | solution.py:188
  30.7 6.8 %all-to-all-start.1 = ((bf16[8,2,192,128]{3,2,1,0:T(8,128)(2,1)}), bf16[8,2,192,128]{3,2,1,0:T(8,128)(2,1)S(1)}, u32[]{:S(2)}, u32[]{:S(2)}) async-start(bf16[8,2,192,128]{3,2,1,0:T(8,128)(2,1)} %get-tuple-element.16), calls=%async_computation.1 | async-start | bytes 1572864 | tf_op jit(solution)/shard_map/all_to_all | solution.py:174
  37.5 0.0 copy-start
  37.5 0.7 copy-done
  38.2 1.5 %fetch.1 = (bf16[768,1280]{1,0:T(8,128)(2,1)S(1)}, f32[1,1280]{1,0:T(1,128)S(1)}) custom-call(bf16[2560,1280]{1,0:T(8,128)(2,1)} %weight_ref.1, f32[1280]{0:T(1024)S(1)} %copy-done), custom_call_target="tpu_custom_call" | custom-call | bytes 3932160 | tf_op jit(solution)/shard_map/fetch/pallas_call | solution.py:202
  39.7 10.2 %all-gather = bf16[768,128]{1,0:T(8,128)(2,1)S(1)} all-gather(bf16[192,128]{1,0:T(8,128)(2,1)S(1)} %get-tuple-element.17), channel_id=2, replica_groups=mesh['zl'=3,'y'=8,'x'=4,'c'=2,'tp'=4] {'x'}, dimensions={0}, use_global_device_ids=true | all-gather | bytes 245760 | tf_op jit(solution)/shard_map/all_gather | solution.py:218
  49.9 10.0 %all-to-all-done.1.key_value_ref = bf16[8,2,192,128]{3,2,1,0:T(8,128)(2,1)S(1)} async-done(((bf16[8,2,192,128]{3,2,1,0:T(8,128)(2,1)}), bf16[8,2,192,128]{3,2,1,0:T(8,128)(2,1)S(1)}, u32[]{:S(2)}, u32[]{:S(2)}) %all-to-all-start.1) | async-done | bytes 786464 | tf_op jit(solution)/shard_map/all_to_all | solution.py:174
  59.9 2.3 %attend.1 = bf16[4,208,128]{2,1,0:T(8,128)(2,1)S(1)} custom-call(bf16[4,192,128]{2,1,0:T(8,128)(2,1)S(1)} %bitcast.14, bf16[8,2,192,128]{3,2,1,0:T(8,128)(2,1)S(1)} %all-to-all-done.1.key_value_ref), custom_call_target="tpu_custom_call" | custom-call | tf_op jit(solution)/shard_map/attend/pallas_call | solution.py:220
  62.2 9.1 %all_to_all.21.part_ref = bf16[4,208,128]{2,1,0:T(8,128)(2,1)S(1)} all-to-all(bf16[4,208,128]{2,1,0:T(8,128)(2,1)S(1)} %attend.1), channel_id=1, replica_groups={{0,8,16,24},{1,9,17,25},{2,10,18,26},{3,11,19,27},{4,12,20,28},{5,13,21..., dimensions={0} | all-to-all | bytes 425984 | tf_op jit(solution)/shard_map/all_to_all | solution.py:174
  71.3 0.9 combine.1
  72.1 20.3 %all_to_all.22.attended_ref = bf16[24,32,128]{2,1,0:T(8,128)(2,1)S(1)} all-to-all(bf16[24,32,128]{2,1,0:T(8,128)(2,1)S(1)} %combine.1), channel_id=1, replica_groups={{0,1,2,3,4,5,6,7,256,257,258,259,260,261,262,263,512,513,514,515,516,51..., dimensions={0} | all-to-all | bytes 393216 | tf_op jit(solution)/shard_map/all_to_all | solution.py:174
  92.5 3.2 %mix.1 = bf16[32,1280]{1,0:T(8,128)(2,1)} custom-call(bf16[24,32,128]{2,1,0:T(8,128)(2,1)S(1)} %all_to_all.22.attended_ref, f32[1,1280]{1,0:T(1,128)S(1)} %get-tuple-element.23.row_ref, bf16[768,1280]{1,0:T(8,128)(2,1)S(1)} %get-tuple-element.24.first_ref, bf16[2560,1280]{1,0:T(8,128)(2,1)} %weight_ref.1), custom_call_target="tpu_custom_call" | custom-call | tf_op jit(solution)/shard_map/mix/pallas_call | solution.py:241
  (1 shorter events, 0.0 us)
Async XLA Ops:
  30.7 29.2 %all-to-all-start.1 = ((bf16[8,2,192,128]{3,2,1,0:T(8,128)(2,1)}), bf16[8,2,192,128]{3,2,1,0:T(8,128)(2,1)S(1)}, u32[]{:S(2)}, u32[]{:S(2)}) async-start(bf16[8,2,192,128]{3,2,1,0:T(8,128)(2,1)} %get-tuple-element.16), calls=%async_computation.1 | async-start | bytes 1572864 | tf_op jit(solution)/shard_map/all_to_all | solution.py:174
  37.5 0.7 copy-start

commit v15 on v13

--- a/solution.py
+++ b/solution.py
@@ -1,3 +1,5 @@
+import functools
+
 import jax
 import jax.numpy as jnp
 from jax import lax
@@ -14,7 +16,8 @@
 STATS = 2
 STAT_LANES = 8
 STAT_ROWS = 16
-GROUP_STEP = 1
+GROUP_STEP = 2
+KEY_BLOCKS = 4
 EARLY_HEADS = 6
 KERNEL_VMEM = 16 * 1024 * 1024
 MIX_VMEM = 50 * 1024 * 1024
@@ -61,31 +64,47 @@
     )
 
 
-def split_kernel(local_ref, query_ref, key_value_ref):
+def split_kernel(local_ref, query_ref, key_value_ref, block_ref, semaphores):
     slots = local_ref.shape[0]
     rows = local_ref.shape[1] // 3
+    for place in range(2):
+        block = local_ref[:, pl.ds((place + 1) * rows, rows)]
+        block_ref[place] = block.reshape(slots * rows, HEAD_DIM)
+    copies = []
+    for copy in range(key_value_ref.shape[0]):
+        copies.append(
+            pltpu.make_async_copy(block_ref, key_value_ref.at[copy], semaphores.at[copy])
+        )
+        copies[copy].start()
     query_ref[...] = local_ref[:, pl.ds(0, rows)].reshape(slots * rows, HEAD_DIM)
-    for place in range(2):
-        block = local_ref[:, pl.ds((place + 1) * rows, rows)].reshape(slots * rows, HEAD_DIM)
-        for copy in range(key_value_ref.shape[0]):
-            key_value_ref[copy, place] = block
+    for copy in copies:
+        copy.wait()
 
 
 def attend_kernel(q_ref, key_value_ref, out_ref):
     groups, tokens, width = q_ref.shape
-    count = key_value_ref.shape[0] * tokens
-    key = key_value_ref[:, 0].reshape(count, width)
-    value = key_value_ref[:, 1].reshape(count, width)
+    blocks = key_value_ref.shape[0] // KEY_BLOCKS
+    count = blocks * tokens
     columns = []
     for group in range(0, groups, GROUP_STEP):
         query = q_ref[pl.ds(group, GROUP_STEP)].reshape(GROUP_STEP * tokens, width)
-        score = lax.dot_general(
-            query, key, (((1,), (1,)), ((), ())), preferred_element_type=jnp.float32
-        )
-        highest = jnp.max(score, axis=1, keepdims=True)
-        expd = jnp.exp2((score - highest) * (SCALE * LOG2E))
-        total = jnp.sum(expd, axis=1, keepdims=True)
-        summed = jnp.dot(expd.astype(jnp.bfloat16), value, preferred_element_type=jnp.float32)
+        scores = []
+        for block in range(KEY_BLOCKS):
+            key = key_value_ref[pl.ds(block * blocks, blocks), 0].reshape(count, width)
+            scores.append(
+                lax.dot_general(
+                    query, key, (((1,), (1,)), ((), ())), preferred_element_type=jnp.float32
+                )
+            )
+        highest = functools.reduce(
+            jnp.maximum, [jnp.max(score, axis=1, keepdims=True) for score in scores]
+        )
+        total, summed = 0.0, 0.0
+        for block, score in enumerate(scores):
+            value = key_value_ref[pl.ds(block * blocks, blocks), 1].reshape(count, width)
+            expd = jnp.exp2((score - highest) * (SCALE * LOG2E))
+            total += jnp.sum(expd, axis=1, keepdims=True)
+            summed += jnp.dot(expd.astype(jnp.bfloat16), value, preferred_element_type=jnp.float32)
         for step in range(GROUP_STEP):
             rows = slice(step * tokens, (step + 1) * tokens)
             out_ref[group + step, pl.ds(0, tokens)] = summed[rows].astype(jnp.bfloat16)
@@ -177,7 +196,11 @@
             jax.ShapeDtypeStruct((lax.axis_size(KEY_AXES), 2, tokens, HEAD_DIM), jnp.bfloat16),
         ],
         in_specs=[IN_VMEM],
-        out_specs=[IN_VMEM] * 2,
+        out_specs=[IN_VMEM, pl.BlockSpec(memory_space=pltpu.HBM)],
+        scratch_shapes=[
+            pltpu.VMEM((2, tokens, HEAD_DIM), jnp.bfloat16),
+            pltpu.SemaphoreType.DMA((lax.axis_size(KEY_AXES),)),
+        ],
         compiler_params=pltpu.CompilerParams(vmem_limit_bytes=KERNEL_VMEM),
         name="split",
     )(exchange(stacked, HEAD_AXES))

time: 96.1 us -> 95.8 us (level)
  no operation moved by 1% of the time
where the time goes in v15:
time: 95.8 us; the launch traced here: 95.4 us
  blocking collectives  68.4 us (71%)
  waiting for transfers between devices  10 us (10%)
  Pallas kernels  8.58 us (9%)
  starting transfers between devices  6.83 us (7%)
    all_to_all x3, blocking collectives, exchange(): return lax.all_to_all(blocks, axes, split_axis=0, concat_axis=0, tiled=True)  58.2 us
    all_gather x1, blocking collectives, on_device(): group = lax.all_gather(own_query, QUERY_AXES, axis=0, tiled=False)  10.2 us
    all_to_all x1, waiting for transfers between devices, exchange(): return lax.all_to_all(blocks, axes, split_axis=0, concat_axis=0, tiled=True)  10 us
    all_to_all x1, starting transfers between devices, exchange(): return lax.all_to_all(blocks, axes, split_axis=0, concat_axis=0, tiled=True)  6.83 us
    pallas_call x1, Pallas kernels, on_device(): pl.pallas_call(mix_kernel, out_shape=jax.ShapeDtypeStruct((own_tokens, ch...  3.21 us
    pallas_call x1, Pallas kernels, on_device(): pl.pallas_call(attend_kernel, out_shape=jax.ShapeDtypeStruct((group.shape...  2.03 us
  transfers between devices with their start and end apart: 1, of which 1 were waited for; matrix products, arithmetic and copies ran while one was open for 0% of the time, Pallas kernels for 2%

profile of v15, /device:TPU:1, one launch (start us, length us, event | category | flops | bytes accessed | tf_op | source)
XLA Modules:
  0.0 95.4 jit_solution(7566353001835026334)
XLA Ops:
  0.0 0.8 maximum_bitcast_fusion
  0.9 28.8 %all_to_all.20.local_ref = bf16[24,24,128]{2,1,0:T(8,128)(2,1)S(1)} all-to-all(bf16[24,24,128]{2,1,0:T(8,128)(2,1)S(1)} %pad.4), channel_id=1, replica_groups=mesh['zl'=3,'y'=8,'x'=4,'c'=2,'tp'=4] {'zl','c','tp'}, dimensions={0} | all-to-all | bytes 294912 | tf_op jit(solution)/shard_map/all_to_all | solution.py:180
  29.7 1.0 %split.1 = (bf16[192,128]{1,0:T(8,128)(2,1)S(1)}, bf16[8,2,192,128]{3,2,1,0:T(8,128)(2,1)}) custom-call(bf16[24,24,128]{2,1,0:T(8,128)(2,1)S(1)} %all_to_all.20.local_ref), custom_call_target="tpu_custom_call" | custom-call | tf_op jit(solution)/shard_map/split/pallas_call | solution.py:192
  30.7 6.8 %all-to-all-start.1 = ((bf16[8,2,192,128]{3,2,1,0:T(8,128)(2,1)}), bf16[8,2,192,128]{3,2,1,0:T(8,128)(2,1)S(1)}, u32[]{:S(2)}, u32[]{:S(2)}) async-start(bf16[8,2,192,128]{3,2,1,0:T(8,128)(2,1)} %get-tuple-element.16), calls=%async_computation.1 | async-start | bytes 1572864 | tf_op jit(solution)/shard_map/all_to_all | solution.py:180
  37.5 0.0 copy-start
  37.5 0.7 copy-done
  38.2 1.5 %fetch.1 = (bf16[768,1280]{1,0:T(8,128)(2,1)S(1)}, f32[1,1280]{1,0:T(1,128)S(1)}) custom-call(bf16[2560,1280]{1,0:T(8,128)(2,1)} %weight_ref.1, f32[1280]{0:T(1024)S(1)} %copy-done), custom_call_target="tpu_custom_call" | custom-call | bytes 3932160 | tf_op jit(solution)/shard_map/fetch/pallas_call | solution.py:210
  39.7 10.2 %all-gather = bf16[768,128]{1,0:T(8,128)(2,1)S(1)} all-gather(bf16[192,128]{1,0:T(8,128)(2,1)S(1)} %get-tuple-element.17), channel_id=2, replica_groups=mesh['zl'=3,'y'=8,'x'=4,'c'=2,'tp'=4] {'x'}, dimensions={0}, use_global_device_ids=true | all-gather | bytes 245760 | tf_op jit(solution)/shard_map/all_gather | solution.py:226
  49.9 10.0 %all-to-all-done.1.key_value_ref = bf16[8,2,192,128]{3,2,1,0:T(8,128)(2,1)S(1)} async-done(((bf16[8,2,192,128]{3,2,1,0:T(8,128)(2,1)}), bf16[8,2,192,128]{3,2,1,0:T(8,128)(2,1)S(1)}, u32[]{:S(2)}, u32[]{:S(2)}) %all-to-all-start.1) | async-done | bytes 786464 | tf_op jit(solution)/shard_map/all_to_all | solution.py:180
  59.9 2.0 %attend.1 = bf16[4,208,128]{2,1,0:T(8,128)(2,1)S(1)} custom-call(bf16[4,192,128]{2,1,0:T(8,128)(2,1)S(1)} %bitcast.14, bf16[8,2,192,128]{3,2,1,0:T(8,128)(2,1)S(1)} %all-to-all-done.1.key_value_ref), custom_call_target="tpu_custom_call" | custom-call | tf_op jit(solution)/shard_map/attend/pallas_call | solution.py:228
  62.0 9.1 %all_to_all.21.part_ref = bf16[4,208,128]{2,1,0:T(8,128)(2,1)S(1)} all-to-all(bf16[4,208,128]{2,1,0:T(8,128)(2,1)S(1)} %attend.1), channel_id=1, replica_groups=mesh['zl'=3,'y'=8,'x'=4,'c'=2,'tp'=4] {'x'}, dimensions={0} | all-to-all | bytes 425984 | tf_op jit(solution)/shard_map/all_to_all | solution.py:180
  71.0 0.9 combine.1
  71.9 20.3 %all_to_all.22.attended_ref = bf16[24,32,128]{2,1,0:T(8,128)(2,1)S(1)} all-to-all(bf16[24,32,128]{2,1,0:T(8,128)(2,1)S(1)} %combine.1), channel_id=1, replica_groups=mesh['zl'=3,'y'=8,'x'=4,'c'=2,'tp'=4] {'zl','c','tp'}, dimensions={0} | all-to-all | bytes 393216 | tf_op jit(solution)/shard_map/all_to_all | solution.py:180
  92.2 3.2 %mix.1 = bf16[32,1280]{1,0:T(8,128)(2,1)} custom-call(bf16[24,32,128]{2,1,0:T(8,128)(2,1)S(1)} %all_to_all.22.attended_ref, f32[1,1280]{1,0:T(1,128)S(1)} %get-tuple-element.23.row_ref, bf16[768,1280]{1,0:T(8,128)(2,1)S(1)} %get-tuple-element.24.first_ref, bf16[2560,1280]{1,0:T(8,128)(2,1)} %weight_ref.1), custom_call_target="tpu_custom_call" | custom-call | tf_op jit(solution)/shard_map/mix/pallas_call | solution.py:249
  (1 shorter events, 0.0 us)
Async XLA Ops:
  30.7 29.2 %all-to-all-start.1 = ((bf16[8,2,192,128]{3,2,1,0:T(8,128)(2,1)}), bf16[8,2,192,128]{3,2,1,0:T(8,128)(2,1)S(1)}, u32[]{:S(2)}, u32[]{:S(2)}) async-start(bf16[8,2,192,128]{3,2,1,0:T(8,128)(2,1)} %get-tuple-element.16), calls=%async_computation.1 | async-start | bytes 1572864 | tf_op jit(solution)/shard_map/all_to_all | solution.py:180
  37.5 0.7 copy-start

commit v16 on v15

--- a/solution.py
+++ b/solution.py
@@ -10,7 +10,7 @@
 HEAD_DIM = 128
 LOG2E = 1.4426950408889634
 SCALE = HEAD_DIM ** -0.5
-HEAD_AXES = ("zl", "c", "tp")
+HEAD_AXES = ("c", "zl", "tp")
 QUERY_AXES = ("x",)
 KEY_AXES = ("y",)
 STATS = 2

time: 95.8 us -> 97.3 us (1.016)
  no operation moved by 1% of the time
where the time goes in v16:
time: 97.3 us; the launch traced here: 96.9 us
  blocking collectives  68.9 us (71%)
  waiting for transfers between devices  10.9 us (11%)
  Pallas kernels  8.58 us (9%)
  starting transfers between devices  6.83 us (7%)
    all_to_all x3, blocking collectives, exchange(): return lax.all_to_all(blocks, axes, split_axis=0, concat_axis=0, tiled=True)  58.4 us
    all_to_all x1, waiting for transfers between devices, exchange(): return lax.all_to_all(blocks, axes, split_axis=0, concat_axis=0, tiled=True)  10.9 us
    all_gather x1, blocking collectives, on_device(): group = lax.all_gather(own_query, QUERY_AXES, axis=0, tiled=False)  10.6 us
    all_to_all x1, starting transfers between devices, exchange(): return lax.all_to_all(blocks, axes, split_axis=0, concat_axis=0, tiled=True)  6.83 us
    pallas_call x1, Pallas kernels, on_device(): pl.pallas_call(mix_kernel, out_shape=jax.ShapeDtypeStruct((own_tokens, ch...  3.21 us
    pallas_call x1, Pallas kernels, on_device(): pl.pallas_call(attend_kernel, out_shape=jax.ShapeDtypeStruct((group.shape...  2.03 us
  transfers between devices with their start and end apart: 1, of which 1 were waited for; matrix products, arithmetic and copies ran while one was open for 0% of the time, Pallas kernels for 2%

profile of v16, /device:TPU:1, one launch (start us, length us, event | category | flops | bytes accessed | tf_op | source)
XLA Modules:
  0.0 96.9 jit_solution(15488972040913679327)
XLA Ops:
  0.0 0.8 maximum_bitcast_fusion
  0.9 29.9 %all_to_all.20.local_ref = bf16[24,24,128]{2,1,0:T(8,128)(2,1)S(1)} all-to-all(bf16[24,24,128]{2,1,0:T(8,128)(2,1)S(1)} %pad.4), channel_id=1, replica_groups=mesh['zl'=3,'y'=8,'x'=4,'c'=2,'tp'=4] {'c','zl','tp'}, dimensions={0} | all-to-all | bytes 294912 | tf_op jit(solution)/shard_map/all_to_all | solution.py:180
  30.7 1.0 %split.1 = (bf16[192,128]{1,0:T(8,128)(2,1)S(1)}, bf16[8,2,192,128]{3,2,1,0:T(8,128)(2,1)}) custom-call(bf16[24,24,128]{2,1,0:T(8,128)(2,1)S(1)} %all_to_all.20.local_ref), custom_call_target="tpu_custom_call" | custom-call | tf_op jit(solution)/shard_map/split/pallas_call | solution.py:192
  31.7 6.8 %all-to-all-start.1 = ((bf16[8,2,192,128]{3,2,1,0:T(8,128)(2,1)}), bf16[8,2,192,128]{3,2,1,0:T(8,128)(2,1)S(1)}, u32[]{:S(2)}, u32[]{:S(2)}) async-start(bf16[8,2,192,128]{3,2,1,0:T(8,128)(2,1)} %get-tuple-element.16), calls=%async_computation.1 | async-start | bytes 1572864 | tf_op jit(solution)/shard_map/all_to_all | solution.py:180
  38.6 0.0 copy-start
  38.6 0.7 copy-done
  39.2 1.5 %fetch.1 = (bf16[768,1280]{1,0:T(8,128)(2,1)S(1)}, f32[1,1280]{1,0:T(1,128)S(1)}) custom-call(bf16[2560,1280]{1,0:T(8,128)(2,1)} %weight_ref.1, f32[1280]{0:T(1024)S(1)} %copy-done), custom_call_target="tpu_custom_call" | custom-call | bytes 3932160 | tf_op jit(solution)/shard_map/fetch/pallas_call | solution.py:210
  40.8 10.6 %all-gather = bf16[768,128]{1,0:T(8,128)(2,1)S(1)} all-gather(bf16[192,128]{1,0:T(8,128)(2,1)S(1)} %get-tuple-element.17), channel_id=2, replica_groups=mesh['zl'=3,'y'=8,'x'=4,'c'=2,'tp'=4] {'x'}, dimensions={0}, use_global_device_ids=true | all-gather | bytes 245760 | tf_op jit(solution)/shard_map/all_gather | solution.py:226
  51.3 10.9 %all-to-all-done.1.key_value_ref = bf16[8,2,192,128]{3,2,1,0:T(8,128)(2,1)S(1)} async-done(((bf16[8,2,192,128]{3,2,1,0:T(8,128)(2,1)}), bf16[8,2,192,128]{3,2,1,0:T(8,128)(2,1)S(1)}, u32[]{:S(2)}, u32[]{:S(2)}) %all-to-all-start.1) | async-done | bytes 786464 | tf_op jit(solution)/shard_map/all_to_all | solution.py:180
  62.3 2.0 %attend.1 = bf16[4,208,128]{2,1,0:T(8,128)(2,1)S(1)} custom-call(bf16[4,192,128]{2,1,0:T(8,128)(2,1)S(1)} %bitcast.14, bf16[8,2,192,128]{3,2,1,0:T(8,128)(2,1)S(1)} %all-to-all-done.1.key_value_ref), custom_call_target="tpu_custom_call" | custom-call | tf_op jit(solution)/shard_map/attend/pallas_call | solution.py:228
  64.3 9.2 %all_to_all.21.part_ref = bf16[4,208,128]{2,1,0:T(8,128)(2,1)S(1)} all-to-all(bf16[4,208,128]{2,1,0:T(8,128)(2,1)S(1)} %attend.1), channel_id=1, replica_groups=mesh['zl'=3,'y'=8,'x'=4,'c'=2,'tp'=4] {'x'}, dimensions={0} | all-to-all | bytes 425984 | tf_op jit(solution)/shard_map/all_to_all | solution.py:180
  73.5 0.9 combine.1
  74.3 19.3 %all_to_all.22.attended_ref = bf16[24,32,128]{2,1,0:T(8,128)(2,1)S(1)} all-to-all(bf16[24,32,128]{2,1,0:T(8,128)(2,1)S(1)} %combine.1), channel_id=1, replica_groups=mesh['zl'=3,'y'=8,'x'=4,'c'=2,'tp'=4] {'c','zl','tp'}, dimensions={0} | all-to-all | bytes 393216 | tf_op jit(solution)/shard_map/all_to_all | solution.py:180
  93.7 3.2 %mix.1 = bf16[32,1280]{1,0:T(8,128)(2,1)} custom-call(bf16[24,32,128]{2,1,0:T(8,128)(2,1)S(1)} %all_to_all.22.attended_ref, f32[1,1280]{1,0:T(1,128)S(1)} %get-tuple-element.23.row_ref, bf16[768,1280]{1,0:T(8,128)(2,1)S(1)} %get-tuple-element.24.first_ref, bf16[2560,1280]{1,0:T(8,128)(2,1)} %weight_ref.1), custom_call_target="tpu_custom_call" | custom-call | tf_op jit(solution)/shard_map/mix/pallas_call | solution.py:249
  (1 shorter events, 0.0 us)
Async XLA Ops:
  31.7 30.5 %all-to-all-start.1 = ((bf16[8,2,192,128]{3,2,1,0:T(8,128)(2,1)}), bf16[8,2,192,128]{3,2,1,0:T(8,128)(2,1)S(1)}, u32[]{:S(2)}, u32[]{:S(2)}) async-start(bf16[8,2,192,128]{3,2,1,0:T(8,128)(2,1)} %get-tuple-element.16), calls=%async_computation.1 | async-start | bytes 1572864 | tf_op jit(solution)/shard_map/all_to_all | solution.py:180
  38.6 0.7 copy-start

commit v17 on v15

--- a/solution.py
+++ b/solution.py
@@ -18,7 +18,7 @@
 STAT_ROWS = 16
 GROUP_STEP = 2
 KEY_BLOCKS = 4
-EARLY_HEADS = 6
+EARLY_HEADS = 7
 KERNEL_VMEM = 16 * 1024 * 1024
 MIX_VMEM = 50 * 1024 * 1024
 IN_VMEM = pl.BlockSpec(memory_space=pltpu.VMEM)
@@ -215,7 +215,7 @@
         ],
         in_specs=[in_hbm, IN_VMEM],
         out_specs=[IN_VMEM] * 2,
-        scratch_shapes=[pltpu.SemaphoreType.DMA((EARLY_HEADS // 2,))],
+        scratch_shapes=[pltpu.SemaphoreType.DMA((EARLY_HEADS,))],
         compiler_params=pltpu.CompilerParams(vmem_limit_bytes=MIX_VMEM),
         cost_estimate=pl.CostEstimate(
             flops=0, bytes_accessed=4 * EARLY_HEADS * HEAD_DIM * channels, transcendentals=0
@@ -253,7 +253,7 @@
         out_specs=IN_VMEM,
         scratch_shapes=[
             pltpu.VMEM((late * HEAD_DIM, channels), out_weight.dtype),
-            pltpu.SemaphoreType.DMA((late // 2,)),
+            pltpu.SemaphoreType.DMA((late,)),
         ],
         compiler_params=pltpu.CompilerParams(vmem_limit_bytes=MIX_VMEM),
         name="mix",

time: 95.8 us -> 95.7 us (level)
  no operation moved by 1% of the time
where the time goes in v17:
time: 95.7 us; the launch traced here: 95.3 us
  blocking collectives  68.4 us (71%)
  waiting for transfers between devices  9.91 us (10%)
  Pallas kernels  8.58 us (9%)
  starting transfers between devices  6.83 us (7%)
    all_to_all x3, blocking collectives, exchange(): return lax.all_to_all(blocks, axes, split_axis=0, concat_axis=0, tiled=True)  58.2 us
    all_gather x1, blocking collectives, on_device(): group = lax.all_gather(own_query, QUERY_AXES, axis=0, tiled=False)  10.2 us
    all_to_all x1, waiting for transfers between devices, exchange(): return lax.all_to_all(blocks, axes, split_axis=0, concat_axis=0, tiled=True)  9.91 us
    all_to_all x1, starting transfers between devices, exchange(): return lax.all_to_all(blocks, axes, split_axis=0, concat_axis=0, tiled=True)  6.83 us
    pallas_call x1, Pallas kernels, on_device(): pl.pallas_call(mix_kernel, out_shape=jax.ShapeDtypeStruct((own_tokens, ch...  3.09 us
    pallas_call x1, Pallas kernels, on_device(): pl.pallas_call(attend_kernel, out_shape=jax.ShapeDtypeStruct((group.shape...  2.03 us
  transfers between devices with their start and end apart: 1, of which 1 were waited for; matrix products, arithmetic and copies ran while one was open for 0% of the time, Pallas kernels for 2%

profile of v17, /device:TPU:1, one launch (start us, length us, event | category | flops | bytes accessed | tf_op | source)
XLA Modules:
  0.0 95.3 jit_solution(4354677886655456348)
XLA Ops:
  0.0 0.8 maximum_bitcast_fusion
  0.9 28.8 %all_to_all.20.local_ref = bf16[24,24,128]{2,1,0:T(8,128)(2,1)S(1)} all-to-all(bf16[24,24,128]{2,1,0:T(8,128)(2,1)S(1)} %pad.4), channel_id=1, replica_groups=mesh['zl'=3,'y'=8,'x'=4,'c'=2,'tp'=4] {'zl','c','tp'}, dimensions={0} | all-to-all | bytes 294912 | tf_op jit(solution)/shard_map/all_to_all | solution.py:180
  29.7 1.0 %split.1 = (bf16[192,128]{1,0:T(8,128)(2,1)S(1)}, bf16[8,2,192,128]{3,2,1,0:T(8,128)(2,1)}) custom-call(bf16[24,24,128]{2,1,0:T(8,128)(2,1)S(1)} %all_to_all.20.local_ref), custom_call_target="tpu_custom_call" | custom-call | tf_op jit(solution)/shard_map/split/pallas_call | solution.py:192
  30.7 6.8 %all-to-all-start.1 = ((bf16[8,2,192,128]{3,2,1,0:T(8,128)(2,1)}), bf16[8,2,192,128]{3,2,1,0:T(8,128)(2,1)S(1)}, u32[]{:S(2)}, u32[]{:S(2)}) async-start(bf16[8,2,192,128]{3,2,1,0:T(8,128)(2,1)} %get-tuple-element.16), calls=%async_computation.1 | async-start | bytes 1572864 | tf_op jit(solution)/shard_map/all_to_all | solution.py:180
  37.5 0.0 copy-start
  37.5 0.7 copy-done
  38.2 1.6 %fetch.1 = (bf16[896,1280]{1,0:T(8,128)(2,1)S(1)}, f32[1,1280]{1,0:T(1,128)S(1)}) custom-call(bf16[2560,1280]{1,0:T(8,128)(2,1)} %weight_ref.1, f32[1280]{0:T(1024)S(1)} %copy-done), custom_call_target="tpu_custom_call" | custom-call | bytes 4587520 | tf_op jit(solution)/shard_map/fetch/pallas_call | solution.py:210
  39.8 10.2 %all-gather = bf16[768,128]{1,0:T(8,128)(2,1)S(1)} all-gather(bf16[192,128]{1,0:T(8,128)(2,1)S(1)} %get-tuple-element.17), channel_id=2, replica_groups=mesh['zl'=3,'y'=8,'x'=4,'c'=2,'tp'=4] {'x'}, dimensions={0}, use_global_device_ids=true | all-gather | bytes 245760 | tf_op jit(solution)/shard_map/all_gather | solution.py:226
  50.0 9.9 %all-to-all-done.1.key_value_ref = bf16[8,2,192,128]{3,2,1,0:T(8,128)(2,1)S(1)} async-done(((bf16[8,2,192,128]{3,2,1,0:T(8,128)(2,1)}), bf16[8,2,192,128]{3,2,1,0:T(8,128)(2,1)S(1)}, u32[]{:S(2)}, u32[]{:S(2)}) %all-to-all-start.1) | async-done | bytes 786464 | tf_op jit(solution)/shard_map/all_to_all | solution.py:180
  59.9 2.0 %attend.1 = bf16[4,208,128]{2,1,0:T(8,128)(2,1)S(1)} custom-call(bf16[4,192,128]{2,1,0:T(8,128)(2,1)S(1)} %bitcast.14, bf16[8,2,192,128]{3,2,1,0:T(8,128)(2,1)S(1)} %all-to-all-done.1.key_value_ref), custom_call_target="tpu_custom_call" | custom-call | tf_op jit(solution)/shard_map/attend/pallas_call | solution.py:228
  62.0 9.1 %all_to_all.21.part_ref = bf16[4,208,128]{2,1,0:T(8,128)(2,1)S(1)} all-to-all(bf16[4,208,128]{2,1,0:T(8,128)(2,1)S(1)} %attend.1), channel_id=1, replica_groups=mesh['zl'=3,'y'=8,'x'=4,'c'=2,'tp'=4] {'x'}, dimensions={0} | all-to-all | bytes 425984 | tf_op jit(solution)/shard_map/all_to_all | solution.py:180
  71.0 0.9 combine.1
  71.9 20.3 %all_to_all.22.attended_ref = bf16[24,32,128]{2,1,0:T(8,128)(2,1)S(1)} all-to-all(bf16[24,32,128]{2,1,0:T(8,128)(2,1)S(1)} %combine.1), channel_id=1, replica_groups=mesh['zl'=3,'y'=8,'x'=4,'c'=2,'tp'=4] {'zl','c','tp'}, dimensions={0} | all-to-all | bytes 393216 | tf_op jit(solution)/shard_map/all_to_all | solution.py:180
  92.2 3.1 %mix.1 = bf16[32,1280]{1,0:T(8,128)(2,1)} custom-call(bf16[24,32,128]{2,1,0:T(8,128)(2,1)S(1)} %all_to_all.22.attended_ref, f32[1,1280]{1,0:T(1,128)S(1)} %get-tuple-element.23.row_ref, bf16[896,1280]{1,0:T(8,128)(2,1)S(1)} %get-tuple-element.24.first_ref, bf16[2560,1280]{1,0:T(8,128)(2,1)} %weight_ref.1), custom_call_target="tpu_custom_call" | custom-call | tf_op jit(solution)/shard_map/mix/pallas_call | solution.py:249
  (1 shorter events, 0.0 us)
Async XLA Ops:
  30.7 29.2 %all-to-all-start.1 = ((bf16[8,2,192,128]{3,2,1,0:T(8,128)(2,1)}), bf16[8,2,192,128]{3,2,1,0:T(8,128)(2,1)S(1)}, u32[]{:S(2)}, u32[]{:S(2)}) async-start(bf16[8,2,192,128]{3,2,1,0:T(8,128)(2,1)} %get-tuple-element.16), calls=%async_computation.1 | async-start | bytes 1572864 | tf_op jit(solution)/shard_map/all_to_all | solution.py:180
  37.5 0.7 copy-start

commit v18 on v15

--- a/solution.py
+++ b/solution.py
@@ -205,7 +205,8 @@
         name="split",
     )(exchange(stacked, HEAD_AXES))
     channels = out_weight.shape[1]
-    key_value_copies, weight = lax.optimization_barrier((key_value_copies, out_weight))
+    group = lax.all_gather(own_query, QUERY_AXES, axis=0, tiled=False)
+    group, weight = lax.optimization_barrier((group, out_weight))
     in_hbm = pl.BlockSpec(memory_space=pltpu.HBM)
     first, row = pl.pallas_call(
         fetch_kernel,
@@ -223,7 +224,6 @@
         name="fetch",
     )(weight, gate)
     key_value = exchange(key_value_copies, KEY_AXES)
-    group = lax.all_gather(own_query, QUERY_AXES, axis=0, tiled=False)
     key_value, group, first, row = lax.optimization_barrier((key_value, group, first, row))
     partial = pl.pallas_call(
         attend_kernel,

time: 95.8 us -> 95.8 us (level)
  no operation moved by 1% of the time
where the time goes in v18:
time: 95.8 us; the launch traced here: 95.4 us
  blocking collectives  68.1 us (71%)
  waiting for transfers between devices  10.3 us (11%)
  Pallas kernels  8.58 us (9%)
  starting transfers between devices  6.83 us (7%)
    all_to_all x3, blocking collectives, exchange(): return lax.all_to_all(blocks, axes, split_axis=0, concat_axis=0, tiled=True)  58.2 us
    all_to_all x1, waiting for transfers between devices, exchange(): return lax.all_to_all(blocks, axes, split_axis=0, concat_axis=0, tiled=True)  10.3 us
    all_gather x1, blocking collectives, on_device(): group = lax.all_gather(own_query, QUERY_AXES, axis=0, tiled=False)  9.87 us
    all_to_all x1, starting transfers between devices, exchange(): return lax.all_to_all(blocks, axes, split_axis=0, concat_axis=0, tiled=True)  6.83 us
    pallas_call x1, Pallas kernels, on_device(): pl.pallas_call(mix_kernel, out_shape=jax.ShapeDtypeStruct((own_tokens, ch...  3.21 us
    pallas_call x1, Pallas kernels, on_device(): pl.pallas_call(attend_kernel, out_shape=jax.ShapeDtypeStruct((group.shape...  2.03 us
  transfers between devices with their start and end apart: 1, of which 1 were waited for; matrix products, arithmetic and copies ran while one was open for 0% of the time, Pallas kernels for 2%

profile of v18, /device:TPU:1, one launch (start us, length us, event | category | flops | bytes accessed | tf_op | source)
XLA Modules:
  0.0 95.4 jit_solution(6107408076408905717)
XLA Ops:
  0.0 0.8 maximum_bitcast_fusion
  0.9 28.8 %all_to_all.20.local_ref = bf16[24,24,128]{2,1,0:T(8,128)(2,1)S(1)} all-to-all(bf16[24,24,128]{2,1,0:T(8,128)(2,1)S(1)} %pad.4), channel_id=1, replica_groups=mesh['zl'=3,'y'=8,'x'=4,'c'=2,'tp'=4] {'zl','c','tp'}, dimensions={0} | all-to-all | bytes 294912 | tf_op jit(solution)/shard_map/all_to_all | solution.py:180
  29.7 1.0 %split.1 = (bf16[192,128]{1,0:T(8,128)(2,1)S(1)}, bf16[8,2,192,128]{3,2,1,0:T(8,128)(2,1)}) custom-call(bf16[24,24,128]{2,1,0:T(8,128)(2,1)S(1)} %all_to_all.20.local_ref), custom_call_target="tpu_custom_call" | custom-call | tf_op jit(solution)/shard_map/split/pallas_call | solution.py:192
  30.7 6.8 %all-to-all-start.1 = ((bf16[8,2,192,128]{3,2,1,0:T(8,128)(2,1)}), bf16[8,2,192,128]{3,2,1,0:T(8,128)(2,1)S(1)}, u32[]{:S(2)}, u32[]{:S(2)}) async-start(bf16[8,2,192,128]{3,2,1,0:T(8,128)(2,1)} %get-tuple-element.15), calls=%async_computation.1 | async-start | bytes 1572864 | tf_op jit(solution)/shard_map/all_to_all | solution.py:180
  37.5 9.9 %all-gather = bf16[768,128]{1,0:T(8,128)(2,1)S(1)} all-gather(bf16[192,128]{1,0:T(8,128)(2,1)S(1)} %get-tuple-element.16), channel_id=2, replica_groups=mesh['zl'=3,'y'=8,'x'=4,'c'=2,'tp'=4] {'x'}, dimensions={0}, use_global_device_ids=true | all-gather | bytes 245760 | tf_op jit(solution)/shard_map/all_gather | solution.py:208
  47.4 0.0 copy-start
  47.4 0.7 copy-done
  48.1 1.5 %fetch.1 = (bf16[768,1280]{1,0:T(8,128)(2,1)S(1)}, f32[1,1280]{1,0:T(1,128)S(1)}) custom-call(bf16[2560,1280]{1,0:T(8,128)(2,1)} %weight_ref.1, f32[1280]{0:T(1024)S(1)} %copy-done), custom_call_target="tpu_custom_call" | custom-call | bytes 3932160 | tf_op jit(solution)/shard_map/fetch/pallas_call | solution.py:211
  49.6 10.3 %all-to-all-done.1.key_value_ref = bf16[8,2,192,128]{3,2,1,0:T(8,128)(2,1)S(1)} async-done(((bf16[8,2,192,128]{3,2,1,0:T(8,128)(2,1)}), bf16[8,2,192,128]{3,2,1,0:T(8,128)(2,1)S(1)}, u32[]{:S(2)}, u32[]{:S(2)}) %all-to-all-start.1) | async-done | bytes 786464 | tf_op jit(solution)/shard_map/all_to_all | solution.py:180
  59.9 2.0 %attend.1 = bf16[4,208,128]{2,1,0:T(8,128)(2,1)S(1)} custom-call(bf16[4,192,128]{2,1,0:T(8,128)(2,1)S(1)} %bitcast.14, bf16[8,2,192,128]{3,2,1,0:T(8,128)(2,1)S(1)} %all-to-all-done.1.key_value_ref), custom_call_target="tpu_custom_call" | custom-call | tf_op jit(solution)/shard_map/attend/pallas_call | solution.py:228
  62.0 9.1 %all_to_all.21.part_ref = bf16[4,208,128]{2,1,0:T(8,128)(2,1)S(1)} all-to-all(bf16[4,208,128]{2,1,0:T(8,128)(2,1)S(1)} %attend.1), channel_id=1, replica_groups=mesh['zl'=3,'y'=8,'x'=4,'c'=2,'tp'=4] {'x'}, dimensions={0} | all-to-all | bytes 425984 | tf_op jit(solution)/shard_map/all_to_all | solution.py:180
  71.0 0.9 combine.1
  71.9 20.3 %all_to_all.22.attended_ref = bf16[24,32,128]{2,1,0:T(8,128)(2,1)S(1)} all-to-all(bf16[24,32,128]{2,1,0:T(8,128)(2,1)S(1)} %combine.1), channel_id=1, replica_groups=mesh['zl'=3,'y'=8,'x'=4,'c'=2,'tp'=4] {'zl','c','tp'}, dimensions={0} | all-to-all | bytes 393216 | tf_op jit(solution)/shard_map/all_to_all | solution.py:180
  92.2 3.2 %mix.1 = bf16[32,1280]{1,0:T(8,128)(2,1)} custom-call(bf16[24,32,128]{2,1,0:T(8,128)(2,1)S(1)} %all_to_all.22.attended_ref, f32[1,1280]{1,0:T(1,128)S(1)} %get-tuple-element.23.row_ref, bf16[768,1280]{1,0:T(8,128)(2,1)S(1)} %get-tuple-element.24.first_ref, bf16[2560,1280]{1,0:T(8,128)(2,1)} %weight_ref.1), custom_call_target="tpu_custom_call" | custom-call | tf_op jit(solution)/shard_map/mix/pallas_call | solution.py:249
  (1 shorter events, 0.0 us)
Async XLA Ops:
  30.7 29.2 %all-to-all-start.1 = ((bf16[8,2,192,128]{3,2,1,0:T(8,128)(2,1)}), bf16[8,2,192,128]{3,2,1,0:T(8,128)(2,1)S(1)}, u32[]{:S(2)}, u32[]{:S(2)}) async-start(bf16[8,2,192,128]{3,2,1,0:T(8,128)(2,1)} %get-tuple-element.15), calls=%async_computation.1 | async-start | bytes 1572864 | tf_op jit(solution)/shard_map/all_to_all | solution.py:180
  47.4 0.7 copy-start
